TPU v7x, 32 devices: a whole 2x2x4 slice. The times are simulated.
32 devices in a mesh: freq: 16 (over z, y, core), rows: 2 (over x).
Axes of the slice: x: 2, y: 2, z: 4, core: 2. Of those that a mesh axis runs over, the one named last changes fastest.
Arguments:
- kernel: bfloat16 [2, 128, 2048, 2048], P(None, 'freq', 'rows'), may hold values from -0.25 to 0.25
- tile_mask: int32 [128, 16, 16], P('freq', 'rows'), may hold values 0 or 1
- direct: float32 [2048, 128, 512], P(('rows', 'freq')), may hold values from -6 to 6
- onsets: int32 [2048, 128], P(('rows', 'freq')), may hold values from 64 to 447
Outputs:
- focusing: float32 [2048, 128, 512], P(('rows', 'freq'))
Inputs may be any that keep to these rules, and one draw needn't show every extreme that they name: `tile_mask`: 0 drops a tile, 1 keeps it.
All inputs are finite; a program needn't handle non-finite values. No bound on the sum of `tile_mask` on one device may be relied on, other than what follows from the above.
Results may differ from a plain program's by a relative error of at most 0.0026.
Values may be sent and summed in bfloat16 or wider, within the bound.
No kernel may reach another device: no remote copies, remote signals or barrier semaphores. Data moves between devices by JAX's collectives and lax.ppermute only.
A program may use at most 320 MiB of HBM per device.

v0:
```python
import math

import jax
import jax.numpy as jnp
from jax import lax
from jax.sharding import PartitionSpec as P

NF = 128
NT = 512
TILE = 128
ITERS = 2


def phase_table():
    freq_ids = jnp.arange(NF, dtype=jnp.int32) + 1
    time_ids = jnp.arange(NT, dtype=jnp.int32)
    phase_ids = freq_ids[:, None] * time_ids[None, :] % NT
    angles = phase_ids.astype(jnp.float32) * (2.0 * math.pi / NT)
    norm_scale = math.sqrt(2.0 / NT)
    return jnp.stack([jnp.cos(angles), -jnp.sin(angles)]) * norm_scale


def multiply(weights, fields):
    real_real = jnp.einsum(
        "fmk,fkp->fmp", weights[0], fields[0], preferred_element_type=jnp.float32
    )
    imag_imag = jnp.einsum(
        "fmk,fkp->fmp", weights[1], fields[1], preferred_element_type=jnp.float32
    )
    real_imag = jnp.einsum(
        "fmk,fkp->fmp", weights[0], fields[1], preferred_element_type=jnp.float32
    )
    imag_real = jnp.einsum(
        "fmk,fkp->fmp", weights[1], fields[0], preferred_element_type=jnp.float32
    )
    return jnp.stack([real_real - imag_imag, real_imag + imag_real])


def products(masked, fields):
    return multiply(masked, lax.all_gather(fields, "rows", axis=2, tiled=True))


def forward(masked, fields, direct, window, dft_table):
    bands = products(masked, fields).astype(jnp.bfloat16)
    traces = lax.all_to_all(bands, "freq", split_axis=2, concat_axis=1, tiled=True)
    series = jnp.einsum(
        "kjrp,kjt->rpt", traces.astype(jnp.float32), dft_table, precision=lax.Precision.HIGHEST
    )
    return direct - jnp.where(window, series, 0.0)


def to_bands(focusing, dft_table):
    spectra = jnp.einsum(
        "rpt,kjt->kjrp", focusing, dft_table, precision=lax.Precision.HIGHEST
    ).astype(jnp.bfloat16)
    bands = lax.all_to_all(spectra, "freq", split_axis=1, concat_axis=2, tiled=True)
    return bands


def local(kernel, tile_mask, direct, onsets):
    dft_table = phase_table()
    full_mask = jnp.repeat(jnp.repeat(tile_mask, TILE, axis=1), TILE, axis=2).astype(jnp.bfloat16)
    masked = kernel * full_mask[None]
    time_ids = jnp.arange(NT, dtype=jnp.int32)
    window = time_ids[None, None, :] < onsets[:, :, None]
    fields = to_bands(direct, dft_table)
    focusing = direct
    for iteration in range(ITERS):
        focusing = forward(masked, fields, direct, window, dft_table)
        if iteration + 1 < ITERS:
            fields = to_bands(focusing, dft_table)
    return focusing


def solution(mesh):
    return jax.shard_map(
        local,
        mesh=mesh,
        in_specs=(
            P(None, "freq", "rows", None),
            P("freq", "rows", None),
            P(("rows", "freq"), None, None),
            P(("rows", "freq"), None),
        ),
        out_specs=P(("rows", "freq"), None, None),
        check_vma=False,
    )
```

profile of v0, /device:TPU:1, one launch (start us, length us, event | category | flops | bytes accessed | tf_op | source)
XLA Modules:
  0.0 853.0 jit_solution(786638177936812693)
XLA Ops:
  6.5 1.1 fusion.40
  7.6 0.0 copy-start
  7.7 0.0 copy-start.2
  7.7 0.7 copy-done
  8.4 0.1 copy-done.2
  8.4 16.9 %fusion.20 = bf16[2,128,64,128]{3,1,2,0:T(8,128)(2,1)S(1)} fusion(f32[64,128,512]{2,1,0:T(8,128)} %param.6, f32[1,128,512]{2,1,0:T(8,128)S(1)} %get-tuple-element.6, f32[1,128,512]{2,1,0:T(8,128)S(1)} %get-tuple-element.5), kind=kOutput, calls=%fused_computation.35 | convolution fusion | flops 12887261184 | bytes 21495808 | tf_op jit(solution)/shard_map/rpt,kjt->kjrp/dot_general | solution.py:53
  25.4 0.0 copy-start.5
  25.4 4.7 copy.21
  30.1 7.3 all-to-all-start
  37.4 0.0 all-gather.3.cloned.1.call-start
  37.5 0.0 copy-done.5
  37.5 0.3 broadcast_in_dim.16
  37.8 21.0 %broadcast_in_dim.17 = bf16[8,1024,16,128]{3,2,1,0:T(8,128)(2,1)} broadcast(bf16[8,1024,16]{2,1,0:T(8,128)(2,1)S(1)} %bitcast.116), dimensions={0,1,2} | broadcast | bytes 33816576 | tf_op jit(solution)/shard_map/broadcast_in_dim | solution.py:62
  58.7 49.3 %convert_element_type.43 = bf16[8,1024,2048]{2,1,0:T(8,128)(2,1)} reshape(bf16[8,1024,16,128]{3,2,1,0:T(8,128)(2,1)} %broadcast_in_dim.17) | data formatting | bytes 67108864 | tf_op jit(solution)/shard_map/convert_element_type | solution.py:62
  108.0 7.5 all-to-all-done
  115.6 5.6 copy.22
  121.2 0.0 all-gather.3.cloned.1.call-update
  121.2 0.3 all-gather.5.cloned.1.call-start
  121.4 56.1 %broadcast_multiply_fusion = bf16[2,8,1024,2048]{3,2,1,0:T(8,128)(2,1)} fusion(bf16[2,8,1024,2048]{3,2,1,0:T(8,128)(2,1)} %param.4, bf16[8,1024,2048]{2,1,0:T(8,128)(2,1)} %convert_element_type.43), kind=kLoop, calls=%fused_computation.2 | loop fusion | flops 33554432 | bytes 167772160 | tf_op jit(solution)/shard_map/mul | solution.py:63
  177.6 61.4 %all-gather.3.cloned.1.call-done = bf16[2,8,2048,128]{3,2,1,0:T(8,128)(2,1)} async-done(((bf16[2,8,1024,128]{3,2,1,0:T(8,128)(2,1)}), bf16[2,8,2048,128]{3,2,1,0:T(8,128)(2,1)}) %all-gather.3.cloned.1.call-update) | async-done | bytes 8388624 | tf_op jit(solution)/shard_map/all_gather | solution.py:40
  239.0 17.6 %fusion.2 = f32[8,1024,128]{2,1,0:T(8,128)} fusion(bf16[2,8,1024,2048]{3,2,1,0:T(8,128)(2,1)} %broadcast_multiply_fusion, bf16[2,8,2048,128]{3,2,1,0:T(8,128)(2,1)} %all-gather.3.cloned.1.call-done), kind=kOutput, calls=%fused_computation.5 | convolution fusion | flops 4294967296 | bytes 41943040 | tf_op jit(solution)/shard_map/fmk,fkp->fmp/dot_general | solution.py:30
  256.6 17.7 %fusion.3 = f32[8,1024,128]{2,1,0:T(8,128)} fusion(bf16[2,8,1024,2048]{3,2,1,0:T(8,128)(2,1)} %broadcast_multiply_fusion, bf16[2,8,2048,128]{3,2,1,0:T(8,128)(2,1)} %all-gather.3.cloned.1.call-done), kind=kOutput, calls=%fused_computation.6 | convolution fusion | flops 4294967296 | bytes 41943040 | tf_op jit(solution)/shard_map/fmk,fkp->fmp/dot_general | solution.py:24
  274.2 16.7 %fusion.27 = bf16[1,8,1024,128]{3,2,1,0:T(8,128)(2,1)S(1)} fusion(f32[8,1024,128]{2,1,0:T(8,128)} %fusion.2, bf16[2,8,2048,128]{3,2,1,0:T(8,128)(2,1)} %all-gather.3.cloned.1.call-done, bf16[2,8,1024,2048]{3,2,1,0:T(8,128)(2,1)} %broadcast_multiply_fusion), kind=kOutput, calls=%fused_computation.38 | convolution fusion | flops 4297064448 | bytes 44040192 | tf_op jit(solution)/shard_map/fmk,fkp->fmp/dot_general | solution.py:33
  290.9 16.9 %fusion.26 = bf16[1,8,1024,128]{3,2,1,0:T(8,128)(2,1)S(1)} fusion(f32[8,1024,128]{2,1,0:T(8,128)} %fusion.3, bf16[2,8,2048,128]{3,2,1,0:T(8,128)(2,1)} %all-gather.3.cloned.1.call-done, bf16[2,8,1024,2048]{3,2,1,0:T(8,128)(2,1)} %broadcast_multiply_fusion), kind=kOutput, calls=%fused_computation.37 | convolution fusion | flops 4297064448 | bytes 44040192 | tf_op jit(solution)/shard_map/fmk,fkp->fmp/dot_general | solution.py:27
  307.8 0.4 pad_maximum_fusion
  308.2 2.7 copy.23
  310.9 0.0 copy-start.1
  310.9 0.0 copy-start.3
  310.9 99.4 %all_to_all.72 = bf16[2,8,1024,128]{3,1,0,2:T(8,128)(2,1)S(1)} all-to-all(bf16[2,8,1024,128]{3,1,0,2:T(8,128)(2,1)S(1)} %copy.23), channel_id=1, replica_groups=mesh['freq'=16,'rows'=2] {'freq'}, dimensions={2} | all-to-all | bytes 8388608 | tf_op jit(solution)/shard_map/all_to_all | solution.py:45
  410.4 0.0 slice-start
  410.4 1.1 copy.25
  411.4 0.0 copy-done.1
  411.4 0.0 copy-done.3
  411.5 0.0 slice-start.1
  411.5 0.0 slice-start.2
  411.5 0.0 slice-start.3
  411.5 0.0 copy-start.4
  411.5 17.6 %fusion.18 = f32[64,128,512,1]{2,1,3,0:T(8,128)} fusion(bf16[2,128,64,128]{3,2,1,0:T(8,128)(2,1)S(1)} %bitcast.109, f32[1,128,512]{2,1,0:T(8,128)S(1)} %copy-done.3, f32[1,128,512]{2,1,0:T(8,128)S(1)} %copy-done.1), kind=kOutput, calls=%fused_computation.29 | convolution fusion | flops 12885164032 | bytes 21495808 | tf_op jit(solution)/shard_map/kjrp,kjt->rpt/dot_general | solution.py:46
  429.1 0.0 slice-done
  429.1 0.0 slice-done.1
  429.1 0.0 slice-done.2
  429.2 0.0 slice-done.3
  429.2 0.0 copy-done.4
  429.2 18.9 %fusion.23 = bf16[2,128,64,128]{3,1,2,0:T(8,128)(2,1)S(1)} fusion(f32[64,128,512]{2,1,0:T(8,128)S(1)} %bitcast.108, f32[64,128,512,1]{2,1,3,0:T(8,128)} %fusion.18, s32[64,128]{1,0:T(8,128)S(1)} %copy-done.4, f32[1,128,512]{2,1,0:T(8,128)S(1)} %copy-done.3, f32[1,128,512]{2,1,0:T(8,128)S(1)} %copy-done.1), kind=kOutput, calls=%fused_computation.36 | convolution fusion | flops 12899844096 | bytes 38305792 | tf_op jit(solution)/shard_map/rpt,kjt->kjrp/dot_general | solution.py:53
  448.1 2.7 copy.27
  450.8 97.4 %all_to_all.73 = bf16[2,128,64,128]{3,2,0,1:T(8,128)(2,1)S(1)} all-to-all(bf16[2,128,64,128]{3,2,0,1:T(8,128)(2,1)S(1)} %copy.27), channel_id=1, replica_groups=mesh['freq'=16,'rows'=2] {'freq'}, dimensions={1} | all-to-all | bytes 8388608 | tf_op jit(solution)/shard_map/all_to_all | solution.py:56
  548.3 3.0 copy.28
  551.2 0.0 all-gather.5.cloned.1.call-update
  551.2 102.6 %all-gather.5.cloned.1.call-done = bf16[2,8,2048,128]{3,2,1,0:T(8,128)(2,1)} async-done(((bf16[2,8,1024,128]{3,2,1,0:T(8,128)(2,1)}), bf16[2,8,2048,128]{3,2,1,0:T(8,128)(2,1)}) %all-gather.5.cloned.1.call-update) | async-done | bytes 8388624 | tf_op jit(solution)/shard_map/all_gather | solution.py:40
  653.8 17.7 %fusion = f32[8,1024,128]{2,1,0:T(8,128)} fusion(bf16[2,8,1024,2048]{3,2,1,0:T(8,128)(2,1)} %broadcast_multiply_fusion, bf16[2,8,2048,128]{3,2,1,0:T(8,128)(2,1)} %all-gather.5.cloned.1.call-done), kind=kOutput, calls=%fused_computation.3 | convolution fusion | flops 4294967296 | bytes 41943040 | tf_op jit(solution)/shard_map/fmk,fkp->fmp/dot_general | solution.py:30
  671.5 17.6 %fusion.1 = f32[8,1024,128]{2,1,0:T(8,128)} fusion(bf16[2,8,1024,2048]{3,2,1,0:T(8,128)(2,1)} %broadcast_multiply_fusion, bf16[2,8,2048,128]{3,2,1,0:T(8,128)(2,1)} %all-gather.5.cloned.1.call-done), kind=kOutput, calls=%fused_computation.4 | convolution fusion | flops 4294967296 | bytes 41943040 | tf_op jit(solution)/shard_map/fmk,fkp->fmp/dot_general | solution.py:24
  689.1 16.7 %fusion.29 = bf16[1,8,1024,128]{3,2,1,0:T(8,128)(2,1)S(1)} fusion(f32[8,1024,128]{2,1,0:T(8,128)} %fusion, bf16[2,8,2048,128]{3,2,1,0:T(8,128)(2,1)} %all-gather.5.cloned.1.call-done, bf16[2,8,1024,2048]{3,2,1,0:T(8,128)(2,1)} %broadcast_multiply_fusion), kind=kOutput, calls=%fused_computation.40 | convolution fusion | flops 4297064448 | bytes 44040192 | tf_op jit(solution)/shard_map/fmk,fkp->fmp/dot_general | solution.py:33
  705.7 16.9 %fusion.28 = bf16[1,8,1024,128]{3,2,1,0:T(8,128)(2,1)S(1)} fusion(f32[8,1024,128]{2,1,0:T(8,128)} %fusion.1, bf16[2,8,2048,128]{3,2,1,0:T(8,128)(2,1)} %all-gather.5.cloned.1.call-done, bf16[2,8,1024,2048]{3,2,1,0:T(8,128)(2,1)} %broadcast_multiply_fusion), kind=kOutput, calls=%fused_computation.39 | convolution fusion | flops 4297064448 | bytes 44040192 | tf_op jit(solution)/shard_map/fmk,fkp->fmp/dot_general | solution.py:27
  722.7 0.4 pad_maximum_fusion.1
  723.1 2.7 copy.29
  725.8 98.8 %all_to_all.74 = bf16[2,8,1024,128]{3,1,0,2:T(8,128)(2,1)S(1)} all-to-all(bf16[2,8,1024,128]{3,1,0,2:T(8,128)(2,1)S(1)} %copy.29), channel_id=1, replica_groups=mesh['freq'=16,'rows'=2] {'freq'}, dimensions={2} | all-to-all | bytes 8388608 | tf_op jit(solution)/shard_map/all_to_all | solution.py:45
  824.6 1.1 copy.31
  825.7 20.1 %fusion.8 = f32[64,128,512]{2,1,0:T(8,128)} fusion(f32[64,128,512]{2,1,0:T(8,128)} %param.6, s32[64,128]{1,0:T(8,128)S(1)} %copy-done.4, bf16[2,128,64,128]{3,2,1,0:T(8,128)(2,1)S(1)} %bitcast.115, f32[1,128,512]{2,1,0:T(8,128)S(1)} %copy-done.3, f32[1,128,512]{2,1,0:T(8,128)S(1)} %copy-done.1), kind=kOutput, calls=%fused_computation.12 | convolution fusion | flops 12897746944 | bytes 38305792 | tf_op jit(solution)/shard_map/kjrp,kjt->rpt/dot_general | solution.py:46
  (3 shorter events, 0.0 us)
Async XLA Ops:
  7.6 0.7 copy-start
  7.7 0.8 copy-start.2
  25.4 12.1 %copy-start.5 = (s32[8,8,16]{2,1,0:T(8,128)S(1)}, s32[8,8,16]{2,1,0:T(8,128)}, u32[]{:S(2)}) copy-start(s32[8,8,16]{2,1,0:T(8,128)} %param.5) | copy-start | bytes 12292
  30.1 85.5 %all-to-all-start = ((bf16[2,128,64,128]{3,2,0,1:T(8,128)(2,1)}), bf16[2,128,64,128]{3,2,0,1:T(8,128)(2,1)}, u32[]{:S(2)}, u32[]{:S(2)}) async-start(bf16[2,128,64,128]{3,2,0,1:T(8,128)(2,1)} %copy.21), calls=%async_computation | async-start | bytes 8388608 | tf_op jit(solution)/shard_map/all_to_all | solution.py:56
  37.4 201.6 %all-gather.3.cloned.1.call-start = ((), (), s32[]{:S(2)}) async-start(), calls=%async_computation.4 | async-start | bytes 12582912 | tf_op jit(solution)/shard_map/all_gather | solution.py:40
  121.2 532.7 %all-gather.5.cloned.1.call-start = ((), (), s32[]{:S(2)}) async-start(), calls=%async_computation.5 | async-start | bytes 12582912 | tf_op jit(solution)/shard_map/all_gather | solution.py:40
  310.9 100.5 %copy-start.1 = (f32[1,128,512]{2,1,0:T(8,128)S(1)}, f32[1,128,512]{2,1,0:T(8,128)}, u32[]{:S(2)}) copy-start(f32[1,128,512]{2,1,0:T(8,128)} %copy-done) | copy-start | bytes 786436
  310.9 100.5 %copy-start.3 = (f32[1,128,512]{2,1,0:T(8,128)S(1)}, f32[1,128,512]{2,1,0:T(8,128)}, u32[]{:S(2)}) copy-start(f32[1,128,512]{2,1,0:T(8,128)} %copy-done.2) | copy-start | bytes 786436
  410.4 18.8 %slice-start = ((s8[16777216]{0:T(1024)(128)(4,1)}), s8[4194304]{0:T(1024)(128)(4,1)S(1)}, s32[]{:S(2)}) async-start(s8[16777216]{0:T(1024)(128)(4,1)} %bitcast.107), calls=%async_computation.6 | async-start | bytes 8388608
  411.5 17.7 %slice-start.1 = ((s8[16777216]{0:T(1024)(128)(4,1)}), s8[4194304]{0:T(1024)(128)(4,1)S(1)}, s32[]{:S(2)}) async-start(s8[16777216]{0:T(1024)(128)(4,1)} %bitcast.107), calls=%async_computation.7 | async-start | bytes 8388608
  411.5 17.7 %slice-start.2 = ((s8[16777216]{0:T(1024)(128)(4,1)}), s8[4194304]{0:T(1024)(128)(4,1)S(1)}, s32[]{:S(2)}) async-start(s8[16777216]{0:T(1024)(128)(4,1)} %bitcast.107), calls=%async_computation.8 | async-start | bytes 8388608
  411.5 17.7 %slice-start.3 = ((s8[16777216]{0:T(1024)(128)(4,1)}), s8[4194304]{0:T(1024)(128)(4,1)S(1)}, s32[]{:S(2)}) async-start(s8[16777216]{0:T(1024)(128)(4,1)} %bitcast.107), calls=%async_computation.9 | async-start | bytes 8388608
  411.5 17.7 %copy-start.4 = (s32[64,128]{1,0:T(8,128)S(1)}, s32[64,128]{1,0:T(8,128)}, u32[]{:S(2)}) copy-start(s32[64,128]{1,0:T(8,128)} %param.7) | copy-start | bytes 98308
Sparse Core Ops, SparseCore 0:
  121.3 117.6 all-gather.2
  551.4 102.4 all-gather.4
where the time goes:
time: 862 us; the launch traced here: 853 us
  blocking collectives  296 us (34%)
  matrix products  211 us (24%)
  waiting for transfers between devices  172 us (20%)
  local copies, waits for them, and re-layouts  94.9 us (11%)
  other arithmetic  58 us (7%)
  between operations  14.1 us (2%)
    all_to_all x2, blocking collectives, forward(): lax.all_to_all(bands, 'freq', split_axis=2, concat_axis=1, tiled=True)  198 us
    all_gather x2, waiting for transfers between devices, products(): return multiply(masked, lax.all_gather(fields, 'rows', axis=2, tiled=True))  164 us
    all_to_all x1, blocking collectives, to_bands(): lax.all_to_all(spectra, 'freq', split_axis=1, concat_axis=2, tiled=True)  97.4 us
    mul x1, other arithmetic, local(): masked = kernel * full_mask[None]  56.1 us
    convert_element_type x1, local copies, waits for them, and re-layouts, local(): jnp.repeat(jnp.repeat(tile_mask, TILE, axis=1), TILE, axis=2)  49.3 us
    dot_general x2, matrix products, forward(): jnp.einsum('kjrp,kjt->rpt', traces.astype(jnp.float32), dft_table, precis...  37.7 us
    dot_general x2, matrix products, to_bands(): jnp.einsum('rpt,kjt->kjrp', focusing, dft_table, precision=lax.Precision....  35.8 us
    dot_general x2, matrix products, multiply(): jnp.einsum('fmk,fkp->fmp', weights[0], fields[1], preferred_element_type=...  35.2 us
  transfers between devices with their start and end apart: 3, of which 3 were waited for; matrix products, arithmetic and copies ran while one was open for 15% of the time, Pallas kernels for 0%

commit v1 on v0

v1 whole, which is shorter than its diff:
```python
import functools
import math

import jax
import jax.numpy as jnp
from jax import lax
from jax.experimental import pallas as pl
from jax.experimental.pallas import tpu as pltpu
from jax.sharding import PartitionSpec as P


NF = 128
NT = 512
TILE = 128
ITERS = 2
LANES = 128
CHUNKS = 2
GROUP = 16
QUAD = 4
SLOTS = 4
BATCH = 8
PARTS = 2
F32 = jnp.float32
BF16 = jnp.bfloat16
VMEM_LIMIT = 60 * 1024 * 1024


def phase_tables():
    freq_ids = jnp.arange(NF, dtype=jnp.int32) + 1
    time_ids = jnp.arange(NT // 2, dtype=jnp.int32)
    phase_ids = freq_ids[:, None] * time_ids[None, :] % NT
    angles = phase_ids.astype(F32) * (2.0 * math.pi / NT)
    norm_scale = math.sqrt(2.0 / NT)
    table = jnp.stack([jnp.cos(angles), -jnp.sin(angles)]) * norm_scale
    table = table.reshape(2, NF // 2, 2, NT // 2).transpose(2, 0, 1, 3).reshape(2, NF, NT // 2)
    high = lax.reduce_precision(table, 8, 7)
    return jnp.concatenate([high, table - high], axis=1).astype(BF16)


def dot(a, b, dims=(1, 0)):
    return lax.dot_general(
        a, b, (((dims[0],), (dims[1],)), ((), ())), preferred_element_type=F32
    )


def split(x):
    high = x.astype(BF16)
    return high, (x - high.astype(F32)).astype(BF16)


def parity_rows(parity, receiver):
    return pl.ds(parity * GROUP + receiver, NF // 2, stride=2 * GROUP)


def to_rows(series, tables_ref, rows_ref, half, first):
    early, late = series[:, : NT // 2], series[:, NT // 2 :]
    for parity, folded in ((0, early - late), (1, early + late)):
        high, low = split(folded)
        both = dot(tables_ref[parity], high, (1, 1))
        spectra = both[:NF] + both[NF:] + dot(tables_ref[parity, :NF], low, (1, 1))
        for place in range(QUAD * half // LANES):
            pair = spectra[:, place * LANES : (place + 1) * LANES]
            real, imag = pair[: NF // 2], pair[NF // 2 :]
            left = lax.broadcasted_iota(jnp.int32, real.shape, 1) < half
            rows_ref[parity_rows(parity, first + 2 * place), :] = jnp.where(
                left, real, pltpu.roll(imag, half, 1)
            )
            rows_ref[parity_rows(parity, first + 2 * place + 1), :] = jnp.where(
                left, pltpu.roll(real, half, 1), imag
            )


def to_traces(rows_ref, tables_ref, half, first):
    odd, even = [], []
    for receiver in range(first, first + QUAD):
        rows = [rows_ref[parity_rows(parity, receiver), :] for parity in range(2)]
        turned = jnp.concatenate(rows, axis=0).T
        real, imag = turned[:half], turned[half:]
        left = lax.broadcasted_iota(jnp.int32, real.shape, 1) < NF // 2
        odd.append(jnp.where(left, real, pltpu.roll(imag, NF // 2, 1)))
        even.append(jnp.where(left, pltpu.roll(real, NF // 2, 1), imag))
    parts = []
    for parity, spectra in enumerate((odd, even)):
        spectra = jnp.concatenate(spectra, axis=0).astype(BF16)
        parts.append(dot(jnp.concatenate([spectra, spectra], axis=1), tables_ref[parity]))
    odd, even = parts
    return jnp.concatenate([even + odd, even - odd], axis=1)


def subtracted(direct_ref, traces, onsets_ref, half, first):
    series = direct_ref[first : first + QUAD].reshape(QUAD * half, NT)
    columns = [onsets_ref[0, :, first + which : first + which + 1] for which in range(QUAD)]
    ends = jnp.concatenate(columns, axis=0)
    times = lax.broadcasted_iota(jnp.int32, traces.shape, 1)
    return series - jnp.where(times < ends, traces, 0.0)


def store_out(out_ref, rows_ref):
    out_ref[...] = rows_ref[...].reshape(out_ref.shape).astype(BF16)


def load_in(rows_ref, bands_ref):
    rows_ref[...] = bands_ref[...].astype(F32).reshape(NF * GROUP, LANES)


def first_kernel(direct_ref, tables_ref, out_ref, rows_ref, *, half):
    for first in range(0, GROUP, QUAD):
        series = direct_ref[first : first + QUAD].reshape(QUAD * half, NT)
        to_rows(series, tables_ref, rows_ref, half, first)
    store_out(out_ref, rows_ref)


def middle_kernel(direct_ref, tables_ref, onsets_ref, bands_ref, out_ref, in_rows, rows_ref, *, half):
    load_in(in_rows, bands_ref)
    for first in range(0, GROUP, QUAD):
        traces = to_traces(in_rows, tables_ref, half, first)
        series = subtracted(direct_ref, traces, onsets_ref, half, first)
        to_rows(series, tables_ref, rows_ref, half, first)
    store_out(out_ref, rows_ref)


def last_kernel(direct_ref, tables_ref, onsets_ref, bands_ref, *rest, half):
    out_ref, in_rows = rest[-2:]
    load_in(in_rows, bands_ref)
    for first in range(0, GROUP, QUAD):
        traces = to_traces(in_rows, tables_ref, half, first)
        series = subtracted(direct_ref, traces, onsets_ref, half, first)
        out_ref[first : first + QUAD] = series.reshape(QUAD, half, NT)


def time_call(kind, chunk, owners, direct, tables, onsets=None, bands=None, out=None):
    receivers, focal, _ = direct.shape
    half = focal // CHUNKS
    freqs = NF // owners
    series_spec = pl.BlockSpec((GROUP, half, NT), lambda g: (g, chunk, 0))
    rows_spec = pl.BlockSpec((owners, freqs, GROUP, LANES), lambda g: (0, 0, g, 0))
    operands = [direct, tables]
    specs = [series_spec, pl.BlockSpec((2, 2 * NF, NT // 2), lambda g: (0, 0, 0))]
    if kind != "first":
        operands += [onsets, bands]
        specs += [pl.BlockSpec((1, half, GROUP), lambda g: (g, chunk, 0)), rows_spec]
    aliases = {}
    if out is not None:
        aliases = {len(operands): 0}
        operands.append(out)
        specs.append(pl.BlockSpec(memory_space=pl.ANY))
    rows_scratch = pltpu.VMEM((NF * GROUP, LANES), F32)
    if kind == "last":
        out_specs, out_shape = series_spec, jax.ShapeDtypeStruct(direct.shape, F32)
    else:
        out_specs = rows_spec
        out_shape = jax.ShapeDtypeStruct((owners, freqs, receivers, LANES), BF16)
    body, passes, scratches = {
        "first": (first_kernel, 3, 1),
        "middle": (middle_kernel, 5, 2),
        "last": (last_kernel, 2, 1),
    }[kind]
    elements = receivers * half * NT
    return pl.pallas_call(
        functools.partial(body, half=half),
        grid=(receivers // GROUP,),
        in_specs=specs,
        out_specs=out_specs,
        out_shape=out_shape,
        scratch_shapes=[rows_scratch] * scratches,
        input_output_aliases=aliases,
        compiler_params=pltpu.CompilerParams(vmem_limit_bytes=VMEM_LIMIT),
        cost_estimate=pl.CostEstimate(
            flops=4 * passes * elements * NF, bytes_accessed=8 * elements, transcendentals=0
        ),
    )(*operands)


def list_kernel(mask_ref, tiles_ref, count_ref):
    freqs, row_tiles, column_tiles = mask_ref.shape
    lines = row_tiles * freqs // PARTS
    for part in range(PARTS):
        base = part * (lines * column_tiles + BATCH)

        def row(line, position, part=part):
            row_tile, freq = line // (freqs // PARTS), lax.rem(line, freqs // PARTS)
            for column in range(column_tiles):
                tiles_ref[position] = line * column_tiles + column
                kept = mask_ref[part * (freqs // PARTS) + freq, row_tile, column] != 0
                position = position + jnp.where(kept, 1, 0)
            return position

        total = lax.fori_loop(0, lines, row, base)
        for extra in range(BATCH):
            tiles_ref[total + extra] = lines * column_tiles
        count_ref[part] = (total - base + BATCH - 1) // BATCH


def list_call(tile_mask):
    freqs, row_tiles, column_tiles = tile_mask.shape
    smem = pl.BlockSpec(memory_space=pltpu.SMEM)
    return pl.pallas_call(
        list_kernel,
        in_specs=[smem],
        out_specs=[smem, smem],
        out_shape=[
            jax.ShapeDtypeStruct((freqs * row_tiles * column_tiles + PARTS * BATCH,), jnp.int32),
            jax.ShapeDtypeStruct((PARTS,), jnp.int32),
        ],
        name="list_tiles",
    )(tile_mask)


def product_kernel(tiles_ref, count_ref, place_ref, kernel_ref, *rest, which_part, parts):
    field_refs, (out_ref, fields, sums, slots, slot_sems, field_sems) = rest[:parts], rest[-6:]
    _, _, rows, columns = kernel_ref.shape
    _, freqs, depth, lanes = out_ref.shape
    row_tiles, column_tiles = rows // TILE, columns // TILE
    lines = row_tiles * freqs
    per_tile = TILE // depth
    tiles_per_part = column_tiles // parts
    half = lanes // 2
    batches = count_ref[which_part]
    base = which_part * (lines * column_tiles + BATCH)

    def tile_copy(batch, which):
        code = tiles_ref[base + batch * BATCH + which]
        column = lax.rem(code, column_tiles)
        line = jnp.minimum(code // column_tiles, lines - 1)
        freq, row_tile = lax.rem(line, freqs), line // freqs
        slot = lax.rem(batch, SLOTS)
        return pltpu.make_async_copy(
            kernel_ref.at[:, which_part * freqs + freq, pl.ds(row_tile * TILE, TILE), pl.ds(column * TILE, TILE)],
            slots.at[slot, which],
            slot_sems.at[slot, which],
        )

    def start(batch):
        @pl.when(batch < batches)
        def _():
            for which in range(BATCH):
                tile_copy(batch, which).start()

    sources = [field_refs[0].at[:, pl.ds(which_part * freqs, freqs)], *field_refs[1:]]
    copies = [
        pltpu.make_async_copy(sources[part], fields.at[place_ref[part]], field_sems.at[part])
        for part in range(parts)
    ]
    for copy in copies:
        copy.start()
    for batch in range(SLOTS - 1):
        start(batch)

    def clear(line, _):
        sums[line] = jnp.zeros((TILE, lanes), F32)
        return 0

    lax.fori_loop(0, lines, clear, 0)
    for copy in copies:
        copy.wait()

    left = lax.broadcasted_iota(jnp.int32, (TILE, lanes), 1) < half

    def batch_step(batch, _):
        start(batch + SLOTS - 1)
        slot = lax.rem(batch, SLOTS)
        results = []
        for which in range(BATCH):
            tile_copy(batch, which).wait()
        for which in range(BATCH):
            code = tiles_ref[base + batch * BATCH + which]
            column, line = lax.rem(code, column_tiles), code // column_tiles
            part, first = column // tiles_per_part, lax.rem(column, tiles_per_part) * per_tile
            field = fields[part, pl.ds(first, per_tile), lax.rem(line, freqs)].reshape(TILE, lanes)
            swapped = pltpu.roll(field.astype(F32), half, 1)
            swapped = jnp.where(left, -swapped, swapped).astype(BF16)
            both = jnp.concatenate([slots[slot, which, 0], slots[slot, which, 1]], axis=1)
            results.append((line, dot(both, jnp.concatenate([field, swapped], axis=0))))
        for line, result in results:
            sums[line] += result
        return 0

    lax.fori_loop(0, batches, batch_step, 0)

    def finish(line, _):
        freq, row_tile = lax.rem(line, freqs), line // freqs
        bands = sums[line].astype(BF16).reshape(per_tile, depth, lanes)
        out_ref[pl.ds(row_tile * per_tile, per_tile), freq] = bands
        return 0

    lax.fori_loop(0, lines, finish, 0)


def product_call(part, tiles, count, places, kernel, fields, out):
    owners, freqs, depth, lanes = fields[0].shape
    freqs = freqs // PARTS
    lines = kernel.shape[2] // TILE * freqs
    parts = len(fields)
    smem = pl.BlockSpec(memory_space=pltpu.SMEM)
    anywhere = pl.BlockSpec(memory_space=pl.ANY)
    operands = [tiles, count, places, kernel, *fields]
    aliases = {}
    if out is not None:
        aliases = {len(operands): 0}
        operands.append(out)
    return pl.pallas_call(
        functools.partial(product_kernel, which_part=part, parts=parts),
        grid=(1,),
        in_specs=[smem, smem, smem] + [anywhere] * (len(operands) - 3),
        out_specs=pl.BlockSpec((owners, freqs, depth, lanes), lambda g: (0, part, 0, 0)),
        out_shape=jax.ShapeDtypeStruct(fields[0].shape, BF16),
        scratch_shapes=[
            pltpu.VMEM((parts, owners, freqs, depth, lanes), BF16),
            pltpu.VMEM((lines + 1, TILE, lanes), F32),
            pltpu.VMEM((SLOTS, BATCH, 2, TILE, TILE), BF16),
            pltpu.SemaphoreType.DMA((SLOTS, BATCH)),
            pltpu.SemaphoreType.DMA((parts,)),
        ],
        input_output_aliases=aliases,
        compiler_params=pltpu.CompilerParams(vmem_limit_bytes=VMEM_LIMIT),
        cost_estimate=pl.CostEstimate(
            flops=2 * kernel.size * lanes // 8 // PARTS,
            bytes_accessed=kernel.size // 4 // PARTS,
            transcendentals=0,
        ),
    )(*operands)


def local(kernel, tile_mask, direct, onsets, *, owners, halves):
    receivers, focal, _ = direct.shape
    tables = phase_tables()
    onsets = onsets.reshape(receivers // GROUP, GROUP, focal).transpose(0, 2, 1)
    mine = lax.axis_index("rows")
    places = jnp.stack([lax.rem(mine - shift + halves, halves) for shift in range(halves)]).astype(jnp.int32)
    tiles, count = list_call(tile_mask)

    def across(rows):
        return lax.all_to_all(rows, "freq", 0, 0, tiled=True)

    def exchange(fields, part):
        freqs = fields.shape[1] // PARTS
        piece = lax.slice_in_dim(fields, part * freqs, (part + 1) * freqs, axis=1)
        got = [fields]
        for shift in range(1, halves):
            ring = [(place, (place + shift) % halves) for place in range(halves)]
            got.append(lax.ppermute(piece, "rows", ring))
        return got

    def time_at(kind, chunk, *operands):
        return time_call(kind, chunk, owners, direct, tables, *operands)

    rows = [time_at("first", chunk) for chunk in range(CHUNKS)]
    out = None
    for turn in range(ITERS):
        bands = [None] * CHUNKS
        for chunk in range(CHUNKS):
            fields = across(rows[chunk])
            for part in range(PARTS):
                both = exchange(fields, part)
                bands[chunk] = product_call(part, tiles, count, places, kernel, both, bands[chunk])
        bands = [across(bands[chunk]) for chunk in range(CHUNKS)]
        for chunk in range(CHUNKS):
            if turn + 1 < ITERS:
                rows[chunk] = time_at("middle", chunk, onsets, bands[chunk])
            else:
                out = time_at("last", chunk, onsets, bands[chunk], out)
    return out


def solution(mesh):
    owners, halves = mesh.shape["freq"], mesh.shape["rows"]
    return jax.shard_map(
        functools.partial(local, owners=owners, halves=halves),
        mesh=mesh,
        in_specs=(
            P(None, "freq", "rows", None),
            P("freq", "rows", None),
            P(("rows", "freq"), None, None),
            P(("rows", "freq"), None),
        ),
        out_specs=P(("rows", "freq"), None, None),
        check_vma=False,
    )
```

time: 862 us -> 496 us (0.58)
  blocking collectives: 296 us -> 0 us
  matrix products: 211 us -> 0 us
  Pallas kernels: 0 us -> 135 us
  waiting for transfers between devices: 172 us -> 257 us
  local copies, waits for them, and re-layouts: 94.9 us -> 18.5 us
  starting transfers between devices: 7.63 us -> 76.4 us
  other arithmetic: 58 us -> 2.02 us
  between operations: 14.1 us -> 0.21 us
    all_to_all x3 -> x0, blocking collectives: 296 us -> none  [the longest x2 198 us: forward(): lax.all_to_all(bands, 'freq', split_axis=2, concat_axis=1, tiled=True)]
    dot_general x12 -> x0, matrix products: 211 us -> none  [the longest x2 37.7 us: forward(): jnp.einsum('kjrp,kjt->rpt', traces.astype(jnp.float32), dft_table, precis...]
    all_gather x2 -> x0, waiting for transfers between devices: 164 us -> none  [products(): return multiply(masked, lax.all_gather(fields, 'rows', axis=2, tiled=True))]
    ppermute x0 -> x8, waiting for transfers between devices: none -> 139 us  [exchange(): got.append(lax.ppermute(piece, 'rows', ring))]
    pallas_call x0 -> x15, Pallas kernels: none -> 135 us  [the longest x6 67.1 us: time_call(): pl.pallas_call(functools.partial(body, half=half), grid=(receivers // GRO...]
    all_to_all x1 -> x8, waiting for transfers between devices: 7.54 us -> 117 us  [across(): return lax.all_to_all(rows, 'freq', 0, 0, tiled=True)]
    all_to_all x1 -> x8, starting transfers between devices: 7.34 us -> 70.4 us  [across(): return lax.all_to_all(rows, 'freq', 0, 0, tiled=True)]
    convert_element_type x3 -> x0, local copies, waits for them, and re-layouts: 56.7 us -> none  [the longest x1 49.3 us: local(): jnp.repeat(jnp.repeat(tile_mask, TILE, axis=1), TILE, axis=2)]
  transfers between devices with their start and end apart: 3 -> 16, of which waited for: 3 -> 12; matrix products, arithmetic and copies ran while one was open for 15% -> 2% of each run, Pallas kernels for 0% -> 24%
where the time goes in v1:
time: 496 us; the launch traced here: 489 us
  waiting for transfers between devices  257 us (52%)
  Pallas kernels  135 us (27%)
  starting transfers between devices  76.4 us (15%)
  local copies, waits for them, and re-layouts  18.5 us (4%)
    ppermute x8, waiting for transfers between devices, exchange(): got.append(lax.ppermute(piece, 'rows', ring))  139 us
    all_to_all x8, waiting for transfers between devices, across(): return lax.all_to_all(rows, 'freq', 0, 0, tiled=True)  117 us
    all_to_all x8, starting transfers between devices, across(): return lax.all_to_all(rows, 'freq', 0, 0, tiled=True)  70.4 us
    pallas_call x6, Pallas kernels, time_call(): pl.pallas_call(functools.partial(body, half=half), grid=(receivers // GRO...  67.1 us
    pallas_call x8, Pallas kernels, product_call(): pl.pallas_call(functools.partial(product_kernel, which_part=part, parts=p...  63.5 us
    unnamed x26, local copies, waits for them, and re-layouts  11.3 us
  transfers between devices with their start and end apart: 16, of which 12 were waited for; matrix products, arithmetic and copies ran while one was open for 2% of the time, Pallas kernels for 24%

profile of v1, /device:TPU:1, one launch (start us, length us, event | category | flops | bytes accessed | tf_op | source)
XLA Modules:
  0.0 489.0 jit_solution(14259021696262434870)
XLA Ops:
  0.0 0.6 fusion.7
  0.7 0.7 pad_maximum_fusion.tables_ref
  1.4 8.9 %shard_map.52 = bf16[16,8,64,128]{3,2,1,0:T(8,128)(2,1)} custom-call(f32[64,128,512]{2,1,0:T(8,128)} %direct_ref.11, bf16[2,256,256]{2,1,0:T(8,128)(2,1)} %pad_maximum_fusion.tables_ref), custom_call_target="tpu_custom_call" | custom-call | flops 3221225472 | bytes 16777216 | tf_op jit(solution)/shard_map/pallas_call | solution.py:159
  10.3 7.3 %all-to-all-start.4 = ((bf16[16,8,64,128]{3,2,1,0:T(8,128)(2,1)}), bf16[16,8,64,128]{3,2,1,0:T(8,128)(2,1)S(1)}, u32[]{:S(2)}, u32[]{:S(2)}) async-start(bf16[16,8,64,128]{3,2,1,0:T(8,128)(2,1)} %shard_map.52), calls=%async_computation.4 | async-start | bytes 4194304 | tf_op jit(solution)/shard_map/all_to_all | solution.py:333
  17.7 8.9 %shard_map.46 = bf16[16,8,64,128]{3,2,1,0:T(8,128)(2,1)} custom-call(f32[64,128,512]{2,1,0:T(8,128)} %direct_ref.11, bf16[2,256,256]{2,1,0:T(8,128)(2,1)} %pad_maximum_fusion.tables_ref), custom_call_target="tpu_custom_call" | custom-call | flops 3221225472 | bytes 16777216 | tf_op jit(solution)/shard_map/pallas_call | solution.py:159
  26.6 32.6 %all-to-all-done.4.rest_0_ = bf16[16,8,64,128]{3,2,1,0:T(8,128)(2,1)S(1)} async-done(((bf16[16,8,64,128]{3,2,1,0:T(8,128)(2,1)}), bf16[16,8,64,128]{3,2,1,0:T(8,128)(2,1)S(1)}, u32[]{:S(2)}, u32[]{:S(2)}) %all-to-all-start.4) | async-done | bytes 2097184 | tf_op jit(solution)/shard_map/all_to_all | solution.py:333
  59.2 1.4 copy-done.1
  60.6 10.7 %all-to-all-start = ((bf16[16,8,64,128]{3,2,1,0:T(8,128)(2,1)}), bf16[16,8,64,128]{3,2,1,0:T(8,128)(2,1)S(1)}, u32[]{:S(2)}, u32[]{:S(2)}) async-start(bf16[16,8,64,128]{3,2,1,0:T(8,128)(2,1)} %shard_map.46), calls=%async_computation | async-start | bytes 4194304 | tf_op jit(solution)/shard_map/all_to_all | solution.py:333
  71.2 3.2 fusion.9
  74.4 1.2 collective-permute-start.5
  75.6 0.3 collective-permute-start.4
  75.9 4.8 list_tiles.1
  80.7 0.6 pad_add_fusion.place_ref
  81.4 17.9 %collective-permute-done.5.rest_1_ = bf16[16,4,64,128]{3,2,1,0:T(8,128)(2,1)S(1)} collective-permute-done((bf16[16,4,64,128]{3,2,1,0:T(8,128)(2,1)}, bf16[16,4,64,128]{3,2,1,0:T(8,128)(2,1)S(1)}, u32[]{:S(2)}, u32[]{:S(2)}) %collective-permute-start.5) | collective-permute-done | bytes 1048608 | tf_op jit(solution)/shard_map/ppermute | solution.py:341
  99.2 1.0 copy-done.6
  100.2 8.5 %shard_map.53.rest_2_ = bf16[16,8,64,128]{3,2,1,0:T(8,128)(2,1)} custom-call(s32[1040]{0:T(1024)} %get-tuple-element.7.tiles_ref, s32[2]{0:T(128)} %get-tuple-element.8.count_ref, s32[2]{0:T(128)} %pad_add_fusion.place_ref, bf16[2,8,1024,2048]{3,2,1,0:T(8,128)(2,1)} %kernel_ref.15, bf16[16,8,64,128]{3,2,1,0:T(8,128)(2,1)} %copy-done.1, ...), custom_call_target="tpu_custom_call" | custom-call | flops 536870912 | bytes 4194304 | tf_op jit(solution)/shard_map/pallas_call | solution.py:301
  108.7 13.1 %collective-permute-done.4.rest_1_ = bf16[16,4,64,128]{3,2,1,0:T(8,128)(2,1)} collective-permute-done((bf16[16,4,64,128]{3,2,1,0:T(8,128)(2,1)}, bf16[16,4,64,128]{3,2,1,0:T(8,128)(2,1)}, u32[]{:S(2)}, u32[]{:S(2)}) %collective-permute-start.4) | collective-permute-done | bytes 1048608 | tf_op jit(solution)/shard_map/ppermute | solution.py:341
  121.8 7.4 %shard_map.54 = bf16[16,8,64,128]{3,2,1,0:T(8,128)(2,1)} custom-call(s32[1040]{0:T(1024)} %get-tuple-element.7.tiles_ref, s32[2]{0:T(128)} %get-tuple-element.8.count_ref, s32[2]{0:T(128)} %pad_add_fusion.place_ref, bf16[2,8,1024,2048]{3,2,1,0:T(8,128)(2,1)} %kernel_ref.15, bf16[16,8,64,128]{3,2,1,0:T(8,128)(2,1)} %copy-done.1, ...), custom_call_target="tpu_custom_call", output_to_operand_aliasing={{}: (6, {})} | custom-call | flops 536870912 | bytes 4194304 | tf_op jit(solution)/shard_map/pallas_call | solution.py:301
  129.2 0.0 copy-start
  129.2 7.8 %all-to-all-start.5 = ((bf16[16,8,64,128]{3,2,1,0:T(8,128)(2,1)}), bf16[16,8,64,128]{3,2,1,0:T(8,128)(2,1)}, u32[]{:S(2)}, u32[]{:S(2)}) async-start(bf16[16,8,64,128]{3,2,1,0:T(8,128)(2,1)} %shard_map.54), calls=%async_computation.5 | async-start | bytes 4194304 | tf_op jit(solution)/shard_map/all_to_all | solution.py:333
  137.0 0.2 fusion.11
  137.2 0.8 collective-permute-start.1
  138.0 0.7 collective-permute-start
  138.7 23.2 %collective-permute-done.1.rest_1_ = bf16[16,4,64,128]{3,2,1,0:T(8,128)(2,1)S(1)} collective-permute-done((bf16[16,4,64,128]{3,2,1,0:T(8,128)(2,1)S(1)}, bf16[16,4,64,128]{3,2,1,0:T(8,128)(2,1)S(1)}, u32[]{:S(2)}, u32[]{:S(2)}) %collective-permute-start.1) | collective-permute-done | bytes 1048608 | tf_op jit(solution)/shard_map/ppermute | solution.py:341
  161.9 1.0 copy-done.7
  162.9 8.5 %shard_map.47.rest_2_ = bf16[16,8,64,128]{3,2,1,0:T(8,128)(2,1)} custom-call(s32[1040]{0:T(1024)} %get-tuple-element.7.tiles_ref, s32[2]{0:T(128)} %get-tuple-element.8.count_ref, s32[2]{0:T(128)} %pad_add_fusion.place_ref, bf16[2,8,1024,2048]{3,2,1,0:T(8,128)(2,1)} %kernel_ref.15, bf16[16,8,64,128]{3,2,1,0:T(8,128)(2,1)} %copy-done, ...), custom_call_target="tpu_custom_call" | custom-call | flops 536870912 | bytes 4194304 | tf_op jit(solution)/shard_map/pallas_call | solution.py:301
  171.4 12.9 %collective-permute-done.rest_1_ = bf16[16,4,64,128]{3,2,1,0:T(8,128)(2,1)S(1)} collective-permute-done((bf16[16,4,64,128]{3,2,1,0:T(8,128)(2,1)S(1)}, bf16[16,4,64,128]{3,2,1,0:T(8,128)(2,1)S(1)}, u32[]{:S(2)}, u32[]{:S(2)}) %collective-permute-start) | collective-permute-done | bytes 1048608 | tf_op jit(solution)/shard_map/ppermute | solution.py:341
  184.3 1.0 copy-done.11
  185.3 7.3 %shard_map.48 = bf16[16,8,64,128]{3,2,1,0:T(8,128)(2,1)} custom-call(s32[1040]{0:T(1024)} %get-tuple-element.7.tiles_ref, s32[2]{0:T(128)} %get-tuple-element.8.count_ref, s32[2]{0:T(128)} %pad_add_fusion.place_ref, bf16[2,8,1024,2048]{3,2,1,0:T(8,128)(2,1)} %kernel_ref.15, bf16[16,8,64,128]{3,2,1,0:T(8,128)(2,1)} %copy-done, ...), custom_call_target="tpu_custom_call", output_to_operand_aliasing={{}: (6, {})} | custom-call | flops 536870912 | bytes 4194304 | tf_op jit(solution)/shard_map/pallas_call | solution.py:301
  192.6 0.0 copy-start.12
  192.6 7.8 %all-to-all-start.1 = ((bf16[16,8,64,128]{3,2,1,0:T(8,128)(2,1)}), bf16[16,8,64,128]{3,2,1,0:T(8,128)(2,1)S(1)}, u32[]{:S(2)}, u32[]{:S(2)}) async-start(bf16[16,8,64,128]{3,2,1,0:T(8,128)(2,1)} %shard_map.48), calls=%async_computation.1 | async-start | bytes 4194304 | tf_op jit(solution)/shard_map/all_to_all | solution.py:333
  200.4 0.9 copy.10
  201.3 14.4 %shard_map.55 = bf16[16,8,64,128]{3,2,1,0:T(8,128)(2,1)} custom-call(f32[64,128,512]{2,1,0:T(8,128)} %direct_ref.11, bf16[2,256,256]{2,1,0:T(8,128)(2,1)} %pad_maximum_fusion.tables_ref, s32[4,128,16]{2,1,0:T(8,128)} %bitcast.9, bf16[16,8,64,128]{3,2,1,0:T(8,128)(2,1)} %all-to-all-done.5.bands_ref), custom_call_target="tpu_custom_call" | custom-call | flops 5368709120 | bytes 16777216 | tf_op jit(solution)/shard_map/pallas_call | solution.py:159
  215.8 26.2 %all-to-all-done.1.bands_ref = bf16[16,8,64,128]{3,2,1,0:T(8,128)(2,1)S(1)} async-done(((bf16[16,8,64,128]{3,2,1,0:T(8,128)(2,1)}), bf16[16,8,64,128]{3,2,1,0:T(8,128)(2,1)S(1)}, u32[]{:S(2)}, u32[]{:S(2)}) %all-to-all-start.1) | async-done | bytes 2097184 | tf_op jit(solution)/shard_map/all_to_all | solution.py:333
  242.0 1.3 copy-done.5
  243.3 10.7 %all-to-all-start.6 = ((bf16[16,8,64,128]{3,2,1,0:T(8,128)(2,1)}), bf16[16,8,64,128]{3,2,1,0:T(8,128)(2,1)S(1)}, u32[]{:S(2)}, u32[]{:S(2)}) async-start(bf16[16,8,64,128]{3,2,1,0:T(8,128)(2,1)} %shard_map.55), calls=%async_computation.6 | async-start | bytes 4194304 | tf_op jit(solution)/shard_map/all_to_all | solution.py:333
  253.9 14.5 %shard_map.49 = bf16[16,8,64,128]{3,2,1,0:T(8,128)(2,1)} custom-call(f32[64,128,512]{2,1,0:T(8,128)} %direct_ref.11, bf16[2,256,256]{2,1,0:T(8,128)(2,1)} %pad_maximum_fusion.tables_ref, s32[4,128,16]{2,1,0:T(8,128)} %bitcast.10, bf16[16,8,64,128]{3,2,1,0:T(8,128)(2,1)} %copy-done.5), custom_call_target="tpu_custom_call" | custom-call | flops 5368709120 | bytes 16777216 | tf_op jit(solution)/shard_map/pallas_call | solution.py:159
  268.4 27.0 %all-to-all-done.6.rest_0_ = bf16[16,8,64,128]{3,2,1,0:T(8,128)(2,1)S(1)} async-done(((bf16[16,8,64,128]{3,2,1,0:T(8,128)(2,1)}), bf16[16,8,64,128]{3,2,1,0:T(8,128)(2,1)S(1)}, u32[]{:S(2)}, u32[]{:S(2)}) %all-to-all-start.6) | async-done | bytes 2097184 | tf_op jit(solution)/shard_map/all_to_all | solution.py:333
  295.5 1.3 copy-done.3
  296.8 10.7 %all-to-all-start.2 = ((bf16[16,8,64,128]{3,2,1,0:T(8,128)(2,1)}), bf16[16,8,64,128]{3,2,1,0:T(8,128)(2,1)S(1)}, u32[]{:S(2)}, u32[]{:S(2)}) async-start(bf16[16,8,64,128]{3,2,1,0:T(8,128)(2,1)} %shard_map.49), calls=%async_computation.2 | async-start | bytes 4194304 | tf_op jit(solution)/shard_map/all_to_all | solution.py:333
  307.5 2.7 fusion.8
  310.2 0.3 collective-permute-start.7
  310.5 1.2 collective-permute-start.6
  311.7 23.1 %collective-permute-done.7.rest_1_ = bf16[16,4,64,128]{3,2,1,0:T(8,128)(2,1)S(1)} collective-permute-done((bf16[16,4,64,128]{3,2,1,0:T(8,128)(2,1)S(1)}, bf16[16,4,64,128]{3,2,1,0:T(8,128)(2,1)S(1)}, u32[]{:S(2)}, u32[]{:S(2)}) %collective-permute-start.7) | collective-permute-done | bytes 1048608 | tf_op jit(solution)/shard_map/ppermute | solution.py:341
  334.8 1.0 copy-done.8
  335.8 8.5 %shard_map.56.rest_2_ = bf16[16,8,64,128]{3,2,1,0:T(8,128)(2,1)} custom-call(s32[1040]{0:T(1024)} %get-tuple-element.7.tiles_ref, s32[2]{0:T(128)} %get-tuple-element.8.count_ref, s32[2]{0:T(128)} %pad_add_fusion.place_ref, bf16[2,8,1024,2048]{3,2,1,0:T(8,128)(2,1)} %kernel_ref.15, bf16[16,8,64,128]{3,2,1,0:T(8,128)(2,1)} %copy-done.3, ...), custom_call_target="tpu_custom_call" | custom-call | flops 536870912 | bytes 4194304 | tf_op jit(solution)/shard_map/pallas_call | solution.py:301
  344.3 13.1 %collective-permute-done.6.rest_1_ = bf16[16,4,64,128]{3,2,1,0:T(8,128)(2,1)} collective-permute-done((bf16[16,4,64,128]{3,2,1,0:T(8,128)(2,1)}, bf16[16,4,64,128]{3,2,1,0:T(8,128)(2,1)}, u32[]{:S(2)}, u32[]{:S(2)}) %collective-permute-start.6) | collective-permute-done | bytes 1048608 | tf_op jit(solution)/shard_map/ppermute | solution.py:341
  357.4 7.4 %shard_map.57 = bf16[16,8,64,128]{3,2,1,0:T(8,128)(2,1)} custom-call(s32[1040]{0:T(1024)} %get-tuple-element.7.tiles_ref, s32[2]{0:T(128)} %get-tuple-element.8.count_ref, s32[2]{0:T(128)} %pad_add_fusion.place_ref, bf16[2,8,1024,2048]{3,2,1,0:T(8,128)(2,1)} %kernel_ref.15, bf16[16,8,64,128]{3,2,1,0:T(8,128)(2,1)} %copy-done.3, ...), custom_call_target="tpu_custom_call", output_to_operand_aliasing={{}: (6, {})} | custom-call | flops 536870912 | bytes 4194304 | tf_op jit(solution)/shard_map/pallas_call | solution.py:301
  364.8 0.0 copy-start.2
  364.8 7.8 %all-to-all-start.7 = ((bf16[16,8,64,128]{3,2,1,0:T(8,128)(2,1)}), bf16[16,8,64,128]{3,2,1,0:T(8,128)(2,1)}, u32[]{:S(2)}, u32[]{:S(2)}) async-start(bf16[16,8,64,128]{3,2,1,0:T(8,128)(2,1)} %shard_map.57), calls=%async_computation.7 | async-start | bytes 4194304 | tf_op jit(solution)/shard_map/all_to_all | solution.py:333
  372.5 0.2 fusion.10
  372.7 0.1 collective-permute-start.3
  372.8 1.5 collective-permute-start.2
  374.3 23.2 %collective-permute-done.3.rest_1_ = bf16[16,4,64,128]{3,2,1,0:T(8,128)(2,1)S(1)} collective-permute-done((bf16[16,4,64,128]{3,2,1,0:T(8,128)(2,1)S(1)}, bf16[16,4,64,128]{3,2,1,0:T(8,128)(2,1)S(1)}, u32[]{:S(2)}, u32[]{:S(2)}) %collective-permute-start.3) | collective-permute-done | bytes 1048608 | tf_op jit(solution)/shard_map/ppermute | solution.py:341
  397.5 1.0 copy-done.9
  398.4 8.5 %shard_map.50.rest_2_ = bf16[16,8,64,128]{3,2,1,0:T(8,128)(2,1)} custom-call(s32[1040]{0:T(1024)} %get-tuple-element.7.tiles_ref, s32[2]{0:T(128)} %get-tuple-element.8.count_ref, s32[2]{0:T(128)} %pad_add_fusion.place_ref, bf16[2,8,1024,2048]{3,2,1,0:T(8,128)(2,1)} %kernel_ref.15, bf16[16,8,64,128]{3,2,1,0:T(8,128)(2,1)} %copy-done.2, ...), custom_call_target="tpu_custom_call" | custom-call | flops 536870912 | bytes 4194304 | tf_op jit(solution)/shard_map/pallas_call | solution.py:301
  406.9 12.9 %collective-permute-done.2.rest_1_ = bf16[16,4,64,128]{3,2,1,0:T(8,128)(2,1)S(1)} collective-permute-done((bf16[16,4,64,128]{3,2,1,0:T(8,128)(2,1)S(1)}, bf16[16,4,64,128]{3,2,1,0:T(8,128)(2,1)S(1)}, u32[]{:S(2)}, u32[]{:S(2)}) %collective-permute-start.2) | collective-permute-done | bytes 1048608 | tf_op jit(solution)/shard_map/ppermute | solution.py:341
  419.8 1.0 copy-done.10
  420.8 7.4 %shard_map.51 = bf16[16,8,64,128]{3,2,1,0:T(8,128)(2,1)} custom-call(s32[1040]{0:T(1024)} %get-tuple-element.7.tiles_ref, s32[2]{0:T(128)} %get-tuple-element.8.count_ref, s32[2]{0:T(128)} %pad_add_fusion.place_ref, bf16[2,8,1024,2048]{3,2,1,0:T(8,128)(2,1)} %kernel_ref.15, bf16[16,8,64,128]{3,2,1,0:T(8,128)(2,1)} %copy-done.2, ...), custom_call_target="tpu_custom_call", output_to_operand_aliasing={{}: (6, {})} | custom-call | flops 536870912 | bytes 4194304 | tf_op jit(solution)/shard_map/pallas_call | solution.py:301
  428.2 7.8 %all-to-all-start.3 = ((bf16[16,8,64,128]{3,2,1,0:T(8,128)(2,1)}), bf16[16,8,64,128]{3,2,1,0:T(8,128)(2,1)S(1)}, u32[]{:S(2)}, u32[]{:S(2)}) async-start(bf16[16,8,64,128]{3,2,1,0:T(8,128)(2,1)} %shard_map.51), calls=%async_computation.3 | async-start | bytes 4194304 | tf_op jit(solution)/shard_map/all_to_all | solution.py:333
  436.0 10.2 %shard_map.58.rest_0_ = f32[64,128,512]{2,1,0:T(8,128)} custom-call(f32[64,128,512]{2,1,0:T(8,128)} %direct_ref.11, bf16[2,256,256]{2,1,0:T(8,128)(2,1)} %pad_maximum_fusion.tables_ref, s32[4,128,16]{2,1,0:T(8,128)} %bitcast.11, bf16[16,8,64,128]{3,2,1,0:T(8,128)(2,1)} %all-to-all-done.7.bands_ref), custom_call_target="tpu_custom_call" | custom-call | flops 2147483648 | bytes 16777216 | tf_op jit(solution)/shard_map/pallas_call | solution.py:159
  446.2 31.4 %all-to-all-done.3.bands_ref = bf16[16,8,64,128]{3,2,1,0:T(8,128)(2,1)S(1)} async-done(((bf16[16,8,64,128]{3,2,1,0:T(8,128)(2,1)}), bf16[16,8,64,128]{3,2,1,0:T(8,128)(2,1)S(1)}, u32[]{:S(2)}, u32[]{:S(2)}) %all-to-all-start.3) | async-done | bytes 2097184 | tf_op jit(solution)/shard_map/all_to_all | solution.py:333
  477.5 1.4 copy-done.4
  478.9 10.1 %shard_map.59 = f32[64,128,512]{2,1,0:T(8,128)} custom-call(f32[64,128,512]{2,1,0:T(8,128)} %direct_ref.11, bf16[2,256,256]{2,1,0:T(8,128)(2,1)} %pad_maximum_fusion.tables_ref, s32[4,128,16]{2,1,0:T(8,128)} %bitcast.12, bf16[16,8,64,128]{3,2,1,0:T(8,128)(2,1)} %copy-done.4, f32[64,128,512]{2,1,0:T(8,128)} %shard_map.58.rest_0_), custom_call_target="tpu_custom_call", output_to_operand_aliasing={{}: (4, {})} | custom-call | flops 2147483648 | bytes 16777216 | tf_op jit(solution)/shard_map/pallas_call | solution.py:159
  (20 shorter events, 0.1 us)
Async XLA Ops:
  10.3 48.9 %all-to-all-start.4 = ((bf16[16,8,64,128]{3,2,1,0:T(8,128)(2,1)}), bf16[16,8,64,128]{3,2,1,0:T(8,128)(2,1)S(1)}, u32[]{:S(2)}, u32[]{:S(2)}) async-start(bf16[16,8,64,128]{3,2,1,0:T(8,128)(2,1)} %shard_map.52), calls=%async_computation.4 | async-start | bytes 4194304 | tf_op jit(solution)/shard_map/all_to_all | solution.py:333
  59.2 1.4 copy-start.1
  60.6 68.6 %all-to-all-start = ((bf16[16,8,64,128]{3,2,1,0:T(8,128)(2,1)}), bf16[16,8,64,128]{3,2,1,0:T(8,128)(2,1)S(1)}, u32[]{:S(2)}, u32[]{:S(2)}) async-start(bf16[16,8,64,128]{3,2,1,0:T(8,128)(2,1)} %shard_map.46), calls=%async_computation | async-start | bytes 4194304 | tf_op jit(solution)/shard_map/all_to_all | solution.py:333
  74.4 24.8 %collective-permute-start.5 = (bf16[16,4,64,128]{3,2,1,0:T(8,128)(2,1)}, bf16[16,4,64,128]{3,2,1,0:T(8,128)(2,1)S(1)}, u32[]{:S(2)}, u32[]{:S(2)}) collective-permute-start(bf16[16,4,64,128]{3,2,1,0:T(8,128)(2,1)} %get-tuple-element.11), channel_id=1, source_target_pairs={{0,1},{1,0},{2,3},{3,2},{4,5},{5,4},{6,7},{7,6},{8,9},{9,8},{10,11... | collective-permute-start | bytes 3145736 | tf_op jit(solution)/shard_map/ppermute | solution.py:341
  75.6 46.2 %collective-permute-start.4 = (bf16[16,4,64,128]{3,2,1,0:T(8,128)(2,1)}, bf16[16,4,64,128]{3,2,1,0:T(8,128)(2,1)}, u32[]{:S(2)}, u32[]{:S(2)}) collective-permute-start(bf16[16,4,64,128]{3,2,1,0:T(8,128)(2,1)} %get-tuple-element.12), channel_id=1, source_target_pairs={{0,1},{1,0},{2,3},{3,2},{4,5},{5,4},{6,7},{7,6},{8,9},{9,8},{10,11... | collective-permute-start | bytes 3145736 | tf_op jit(solution)/shard_map/ppermute | solution.py:341
  99.2 1.0 copy-start.6
  129.2 7.8 %copy-start = (bf16[16,8,64,128]{3,2,1,0:T(8,128)(2,1)}, bf16[16,8,64,128]{3,2,1,0:T(8,128)(2,1)S(1)}, u32[]{:S(2)}) copy-start(bf16[16,8,64,128]{3,2,1,0:T(8,128)(2,1)S(1)} %all-to-all-done.rest_0_) | copy-start | bytes 6291460
  129.2 63.4 %all-to-all-start.5 = ((bf16[16,8,64,128]{3,2,1,0:T(8,128)(2,1)}), bf16[16,8,64,128]{3,2,1,0:T(8,128)(2,1)}, u32[]{:S(2)}, u32[]{:S(2)}) async-start(bf16[16,8,64,128]{3,2,1,0:T(8,128)(2,1)} %shard_map.54), calls=%async_computation.5 | async-start | bytes 4194304 | tf_op jit(solution)/shard_map/all_to_all | solution.py:333
  137.2 24.7 %collective-permute-start.1 = (bf16[16,4,64,128]{3,2,1,0:T(8,128)(2,1)S(1)}, bf16[16,4,64,128]{3,2,1,0:T(8,128)(2,1)S(1)}, u32[]{:S(2)}, u32[]{:S(2)}) collective-permute-start(bf16[16,4,64,128]{3,2,1,0:T(8,128)(2,1)S(1)} %get-tuple-element.15), channel_id=1, source_target_pairs={{0,1},{1,0},{2,3},{3,2},{4,5},{5,4},{6,7},{7,6},{8,9},{9,8},{10,11... | collective-permute-start | bytes 3145736 | tf_op jit(solution)/shard_map/ppermute | solution.py:341
  138.0 46.3 %collective-permute-start = (bf16[16,4,64,128]{3,2,1,0:T(8,128)(2,1)S(1)}, bf16[16,4,64,128]{3,2,1,0:T(8,128)(2,1)S(1)}, u32[]{:S(2)}, u32[]{:S(2)}) collective-permute-start(bf16[16,4,64,128]{3,2,1,0:T(8,128)(2,1)S(1)} %get-tuple-element.16), channel_id=1, source_target_pairs={{0,1},{1,0},{2,3},{3,2},{4,5},{5,4},{6,7},{7,6},{8,9},{9,8},{10,11... | collective-permute-start | bytes 3145736 | tf_op jit(solution)/shard_map/ppermute | solution.py:341
  161.9 1.0 copy-start.7
  184.3 1.0 copy-start.11
  192.6 7.8 %copy-start.12 = (s32[64,128]{1,0:T(8,128)S(1)}, s32[64,128]{1,0:T(8,128)}, u32[]{:S(2)}) copy-start(s32[64,128]{1,0:T(8,128)} %param.7) | copy-start | bytes 98308
  192.6 49.3 %all-to-all-start.1 = ((bf16[16,8,64,128]{3,2,1,0:T(8,128)(2,1)}), bf16[16,8,64,128]{3,2,1,0:T(8,128)(2,1)S(1)}, u32[]{:S(2)}, u32[]{:S(2)}) async-start(bf16[16,8,64,128]{3,2,1,0:T(8,128)(2,1)} %shard_map.48), calls=%async_computation.1 | async-start | bytes 4194304 | tf_op jit(solution)/shard_map/all_to_all | solution.py:333
  242.0 1.3 copy-start.5
  243.3 52.2 %all-to-all-start.6 = ((bf16[16,8,64,128]{3,2,1,0:T(8,128)(2,1)}), bf16[16,8,64,128]{3,2,1,0:T(8,128)(2,1)S(1)}, u32[]{:S(2)}, u32[]{:S(2)}) async-start(bf16[16,8,64,128]{3,2,1,0:T(8,128)(2,1)} %shard_map.55), calls=%async_computation.6 | async-start | bytes 4194304 | tf_op jit(solution)/shard_map/all_to_all | solution.py:333
  295.5 1.3 copy-start.3
  296.8 68.0 %all-to-all-start.2 = ((bf16[16,8,64,128]{3,2,1,0:T(8,128)(2,1)}), bf16[16,8,64,128]{3,2,1,0:T(8,128)(2,1)S(1)}, u32[]{:S(2)}, u32[]{:S(2)}) async-start(bf16[16,8,64,128]{3,2,1,0:T(8,128)(2,1)} %shard_map.49), calls=%async_computation.2 | async-start | bytes 4194304 | tf_op jit(solution)/shard_map/all_to_all | solution.py:333
  310.2 24.6 %collective-permute-start.7 = (bf16[16,4,64,128]{3,2,1,0:T(8,128)(2,1)S(1)}, bf16[16,4,64,128]{3,2,1,0:T(8,128)(2,1)S(1)}, u32[]{:S(2)}, u32[]{:S(2)}) collective-permute-start(bf16[16,4,64,128]{3,2,1,0:T(8,128)(2,1)S(1)} %get-tuple-element.9), channel_id=1, source_target_pairs={{0,1},{1,0},{2,3},{3,2},{4,5},{5,4},{6,7},{7,6},{8,9},{9,8},{10,11... | collective-permute-start | bytes 3145736 | tf_op jit(solution)/shard_map/ppermute | solution.py:341
  310.5 46.9 %collective-permute-start.6 = (bf16[16,4,64,128]{3,2,1,0:T(8,128)(2,1)}, bf16[16,4,64,128]{3,2,1,0:T(8,128)(2,1)}, u32[]{:S(2)}, u32[]{:S(2)}) collective-permute-start(bf16[16,4,64,128]{3,2,1,0:T(8,128)(2,1)} %get-tuple-element.10), channel_id=1, source_target_pairs={{0,1},{1,0},{2,3},{3,2},{4,5},{5,4},{6,7},{7,6},{8,9},{9,8},{10,11... | collective-permute-start | bytes 3145736 | tf_op jit(solution)/shard_map/ppermute | solution.py:341
  334.8 1.0 copy-start.8
  364.8 7.8 %copy-start.2 = (bf16[16,8,64,128]{3,2,1,0:T(8,128)(2,1)}, bf16[16,8,64,128]{3,2,1,0:T(8,128)(2,1)S(1)}, u32[]{:S(2)}) copy-start(bf16[16,8,64,128]{3,2,1,0:T(8,128)(2,1)S(1)} %all-to-all-done.2.rest_0_) | copy-start | bytes 6291460
  364.8 63.4 %all-to-all-start.7 = ((bf16[16,8,64,128]{3,2,1,0:T(8,128)(2,1)}), bf16[16,8,64,128]{3,2,1,0:T(8,128)(2,1)}, u32[]{:S(2)}, u32[]{:S(2)}) async-start(bf16[16,8,64,128]{3,2,1,0:T(8,128)(2,1)} %shard_map.57), calls=%async_computation.7 | async-start | bytes 4194304 | tf_op jit(solution)/shard_map/all_to_all | solution.py:333
  372.7 24.7 %collective-permute-start.3 = (bf16[16,4,64,128]{3,2,1,0:T(8,128)(2,1)S(1)}, bf16[16,4,64,128]{3,2,1,0:T(8,128)(2,1)S(1)}, u32[]{:S(2)}, u32[]{:S(2)}) collective-permute-start(bf16[16,4,64,128]{3,2,1,0:T(8,128)(2,1)S(1)} %get-tuple-element.13), channel_id=1, source_target_pairs={{0,1},{1,0},{2,3},{3,2},{4,5},{5,4},{6,7},{7,6},{8,9},{9,8},{10,11... | collective-permute-start | bytes 3145736 | tf_op jit(solution)/shard_map/ppermute | solution.py:341
  372.8 47.0 %collective-permute-start.2 = (bf16[16,4,64,128]{3,2,1,0:T(8,128)(2,1)S(1)}, bf16[16,4,64,128]{3,2,1,0:T(8,128)(2,1)S(1)}, u32[]{:S(2)}, u32[]{:S(2)}) collective-permute-start(bf16[16,4,64,128]{3,2,1,0:T(8,128)(2,1)S(1)} %get-tuple-element.14), channel_id=1, source_target_pairs={{0,1},{1,0},{2,3},{3,2},{4,5},{5,4},{6,7},{7,6},{8,9},{9,8},{10,11... | collective-permute-start | bytes 3145736 | tf_op jit(solution)/shard_map/ppermute | solution.py:341
  397.5 1.0 copy-start.9
  419.8 1.0 copy-start.10
  428.2 49.3 %all-to-all-start.3 = ((bf16[16,8,64,128]{3,2,1,0:T(8,128)(2,1)}), bf16[16,8,64,128]{3,2,1,0:T(8,128)(2,1)S(1)}, u32[]{:S(2)}, u32[]{:S(2)}) async-start(bf16[16,8,64,128]{3,2,1,0:T(8,128)(2,1)} %shard_map.51), calls=%async_computation.3 | async-start | bytes 4194304 | tf_op jit(solution)/shard_map/all_to_all | solution.py:333
  477.5 1.4 copy-start.4

commit v2 on v1

--- a/solution.py
+++ b/solution.py
@@ -19,7 +19,7 @@
 QUAD = 4
 SLOTS = 4
 BATCH = 8
-PARTS = 2
+REACHES = 2
 F32 = jnp.float32
 BF16 = jnp.bfloat16
 VMEM_LIMIT = 60 * 1024 * 1024
@@ -95,31 +95,37 @@
     return series - jnp.where(times < ends, traces, 0.0)
 
 
-def store_out(out_ref, rows_ref):
-    out_ref[...] = rows_ref[...].reshape(out_ref.shape).astype(BF16)
+def store_out(out_refs, rows_ref, mine):
+    for shift, out_ref in enumerate(out_refs):
+        owner = lax.bitwise_xor(mine, shift)
+        size = NF // len(out_refs) * GROUP
+        rows = rows_ref[pl.ds(pl.multiple_of(owner * size, size), size), :]
+        out_ref[...] = rows.reshape(out_ref.shape).astype(BF16)
 
 
 def load_in(rows_ref, bands_ref):
     rows_ref[...] = bands_ref[...].astype(F32).reshape(NF * GROUP, LANES)
 
 
-def first_kernel(direct_ref, tables_ref, out_ref, rows_ref, *, half):
+def first_kernel(mine_ref, direct_ref, tables_ref, *rest, half):
+    out_refs, rows_ref = rest[:-1], rest[-1]
     for first in range(0, GROUP, QUAD):
         series = direct_ref[first : first + QUAD].reshape(QUAD * half, NT)
         to_rows(series, tables_ref, rows_ref, half, first)
-    store_out(out_ref, rows_ref)
-
-
-def middle_kernel(direct_ref, tables_ref, onsets_ref, bands_ref, out_ref, in_rows, rows_ref, *, half):
+    store_out(out_refs, rows_ref, mine_ref[0])
+
+
+def middle_kernel(mine_ref, direct_ref, tables_ref, onsets_ref, bands_ref, *rest, half):
+    out_refs, (in_rows, rows_ref) = rest[:-2], rest[-2:]
     load_in(in_rows, bands_ref)
     for first in range(0, GROUP, QUAD):
         traces = to_traces(in_rows, tables_ref, half, first)
         series = subtracted(direct_ref, traces, onsets_ref, half, first)
         to_rows(series, tables_ref, rows_ref, half, first)
-    store_out(out_ref, rows_ref)
-
-
-def last_kernel(direct_ref, tables_ref, onsets_ref, bands_ref, *rest, half):
+    store_out(out_refs, rows_ref, mine_ref[0])
+
+
+def last_kernel(mine_ref, direct_ref, tables_ref, onsets_ref, bands_ref, *rest, half):
     out_ref, in_rows = rest[-2:]
     load_in(in_rows, bands_ref)
     for first in range(0, GROUP, QUAD):
@@ -128,14 +134,14 @@
         out_ref[first : first + QUAD] = series.reshape(QUAD, half, NT)
 
 
-def time_call(kind, chunk, owners, direct, tables, onsets=None, bands=None, out=None):
+def time_call(kind, chunk, owners, mine, direct, tables, onsets=None, bands=None, out=None):
     receivers, focal, _ = direct.shape
     half = focal // CHUNKS
     freqs = NF // owners
     series_spec = pl.BlockSpec((GROUP, half, NT), lambda g: (g, chunk, 0))
     rows_spec = pl.BlockSpec((owners, freqs, GROUP, LANES), lambda g: (0, 0, g, 0))
-    operands = [direct, tables]
-    specs = [series_spec, pl.BlockSpec((2, 2 * NF, NT // 2), lambda g: (0, 0, 0))]
+    operands = [mine, direct, tables]
+    specs = [pl.BlockSpec(memory_space=pltpu.SMEM), series_spec, pl.BlockSpec((2, 2 * NF, NT // 2), lambda g: (0, 0, 0))]
     if kind != "first":
         operands += [onsets, bands]
         specs += [pl.BlockSpec((1, half, GROUP), lambda g: (g, chunk, 0)), rows_spec]
@@ -148,8 +154,8 @@
     if kind == "last":
         out_specs, out_shape = series_spec, jax.ShapeDtypeStruct(direct.shape, F32)
     else:
-        out_specs = rows_spec
-        out_shape = jax.ShapeDtypeStruct((owners, freqs, receivers, LANES), BF16)
+        out_specs = [pl.BlockSpec((freqs, GROUP, LANES), lambda g: (0, g, 0))] * owners
+        out_shape = [jax.ShapeDtypeStruct((freqs, receivers, LANES), BF16)] * owners
     body, passes, scratches = {
         "first": (first_kernel, 3, 1),
         "middle": (middle_kernel, 5, 2),
@@ -173,22 +179,19 @@
 
 def list_kernel(mask_ref, tiles_ref, count_ref):
     freqs, row_tiles, column_tiles = mask_ref.shape
-    lines = row_tiles * freqs // PARTS
-    for part in range(PARTS):
-        base = part * (lines * column_tiles + BATCH)
-
-        def row(line, position, part=part):
-            row_tile, freq = line // (freqs // PARTS), lax.rem(line, freqs // PARTS)
-            for column in range(column_tiles):
-                tiles_ref[position] = line * column_tiles + column
-                kept = mask_ref[part * (freqs // PARTS) + freq, row_tile, column] != 0
-                position = position + jnp.where(kept, 1, 0)
-            return position
-
-        total = lax.fori_loop(0, lines, row, base)
-        for extra in range(BATCH):
-            tiles_ref[total + extra] = lines * column_tiles
-        count_ref[part] = (total - base + BATCH - 1) // BATCH
+    lines = row_tiles * freqs
+
+    def row(line, position):
+        row_tile, freq = line // freqs, lax.rem(line, freqs)
+        for column in range(column_tiles):
+            tiles_ref[position] = line * column_tiles + column
+            position = position + jnp.where(mask_ref[freq, row_tile, column] != 0, 1, 0)
+        return position
+
+    total = lax.fori_loop(0, lines, row, 0)
+    for extra in range(BATCH):
+        tiles_ref[total + extra] = lines * column_tiles
+    count_ref[0] = (total + BATCH - 1) // BATCH
 
 
 def list_call(tile_mask):
@@ -199,15 +202,15 @@
         in_specs=[smem],
         out_specs=[smem, smem],
         out_shape=[
-            jax.ShapeDtypeStruct((freqs * row_tiles * column_tiles + PARTS * BATCH,), jnp.int32),
-            jax.ShapeDtypeStruct((PARTS,), jnp.int32),
+            jax.ShapeDtypeStruct((freqs * row_tiles * column_tiles + BATCH,), jnp.int32),
+            jax.ShapeDtypeStruct((1,), jnp.int32),
         ],
         name="list_tiles",
     )(tile_mask)
 
 
-def product_kernel(tiles_ref, count_ref, place_ref, kernel_ref, *rest, which_part, parts):
-    field_refs, (out_ref, fields, sums, slots, slot_sems, field_sems) = rest[:parts], rest[-6:]
+def product_kernel(tiles_ref, count_ref, place_ref, kernel_ref, *rest, parts):
+    field_refs, (out_ref, fields, sums, slots, slot_sems, field_sems) = rest[:-6], rest[-6:]
     _, _, rows, columns = kernel_ref.shape
     _, freqs, depth, lanes = out_ref.shape
     row_tiles, column_tiles = rows // TILE, columns // TILE
@@ -215,17 +218,16 @@
     per_tile = TILE // depth
     tiles_per_part = column_tiles // parts
     half = lanes // 2
-    batches = count_ref[which_part]
-    base = which_part * (lines * column_tiles + BATCH)
+    batches = count_ref[0]
 
     def tile_copy(batch, which):
-        code = tiles_ref[base + batch * BATCH + which]
+        code = tiles_ref[batch * BATCH + which]
         column = lax.rem(code, column_tiles)
         line = jnp.minimum(code // column_tiles, lines - 1)
         freq, row_tile = lax.rem(line, freqs), line // freqs
         slot = lax.rem(batch, SLOTS)
         return pltpu.make_async_copy(
-            kernel_ref.at[:, which_part * freqs + freq, pl.ds(row_tile * TILE, TILE), pl.ds(column * TILE, TILE)],
+            kernel_ref.at[:, freq, pl.ds(row_tile * TILE, TILE), pl.ds(column * TILE, TILE)],
             slots.at[slot, which],
             slot_sems.at[slot, which],
         )
@@ -236,11 +238,14 @@
             for which in range(BATCH):
                 tile_copy(batch, which).start()
 
-    sources = [field_refs[0].at[:, pl.ds(which_part * freqs, freqs)], *field_refs[1:]]
-    copies = [
-        pltpu.make_async_copy(sources[part], fields.at[place_ref[part]], field_sems.at[part])
-        for part in range(parts)
-    ]
+    mine = place_ref[parts]
+    groups = len(field_refs) // parts
+    copies = []
+    for index, field_ref in enumerate(field_refs):
+        part, group = index // groups, index % groups
+        size = field_ref.shape[0]
+        target = fields.at[place_ref[part], pl.ds(group * size, size)]
+        copies.append(pltpu.make_async_copy(field_ref, target, field_sems.at[index]))
     for copy in copies:
         copy.start()
     for batch in range(SLOTS - 1):
@@ -263,10 +268,12 @@
         for which in range(BATCH):
             tile_copy(batch, which).wait()
         for which in range(BATCH):
-            code = tiles_ref[base + batch * BATCH + which]
+            code = tiles_ref[batch * BATCH + which]
             column, line = lax.rem(code, column_tiles), code // column_tiles
             part, first = column // tiles_per_part, lax.rem(column, tiles_per_part) * per_tile
-            field = fields[part, pl.ds(first, per_tile), lax.rem(line, freqs)].reshape(TILE, lanes)
+            freq = lax.rem(line, freqs)
+            field = [fields[part, lax.bitwise_xor(first + k, mine), freq] for k in range(per_tile)]
+            field = jnp.concatenate(field, axis=0)
             swapped = pltpu.roll(field.astype(F32), half, 1)
             swapped = jnp.where(left, -swapped, swapped).astype(BF16)
             both = jnp.concatenate([slots[slot, which, 0], slots[slot, which, 1]], axis=1)
@@ -286,77 +293,97 @@
     lax.fori_loop(0, lines, finish, 0)
 
 
-def product_call(part, tiles, count, places, kernel, fields, out):
-    owners, freqs, depth, lanes = fields[0].shape
-    freqs = freqs // PARTS
+def product_call(tiles, count, places, kernel, fields, parts):
+    owners = sum(field.shape[0] for field in fields) // parts
+    _, freqs, depth, lanes = fields[0].shape
     lines = kernel.shape[2] // TILE * freqs
-    parts = len(fields)
     smem = pl.BlockSpec(memory_space=pltpu.SMEM)
     anywhere = pl.BlockSpec(memory_space=pl.ANY)
-    operands = [tiles, count, places, kernel, *fields]
-    aliases = {}
-    if out is not None:
-        aliases = {len(operands): 0}
-        operands.append(out)
     return pl.pallas_call(
-        functools.partial(product_kernel, which_part=part, parts=parts),
-        grid=(1,),
-        in_specs=[smem, smem, smem] + [anywhere] * (len(operands) - 3),
-        out_specs=pl.BlockSpec((owners, freqs, depth, lanes), lambda g: (0, part, 0, 0)),
-        out_shape=jax.ShapeDtypeStruct(fields[0].shape, BF16),
+        functools.partial(product_kernel, parts=parts),
+        in_specs=[smem, smem, smem, anywhere] + [anywhere] * len(fields),
+        out_specs=pl.BlockSpec(memory_space=pltpu.VMEM),
+        out_shape=jax.ShapeDtypeStruct((owners, freqs, depth, lanes), BF16),
         scratch_shapes=[
             pltpu.VMEM((parts, owners, freqs, depth, lanes), BF16),
             pltpu.VMEM((lines + 1, TILE, lanes), F32),
             pltpu.VMEM((SLOTS, BATCH, 2, TILE, TILE), BF16),
             pltpu.SemaphoreType.DMA((SLOTS, BATCH)),
-            pltpu.SemaphoreType.DMA((parts,)),
+            pltpu.SemaphoreType.DMA((len(fields),)),
         ],
-        input_output_aliases=aliases,
         compiler_params=pltpu.CompilerParams(vmem_limit_bytes=VMEM_LIMIT),
         cost_estimate=pl.CostEstimate(
-            flops=2 * kernel.size * lanes // 8 // PARTS,
-            bytes_accessed=kernel.size // 4 // PARTS,
-            transcendentals=0,
+            flops=2 * kernel.size * lanes // 8, bytes_accessed=kernel.size // 4, transcendentals=0
         ),
-    )(*operands)
+    )(tiles, count, places, kernel, *fields)
+
+
+def collect_kernel(*refs):
+    blocks, (out_ref, sems) = refs[:-2], refs[-2:]
+    copies = [
+        pltpu.make_async_copy(block, out_ref.at[place], sems.at[place]) for place, block in enumerate(blocks)
+    ]
+    for copy in copies:
+        copy.start()
+    for copy in copies:
+        copy.wait()
+
+
+def collect_call(blocks):
+    size = len(blocks) * blocks[0].size
+    return pl.pallas_call(
+        collect_kernel,
+        in_specs=[pl.BlockSpec(memory_space=pl.ANY)] * len(blocks),
+        out_specs=pl.BlockSpec(memory_space=pltpu.VMEM),
+        out_shape=jax.ShapeDtypeStruct((len(blocks),) + blocks[0].shape, BF16),
+        scratch_shapes=[pltpu.SemaphoreType.DMA((len(blocks),))],
+        compiler_params=pltpu.CompilerParams(vmem_limit_bytes=VMEM_LIMIT),
+        cost_estimate=pl.CostEstimate(flops=0, bytes_accessed=4 * size, transcendentals=0),
+    )(*blocks)
 
 
 def local(kernel, tile_mask, direct, onsets, *, owners, halves):
     receivers, focal, _ = direct.shape
     tables = phase_tables()
     onsets = onsets.reshape(receivers // GROUP, GROUP, focal).transpose(0, 2, 1)
-    mine = lax.axis_index("rows")
-    places = jnp.stack([lax.rem(mine - shift + halves, halves) for shift in range(halves)]).astype(jnp.int32)
+    row, mine = lax.axis_index("rows"), lax.axis_index("freq").astype(jnp.int32)
+    places = [lax.rem(row - shift + halves, halves) for shift in range(halves)]
+    places = jnp.stack([*places, mine]).astype(jnp.int32)
+    mine = mine[None]
     tiles, count = list_call(tile_mask)
 
-    def across(rows):
-        return lax.all_to_all(rows, "freq", 0, 0, tiled=True)
-
-    def exchange(fields, part):
-        freqs = fields.shape[1] // PARTS
-        piece = lax.slice_in_dim(fields, part * freqs, (part + 1) * freqs, axis=1)
-        got = [fields]
-        for shift in range(1, halves):
-            ring = [(place, (place + shift) % halves) for place in range(halves)]
-            got.append(lax.ppermute(piece, "rows", ring))
-        return got
-
     def time_at(kind, chunk, *operands):
-        return time_call(kind, chunk, owners, direct, tables, *operands)
-
-    rows = [time_at("first", chunk) for chunk in range(CHUNKS)]
+        return time_call(kind, chunk, owners, mine, direct, tables, *operands)
+
+    def spread(blocks):
+        got = list(blocks)
+        for shift in range(1, owners):
+            pairs = [(place, place ^ shift) for place in range(owners)]
+            got[shift] = lax.ppermute(blocks[shift], "freq", pairs)
+        size = owners // REACHES
+        fields = [[] for _ in range(halves)]
+        for reach in range(REACHES):
+            mine = collect_call(got[reach * size : (reach + 1) * size])
+            fields[0].append(mine)
+            for shift in range(1, halves):
+                ring = [(place, (place + shift) % halves) for place in range(halves)]
+                fields[shift].append(lax.ppermute(mine, "rows", ring))
+        return [field for of_shift in fields for field in of_shift]
+
+    def gather(bands):
+        return lax.all_to_all(bands, "freq", 0, 0, tiled=True)
+
+    blocks = [time_at("first", chunk) for chunk in range(CHUNKS)]
     out = None
     for turn in range(ITERS):
         bands = [None] * CHUNKS
         for chunk in range(CHUNKS):
-            fields = across(rows[chunk])
-            for part in range(PARTS):
-                both = exchange(fields, part)
-                bands[chunk] = product_call(part, tiles, count, places, kernel, both, bands[chunk])
-        bands = [across(bands[chunk]) for chunk in range(CHUNKS)]
+            fields = spread(blocks[chunk])
+            bands[chunk] = product_call(tiles, count, places, kernel, fields, halves)
+        bands = [gather(bands[chunk]) for chunk in range(CHUNKS)]
         for chunk in range(CHUNKS):
             if turn + 1 < ITERS:
-                rows[chunk] = time_at("middle", chunk, onsets, bands[chunk])
+                blocks[chunk] = time_at("middle", chunk, onsets, bands[chunk])
             else:
                 out = time_at("last", chunk, onsets, bands[chunk], out)
     return out

time: 496 us -> 690 us (1.39)
  waiting for transfers between devices: 257 us -> 355 us
  starting transfers between devices: 76.4 us -> 167 us
  Pallas kernels: 135 us -> 150 us
  local copies, waits for them, and re-layouts: 18.5 us -> 7.96 us
    ppermute x8 -> x68, waiting for transfers between devices: 139 us -> 324 us  [the longest x60 163 us: spread(): got[shift] = lax.ppermute(blocks[shift], 'freq', pairs)]
    ppermute x8 -> x68, starting transfers between devices: 5.99 us -> 144 us  [the longest x60 134 us: spread(): got[shift] = lax.ppermute(blocks[shift], 'freq', pairs)]
    all_to_all x8 -> x4, waiting for transfers between devices: 117 us -> 31.5 us  [gather(): return lax.all_to_all(bands, 'freq', 0, 0, tiled=True)]
    all_to_all x8 -> x4, starting transfers between devices: 70.4 us -> 23.7 us  [gather(): return lax.all_to_all(bands, 'freq', 0, 0, tiled=True)]
    pallas_call x8 -> x12, Pallas kernels: 63.5 us -> 77.4 us  [the longest x4 58.7 us: product_call(): pl.pallas_call(functools.partial(product_kernel, parts=parts), in_specs=[...]
  transfers between devices with their start and end apart: 16 -> 72, of which waited for: 12 -> 29; matrix products, arithmetic and copies ran while one was open for 2% -> 0% of each run, Pallas kernels for 24% -> 17%
where the time goes in v2:
time: 690 us; the launch traced here: 684 us
  waiting for transfers between devices  355 us (51%)
  starting transfers between devices  167 us (24%)
  Pallas kernels  150 us (22%)
  local copies, waits for them, and re-layouts  7.96 us (1%)
    ppermute x60, waiting for transfers between devices, spread(): got[shift] = lax.ppermute(blocks[shift], 'freq', pairs)  163 us
    ppermute x8, waiting for transfers between devices, spread(): fields[shift].append(lax.ppermute(mine, 'rows', ring))  161 us
    ppermute x60, starting transfers between devices, spread(): got[shift] = lax.ppermute(blocks[shift], 'freq', pairs)  134 us
    pallas_call x6, Pallas kernels, time_call(): pl.pallas_call(functools.partial(body, half=half), grid=(receivers // GRO...  68.1 us
    pallas_call x4, Pallas kernels, product_call(): pl.pallas_call(functools.partial(product_kernel, parts=parts), in_specs=[...  58.7 us
    all_to_all x4, waiting for transfers between devices, gather(): return lax.all_to_all(bands, 'freq', 0, 0, tiled=True)  31.5 us
    all_to_all x4, starting transfers between devices, gather(): return lax.all_to_all(bands, 'freq', 0, 0, tiled=True)  23.7 us
    pallas_call x8, Pallas kernels, collect_call(): pl.pallas_call(collect_kernel, in_specs=[pl.BlockSpec(memory_space=pl.ANY...  18.7 us
  transfers between devices with their start and end apart: 72, of which 29 were waited for; matrix products, arithmetic and copies ran while one was open for 0% of the time, Pallas kernels for 17%

profile of v2, /device:TPU:1, one launch (start us, length us, event | category | flops | bytes accessed | tf_op | source)
XLA Modules:
  0.0 683.7 jit_solution(14203562880959628512)
XLA Ops:
  1.4 9.0 %shard_map.54 = (bf16[8,64,128]{2,1,0:T(8,128)(2,1)}, bf16[8,64,128]{2,1,0:T(8,128)(2,1)}, bf16[8,64,128]{2,1,0:T(8,128)(2,1)}, bf16[8,64,128]{2,1,0:T(8,128)(2,...) custom-call(s32[1]{0:T(128)} %bitcast.mine_ref, ...), custom_call_target="tpu_custom_call" | custom-call | flops 3221225472 | bytes 16777216 | tf_op jit(solution)/shard_map/pallas_call | solution.py:165
  10.5 2.7 collective-permute-start.35
  19.6 3.1 collective-permute-start.45
  22.7 10.3 %collective-permute-done.41.refs_0_ = bf16[8,64,128]{2,1,0:T(8,128)(2,1)S(1)} collective-permute-done((bf16[8,64,128]{2,1,0:T(8,128)(2,1)}, bf16[8,64,128]{2,1,0:T(8,128)(2,1)S(1)}, u32[]{:S(2)}, u32[]{:S(2)}) %collective-permute-start.41) | collective-permute-done | bytes 131104 | tf_op jit(solution)/shard_map/ppermute | solution.py:362
  33.0 4.4 collective-permute-start.46
  39.7 9.8 %collective-permute-start.48 = (bf16[8,64,128]{2,1,0:T(8,128)(2,1)}, bf16[8,64,128]{2,1,0:T(8,128)(2,1)S(1)}, u32[]{:S(2)}, u32[]{:S(2)}) collective-permute-start(bf16[8,64,128]{2,1,0:T(8,128)(2,1)} %get-tuple-element.120), channel_id=1, source_target_pairs={{0,30},{2,28},{4,26},{6,24},{8,22},{10,20},{12,18},{14,16},{16,14}... | collective-permute-start | bytes 393224 | tf_op jit(solution)/shard_map/ppermute | solution.py:362
  51.6 5.6 collective-permute-start.38
  59.5 3.2 collective-permute-start.40
  62.7 2.3 shard_map.56.rest_1_
  67.2 2.3 shard_map.55.rest_0_
  70.7 4.9 list_tiles.1
  76.1 13.4 %collective-permute-done.50.rest_3_ = bf16[8,8,64,128]{3,2,1,0:T(8,128)(2,1)S(1)} collective-permute-done((bf16[8,8,64,128]{3,2,1,0:T(8,128)(2,1)}, bf16[8,8,64,128]{3,2,1,0:T(8,128)(2,1)S(1)}, u32[]{:S(2)}, u32[]{:S(2)}) %collective-permute-start.50) | collective-permute-done | bytes 1048608 | tf_op jit(solution)/shard_map/ppermute | solution.py:370
  89.5 22.5 %collective-permute-done.49.rest_2_ = bf16[8,8,64,128]{3,2,1,0:T(8,128)(2,1)S(1)} collective-permute-done((bf16[8,8,64,128]{3,2,1,0:T(8,128)(2,1)}, bf16[8,8,64,128]{3,2,1,0:T(8,128)(2,1)S(1)}, u32[]{:S(2)}, u32[]{:S(2)}) %collective-permute-start.49) | collective-permute-done | bytes 1048608 | tf_op jit(solution)/shard_map/ppermute | solution.py:370
  113.0 14.7 %shard_map.57 = bf16[16,8,64,128]{3,2,1,0:T(8,128)(2,1)} custom-call(s32[1032]{0:T(1024)} %get-tuple-element.71.tiles_ref, s32[1]{0:T(128)} %get-tuple-element.72.count_ref, s32[3]{0:T(128)} %pad_add_fusion.place_ref, bf16[2,8,1024,2048]{3,2,1,0:T(8,128)(2,1)} %kernel_ref.7, bf16[8,8,64,128]{3,2,1,0:T(8,128)(2,1)} %shard_map.55.rest_0_, ...), custom_call_target="tpu_custom_call" | custom-call | flops 1073741824 | bytes 8388608 | tf_op jit(solution)/shard_map/pallas_call | solution.py:302
  127.6 7.4 %all-to-all-start.2 = ((bf16[16,8,64,128]{3,2,1,0:T(8,128)(2,1)}), bf16[16,8,64,128]{3,2,1,0:T(8,128)(2,1)S(1)}, u32[]{:S(2)}, u32[]{:S(2)}) async-start(bf16[16,8,64,128]{3,2,1,0:T(8,128)(2,1)} %shard_map.57), calls=%async_computation.2 | async-start | bytes 4194304 | tf_op jit(solution)/shard_map/all_to_all | solution.py:374
  135.1 9.0 %shard_map.46 = (bf16[8,64,128]{2,1,0:T(8,128)(2,1)}, bf16[8,64,128]{2,1,0:T(8,128)(2,1)}, bf16[8,64,128]{2,1,0:T(8,128)(2,1)}, bf16[8,64,128]{2,1,0:T(8,128)(2,...) custom-call(s32[1]{0:T(128)} %bitcast.mine_ref, ...), custom_call_target="tpu_custom_call" | custom-call | flops 3221225472 | bytes 16777216 | tf_op jit(solution)/shard_map/pallas_call | solution.py:165
  152.4 2.9 collective-permute-start.11
  155.4 44.7 %collective-permute-done.7.refs_0_ = bf16[8,64,128]{2,1,0:T(8,128)(2,1)S(1)} collective-permute-done((bf16[8,64,128]{2,1,0:T(8,128)(2,1)}, bf16[8,64,128]{2,1,0:T(8,128)(2,1)S(1)}, u32[]{:S(2)}, u32[]{:S(2)}) %collective-permute-start.7) | collective-permute-done | bytes 131104 | tf_op jit(solution)/shard_map/ppermute | solution.py:362
  200.1 2.6 collective-permute-start.12
  205.8 6.5 collective-permute-done.9.refs_2_
  212.2 2.6 collective-permute-start.14
  215.9 2.7 collective-permute-start.3
  218.6 4.5 collective-permute-start.4
  223.1 3.4 collective-permute-start.5
  226.5 3.1 collective-permute-start.6
  229.7 2.3 shard_map.48.rest_1_
  234.1 2.4 shard_map.47.rest_0_
  237.4 19.2 %collective-permute-done.16.rest_3_ = bf16[8,8,64,128]{3,2,1,0:T(8,128)(2,1)S(1)} collective-permute-done((bf16[8,8,64,128]{3,2,1,0:T(8,128)(2,1)}, bf16[8,8,64,128]{3,2,1,0:T(8,128)(2,1)S(1)}, u32[]{:S(2)}, u32[]{:S(2)}) %collective-permute-start.16) | collective-permute-done | bytes 1048608 | tf_op jit(solution)/shard_map/ppermute | solution.py:370
  256.6 22.6 %collective-permute-done.15.rest_2_ = bf16[8,8,64,128]{3,2,1,0:T(8,128)(2,1)} collective-permute-done((bf16[8,8,64,128]{3,2,1,0:T(8,128)(2,1)}, bf16[8,8,64,128]{3,2,1,0:T(8,128)(2,1)}, u32[]{:S(2)}, u32[]{:S(2)}) %collective-permute-start.15) | collective-permute-done | bytes 1048608 | tf_op jit(solution)/shard_map/ppermute | solution.py:370
  279.2 14.7 %shard_map.49 = bf16[16,8,64,128]{3,2,1,0:T(8,128)(2,1)} custom-call(s32[1032]{0:T(1024)} %get-tuple-element.71.tiles_ref, s32[1]{0:T(128)} %get-tuple-element.72.count_ref, s32[3]{0:T(128)} %pad_add_fusion.place_ref, bf16[2,8,1024,2048]{3,2,1,0:T(8,128)(2,1)} %kernel_ref.7, bf16[8,8,64,128]{3,2,1,0:T(8,128)(2,1)} %shard_map.47.rest_0_, ...), custom_call_target="tpu_custom_call" | custom-call | flops 1073741824 | bytes 8388608 | tf_op jit(solution)/shard_map/pallas_call | solution.py:302
  295.2 5.4 all-to-all-start
  301.5 14.9 %shard_map.58 = (bf16[8,64,128]{2,1,0:T(8,128)(2,1)}, bf16[8,64,128]{2,1,0:T(8,128)(2,1)}, bf16[8,64,128]{2,1,0:T(8,128)(2,1)}, bf16[8,64,128]{2,1,0:T(8,128)(2,...) custom-call(s32[1]{0:T(128)} %bitcast.mine_ref, ...), custom_call_target="tpu_custom_call" | custom-call | flops 5368709120 | bytes 16777216 | tf_op jit(solution)/shard_map/pallas_call | solution.py:165
  327.4 38.2 %collective-permute-done.58.refs_0_ = bf16[8,64,128]{2,1,0:T(8,128)(2,1)S(1)} collective-permute-done((bf16[8,64,128]{2,1,0:T(8,128)(2,1)}, bf16[8,64,128]{2,1,0:T(8,128)(2,1)S(1)}, u32[]{:S(2)}, u32[]{:S(2)}) %collective-permute-start.58) | collective-permute-done | bytes 131104 | tf_op jit(solution)/shard_map/ppermute | solution.py:362
  365.7 2.6 collective-permute-start.63
  371.4 6.5 collective-permute-done.60.refs_2_
  377.9 2.6 collective-permute-start.65
  381.5 2.7 collective-permute-start.54
  384.2 4.5 collective-permute-start.55
  388.7 3.4 collective-permute-start.56
  392.1 3.1 collective-permute-start.57
  395.3 2.3 shard_map.60.rest_1_
  399.7 2.4 shard_map.59.rest_0_
  403.0 19.2 %collective-permute-done.67.rest_3_ = bf16[8,8,64,128]{3,2,1,0:T(8,128)(2,1)S(1)} collective-permute-done((bf16[8,8,64,128]{3,2,1,0:T(8,128)(2,1)}, bf16[8,8,64,128]{3,2,1,0:T(8,128)(2,1)S(1)}, u32[]{:S(2)}, u32[]{:S(2)}) %collective-permute-start.67) | collective-permute-done | bytes 1048608 | tf_op jit(solution)/shard_map/ppermute | solution.py:370
  422.2 22.6 %collective-permute-done.66.rest_2_ = bf16[8,8,64,128]{3,2,1,0:T(8,128)(2,1)} collective-permute-done((bf16[8,8,64,128]{3,2,1,0:T(8,128)(2,1)}, bf16[8,8,64,128]{3,2,1,0:T(8,128)(2,1)}, u32[]{:S(2)}, u32[]{:S(2)}) %collective-permute-start.66) | collective-permute-done | bytes 1048608 | tf_op jit(solution)/shard_map/ppermute | solution.py:370
  444.8 14.7 %shard_map.61 = bf16[16,8,64,128]{3,2,1,0:T(8,128)(2,1)} custom-call(s32[1032]{0:T(1024)} %get-tuple-element.71.tiles_ref, s32[1]{0:T(128)} %get-tuple-element.72.count_ref, s32[3]{0:T(128)} %pad_add_fusion.place_ref, bf16[2,8,1024,2048]{3,2,1,0:T(8,128)(2,1)} %kernel_ref.7, bf16[8,8,64,128]{3,2,1,0:T(8,128)(2,1)} %shard_map.59.rest_0_, ...), custom_call_target="tpu_custom_call" | custom-call | flops 1073741824 | bytes 8388608 | tf_op jit(solution)/shard_map/pallas_call | solution.py:302
  460.8 5.4 all-to-all-start.3
  466.3 14.9 %shard_map.50 = (bf16[8,64,128]{2,1,0:T(8,128)(2,1)}, bf16[8,64,128]{2,1,0:T(8,128)(2,1)}, bf16[8,64,128]{2,1,0:T(8,128)(2,1)}, bf16[8,64,128]{2,1,0:T(8,128)(2,...) custom-call(s32[1]{0:T(128)} %bitcast.mine_ref, ...), custom_call_target="tpu_custom_call" | custom-call | flops 5368709120 | bytes 16777216 | tf_op jit(solution)/shard_map/pallas_call | solution.py:165
  492.2 39.1 %collective-permute-done.24.refs_0_ = bf16[8,64,128]{2,1,0:T(8,128)(2,1)S(1)} collective-permute-done((bf16[8,64,128]{2,1,0:T(8,128)(2,1)}, bf16[8,64,128]{2,1,0:T(8,128)(2,1)S(1)}, u32[]{:S(2)}, u32[]{:S(2)}) %collective-permute-start.24) | collective-permute-done | bytes 131104 | tf_op jit(solution)/shard_map/ppermute | solution.py:362
  531.3 2.6 collective-permute-start.29
  537.0 6.5 collective-permute-done.26.refs_2_
  543.5 2.6 collective-permute-start.31
  547.1 2.7 collective-permute-start.20
  549.8 4.5 collective-permute-start.21
  554.3 3.4 collective-permute-start.22
  557.7 3.1 collective-permute-start.23
  560.9 2.3 shard_map.52.rest_1_
  565.3 2.3 shard_map.51.rest_0_
  568.6 19.3 %collective-permute-done.33.rest_3_ = bf16[8,8,64,128]{3,2,1,0:T(8,128)(2,1)S(1)} collective-permute-done((bf16[8,8,64,128]{3,2,1,0:T(8,128)(2,1)}, bf16[8,8,64,128]{3,2,1,0:T(8,128)(2,1)S(1)}, u32[]{:S(2)}, u32[]{:S(2)}) %collective-permute-start.33) | collective-permute-done | bytes 1048608 | tf_op jit(solution)/shard_map/ppermute | solution.py:370
  587.9 22.6 %collective-permute-done.32.rest_2_ = bf16[8,8,64,128]{3,2,1,0:T(8,128)(2,1)} collective-permute-done((bf16[8,8,64,128]{3,2,1,0:T(8,128)(2,1)}, bf16[8,8,64,128]{3,2,1,0:T(8,128)(2,1)}, u32[]{:S(2)}, u32[]{:S(2)}) %collective-permute-start.32) | collective-permute-done | bytes 1048608 | tf_op jit(solution)/shard_map/ppermute | solution.py:370
  610.4 14.7 %shard_map.53 = bf16[16,8,64,128]{3,2,1,0:T(8,128)(2,1)} custom-call(s32[1032]{0:T(1024)} %get-tuple-element.71.tiles_ref, s32[1]{0:T(128)} %get-tuple-element.72.count_ref, s32[3]{0:T(128)} %pad_add_fusion.place_ref, bf16[2,8,1024,2048]{3,2,1,0:T(8,128)(2,1)} %kernel_ref.7, bf16[8,8,64,128]{3,2,1,0:T(8,128)(2,1)} %shard_map.51.rest_0_, ...), custom_call_target="tpu_custom_call" | custom-call | flops 1073741824 | bytes 8388608 | tf_op jit(solution)/shard_map/pallas_call | solution.py:302
  626.5 5.4 all-to-all-start.1
  631.9 10.2 %shard_map.62.rest_0_ = f32[64,128,512]{2,1,0:T(8,128)} custom-call(s32[1]{0:T(128)} %bitcast.mine_ref, f32[64,128,512]{2,1,0:T(8,128)} %direct_ref.11, bf16[2,256,256]{2,1,0:T(8,128)(2,1)} %pad_maximum_fusion.tables_ref, s32[4,128,16]{2,1,0:T(8,128)} %bitcast.12, bf16[16,8,64,128]{3,2,1,0:T(8,128)(2,1)} %copy-done), custom_call_target="tpu_custom_call" | custom-call | flops 2147483648 | bytes 16777216 | tf_op jit(solution)/shard_map/pallas_call | solution.py:165
  642.1 31.5 %all-to-all-done.1.bands_ref = bf16[16,8,64,128]{3,2,1,0:T(8,128)(2,1)} async-done(((bf16[16,8,64,128]{3,2,1,0:T(8,128)(2,1)}), bf16[16,8,64,128]{3,2,1,0:T(8,128)(2,1)}, u32[]{:S(2)}, u32[]{:S(2)}) %all-to-all-start.1) | async-done | bytes 2097184 | tf_op jit(solution)/shard_map/all_to_all | solution.py:374
  673.6 10.1 %shard_map.63 = f32[64,128,512]{2,1,0:T(8,128)} custom-call(s32[1]{0:T(128)} %bitcast.mine_ref, f32[64,128,512]{2,1,0:T(8,128)} %direct_ref.11, bf16[2,256,256]{2,1,0:T(8,128)(2,1)} %pad_maximum_fusion.tables_ref, s32[4,128,16]{2,1,0:T(8,128)} %bitcast.13, bf16[16,8,64,128]{3,2,1,0:T(8,128)(2,1)} %all-to-all-done.1.bands_ref, ...), custom_call_target="tpu_custom_call", output_to_operand_aliasing={{}: (5, {})} | custom-call | flops 2147483648 | bytes 16777216 | tf_op jit(solution)/shard_map/pallas_call | solution.py:165
  (232 shorter events, 76.3 us)
Async XLA Ops:
  10.5 9.1 %collective-permute-start.35 = (bf16[8,64,128]{2,1,0:T(8,128)(2,1)}, bf16[8,64,128]{2,1,0:T(8,128)(2,1)S(1)}, u32[]{:S(2)}, u32[]{:S(2)}) collective-permute-start(bf16[8,64,128]{2,1,0:T(8,128)(2,1)} %get-tuple-element.107), channel_id=1, source_target_pairs={{0,4},{2,6},{4,0},{6,2},{8,12},{10,14},{12,8},{14,10},{16,20},{18,... | collective-permute-start | bytes 393224 | tf_op jit(solution)/shard_map/ppermute | solution.py:362
  13.2 19.8 %collective-permute-start.41 = (bf16[8,64,128]{2,1,0:T(8,128)(2,1)}, bf16[8,64,128]{2,1,0:T(8,128)(2,1)S(1)}, u32[]{:S(2)}, u32[]{:S(2)}) collective-permute-start(bf16[8,64,128]{2,1,0:T(8,128)(2,1)} %get-tuple-element.113), channel_id=1, source_target_pairs={{0,16},{2,18},{4,20},{6,22},{8,24},{10,26},{12,28},{14,30},{16,0},... | collective-permute-start | bytes 393224 | tf_op jit(solution)/shard_map/ppermute | solution.py:362
  15.5 22.0 %collective-permute-start.42 = (bf16[8,64,128]{2,1,0:T(8,128)(2,1)}, bf16[8,64,128]{2,1,0:T(8,128)(2,1)S(1)}, u32[]{:S(2)}, u32[]{:S(2)}) collective-permute-start(bf16[8,64,128]{2,1,0:T(8,128)(2,1)} %get-tuple-element.114), channel_id=1, source_target_pairs={{0,18},{2,16},{4,22},{6,20},{8,26},{10,24},{12,30},{14,28},{16,2},... | collective-permute-start | bytes 393224 | tf_op jit(solution)/shard_map/ppermute | solution.py:362
  16.1 23.7 %collective-permute-start.43 = (bf16[8,64,128]{2,1,0:T(8,128)(2,1)}, bf16[8,64,128]{2,1,0:T(8,128)(2,1)S(1)}, u32[]{:S(2)}, u32[]{:S(2)}) collective-permute-start(bf16[8,64,128]{2,1,0:T(8,128)(2,1)} %get-tuple-element.115), channel_id=1, source_target_pairs={{0,20},{2,22},{4,16},{6,18},{8,28},{10,30},{12,24},{14,26},{16,4},... | collective-permute-start | bytes 393224 | tf_op jit(solution)/shard_map/ppermute | solution.py:362
  18.3 31.2 %collective-permute-start.44 = (bf16[8,64,128]{2,1,0:T(8,128)(2,1)}, bf16[8,64,128]{2,1,0:T(8,128)(2,1)S(1)}, u32[]{:S(2)}, u32[]{:S(2)}) collective-permute-start(bf16[8,64,128]{2,1,0:T(8,128)(2,1)} %get-tuple-element.116), channel_id=1, source_target_pairs={{0,22},{2,20},{4,18},{6,16},{8,30},{10,28},{12,26},{14,24},{16,6},... | collective-permute-start | bytes 393224 | tf_op jit(solution)/shard_map/ppermute | solution.py:362
  19.6 30.0 %collective-permute-start.45 = (bf16[8,64,128]{2,1,0:T(8,128)(2,1)}, bf16[8,64,128]{2,1,0:T(8,128)(2,1)S(1)}, u32[]{:S(2)}, u32[]{:S(2)}) collective-permute-start(bf16[8,64,128]{2,1,0:T(8,128)(2,1)} %get-tuple-element.117), channel_id=1, source_target_pairs={{0,24},{2,26},{4,28},{6,30},{8,16},{10,18},{12,20},{14,22},{16,8},... | collective-permute-start | bytes 393224 | tf_op jit(solution)/shard_map/ppermute | solution.py:362
  33.0 18.5 %collective-permute-start.46 = (bf16[8,64,128]{2,1,0:T(8,128)(2,1)}, bf16[8,64,128]{2,1,0:T(8,128)(2,1)S(1)}, u32[]{:S(2)}, u32[]{:S(2)}) collective-permute-start(bf16[8,64,128]{2,1,0:T(8,128)(2,1)} %get-tuple-element.118), channel_id=1, source_target_pairs={{0,26},{2,24},{4,30},{6,28},{8,18},{10,16},{12,22},{14,20},{16,10}... | collective-permute-start | bytes 393224 | tf_op jit(solution)/shard_map/ppermute | solution.py:362
  37.5 19.7 %collective-permute-start.47 = (bf16[8,64,128]{2,1,0:T(8,128)(2,1)}, bf16[8,64,128]{2,1,0:T(8,128)(2,1)S(1)}, u32[]{:S(2)}, u32[]{:S(2)}) collective-permute-start(bf16[8,64,128]{2,1,0:T(8,128)(2,1)} %get-tuple-element.119), channel_id=1, source_target_pairs={{0,28},{2,30},{4,24},{6,26},{8,20},{10,22},{12,16},{14,18},{16,12}... | collective-permute-start | bytes 393224 | tf_op jit(solution)/shard_map/ppermute | solution.py:362
  39.7 19.8 %collective-permute-start.48 = (bf16[8,64,128]{2,1,0:T(8,128)(2,1)}, bf16[8,64,128]{2,1,0:T(8,128)(2,1)S(1)}, u32[]{:S(2)}, u32[]{:S(2)}) collective-permute-start(bf16[8,64,128]{2,1,0:T(8,128)(2,1)} %get-tuple-element.120), channel_id=1, source_target_pairs={{0,30},{2,28},{4,26},{6,24},{8,22},{10,20},{12,18},{14,16},{16,14}... | collective-permute-start | bytes 393224 | tf_op jit(solution)/shard_map/ppermute | solution.py:362
  49.5 15.5 %collective-permute-start.36 = (bf16[8,64,128]{2,1,0:T(8,128)(2,1)}, bf16[8,64,128]{2,1,0:T(8,128)(2,1)S(1)}, u32[]{:S(2)}, u32[]{:S(2)}) collective-permute-start(bf16[8,64,128]{2,1,0:T(8,128)(2,1)} %get-tuple-element.108), channel_id=1, source_target_pairs={{0,6},{2,4},{4,2},{6,0},{8,14},{10,12},{12,10},{14,8},{16,22},{18,... | collective-permute-start | bytes 393224 | tf_op jit(solution)/shard_map/ppermute | solution.py:362
  49.6 16.8 %collective-permute-start.37 = (bf16[8,64,128]{2,1,0:T(8,128)(2,1)}, bf16[8,64,128]{2,1,0:T(8,128)(2,1)S(1)}, u32[]{:S(2)}, u32[]{:S(2)}) collective-permute-start(bf16[8,64,128]{2,1,0:T(8,128)(2,1)} %get-tuple-element.109), channel_id=1, source_target_pairs={{0,8},{2,10},{4,12},{6,14},{8,0},{10,2},{12,4},{14,6},{16,24},{18,... | collective-permute-start | bytes 393224 | tf_op jit(solution)/shard_map/ppermute | solution.py:362
  51.6 14.8 %collective-permute-start.38 = (bf16[8,64,128]{2,1,0:T(8,128)(2,1)}, bf16[8,64,128]{2,1,0:T(8,128)(2,1)S(1)}, u32[]{:S(2)}, u32[]{:S(2)}) collective-permute-start(bf16[8,64,128]{2,1,0:T(8,128)(2,1)} %get-tuple-element.110), channel_id=1, source_target_pairs={{0,10},{2,8},{4,14},{6,12},{8,2},{10,0},{12,6},{14,4},{16,26},{18,... | collective-permute-start | bytes 393224 | tf_op jit(solution)/shard_map/ppermute | solution.py:362
  57.2 9.2 %collective-permute-start.39 = (bf16[8,64,128]{2,1,0:T(8,128)(2,1)}, bf16[8,64,128]{2,1,0:T(8,128)(2,1)S(1)}, u32[]{:S(2)}, u32[]{:S(2)}) collective-permute-start(bf16[8,64,128]{2,1,0:T(8,128)(2,1)} %get-tuple-element.111), channel_id=1, source_target_pairs={{0,12},{2,14},{4,8},{6,10},{8,4},{10,6},{12,0},{14,2},{16,28},{18,... | collective-permute-start | bytes 393224 | tf_op jit(solution)/shard_map/ppermute | solution.py:362
  65.1 24.4 %collective-permute-start.50 = (bf16[8,8,64,128]{3,2,1,0:T(8,128)(2,1)}, bf16[8,8,64,128]{3,2,1,0:T(8,128)(2,1)S(1)}, u32[]{:S(2)}, u32[]{:S(2)}) collective-permute-start(bf16[8,8,64,128]{3,2,1,0:T(8,128)(2,1)} %shard_map.56.rest_1_), channel_id=1, source_target_pairs={{0,1},{1,0},{2,3},{3,2},{4,5},{5,4},{6,7},{7,6},{8,9},{9,8},{10,11... | collective-permute-start | bytes 3145736 | tf_op jit(solution)/shard_map/ppermute | solution.py:370
  69.5 42.5 %collective-permute-start.49 = (bf16[8,8,64,128]{3,2,1,0:T(8,128)(2,1)}, bf16[8,8,64,128]{3,2,1,0:T(8,128)(2,1)S(1)}, u32[]{:S(2)}, u32[]{:S(2)}) collective-permute-start(bf16[8,8,64,128]{3,2,1,0:T(8,128)(2,1)} %shard_map.55.rest_0_), channel_id=1, source_target_pairs={{0,1},{1,0},{2,3},{3,2},{4,5},{5,4},{6,7},{7,6},{8,9},{9,8},{10,11... | collective-permute-start | bytes 3145736 | tf_op jit(solution)/shard_map/ppermute | solution.py:370
  127.6 166.2 %all-to-all-start.2 = ((bf16[16,8,64,128]{3,2,1,0:T(8,128)(2,1)}), bf16[16,8,64,128]{3,2,1,0:T(8,128)(2,1)S(1)}, u32[]{:S(2)}, u32[]{:S(2)}) async-start(bf16[16,8,64,128]{3,2,1,0:T(8,128)(2,1)} %shard_map.57), calls=%async_computation.2 | async-start | bytes 4194304 | tf_op jit(solution)/shard_map/all_to_all | solution.py:374
  144.2 8.2 %collective-permute-start.1 = (bf16[8,64,128]{2,1,0:T(8,128)(2,1)}, bf16[8,64,128]{2,1,0:T(8,128)(2,1)S(1)}, u32[]{:S(2)}, u32[]{:S(2)}) collective-permute-start(bf16[8,64,128]{2,1,0:T(8,128)(2,1)} %get-tuple-element.75), channel_id=1, source_target_pairs={{0,4},{2,6},{4,0},{6,2},{8,12},{10,14},{12,8},{14,10},{16,20},{18,... | collective-permute-start | bytes 393224 | tf_op jit(solution)/shard_map/ppermute | solution.py:362
  145.8 54.2 %collective-permute-start.7 = (bf16[8,64,128]{2,1,0:T(8,128)(2,1)}, bf16[8,64,128]{2,1,0:T(8,128)(2,1)S(1)}, u32[]{:S(2)}, u32[]{:S(2)}) collective-permute-start(bf16[8,64,128]{2,1,0:T(8,128)(2,1)} %get-tuple-element.81), channel_id=1, source_target_pairs={{0,16},{2,18},{4,20},{6,22},{8,24},{10,26},{12,28},{14,30},{16,0},... | collective-permute-start | bytes 393224 | tf_op jit(solution)/shard_map/ppermute | solution.py:362
  147.9 55.8 %collective-permute-start.8 = (bf16[8,64,128]{2,1,0:T(8,128)(2,1)}, bf16[8,64,128]{2,1,0:T(8,128)(2,1)S(1)}, u32[]{:S(2)}, u32[]{:S(2)}) collective-permute-start(bf16[8,64,128]{2,1,0:T(8,128)(2,1)} %get-tuple-element.82), channel_id=1, source_target_pairs={{0,18},{2,16},{4,22},{6,20},{8,26},{10,24},{12,30},{14,28},{16,2},... | collective-permute-start | bytes 393224 | tf_op jit(solution)/shard_map/ppermute | solution.py:362
  148.8 63.5 %collective-permute-start.9 = (bf16[8,64,128]{2,1,0:T(8,128)(2,1)}, bf16[8,64,128]{2,1,0:T(8,128)(2,1)S(1)}, u32[]{:S(2)}, u32[]{:S(2)}) collective-permute-start(bf16[8,64,128]{2,1,0:T(8,128)(2,1)} %get-tuple-element.83), channel_id=1, source_target_pairs={{0,20},{2,22},{4,16},{6,18},{8,28},{10,30},{12,24},{14,26},{16,4},... | collective-permute-start | bytes 393224 | tf_op jit(solution)/shard_map/ppermute | solution.py:362
  150.9 65.0 %collective-permute-start.10 = (bf16[8,64,128]{2,1,0:T(8,128)(2,1)}, bf16[8,64,128]{2,1,0:T(8,128)(2,1)S(1)}, u32[]{:S(2)}, u32[]{:S(2)}) collective-permute-start(bf16[8,64,128]{2,1,0:T(8,128)(2,1)} %get-tuple-element.84), channel_id=1, source_target_pairs={{0,22},{2,20},{4,18},{6,16},{8,30},{10,28},{12,26},{14,24},{16,6},... | collective-permute-start | bytes 393224 | tf_op jit(solution)/shard_map/ppermute | solution.py:362
  152.4 63.5 %collective-permute-start.11 = (bf16[8,64,128]{2,1,0:T(8,128)(2,1)}, bf16[8,64,128]{2,1,0:T(8,128)(2,1)S(1)}, u32[]{:S(2)}, u32[]{:S(2)}) collective-permute-start(bf16[8,64,128]{2,1,0:T(8,128)(2,1)} %get-tuple-element.85), channel_id=1, source_target_pairs={{0,24},{2,26},{4,28},{6,30},{8,16},{10,18},{12,20},{14,22},{16,8},... | collective-permute-start | bytes 393224 | tf_op jit(solution)/shard_map/ppermute | solution.py:362
  200.1 18.5 %collective-permute-start.12 = (bf16[8,64,128]{2,1,0:T(8,128)(2,1)}, bf16[8,64,128]{2,1,0:T(8,128)(2,1)S(1)}, u32[]{:S(2)}, u32[]{:S(2)}) collective-permute-start(bf16[8,64,128]{2,1,0:T(8,128)(2,1)} %get-tuple-element.86), channel_id=1, source_target_pairs={{0,26},{2,24},{4,30},{6,28},{8,18},{10,16},{12,22},{14,20},{16,10}... | collective-permute-start | bytes 393224 | tf_op jit(solution)/shard_map/ppermute | solution.py:362
  203.7 19.4 %collective-permute-start.13 = (bf16[8,64,128]{2,1,0:T(8,128)(2,1)}, bf16[8,64,128]{2,1,0:T(8,128)(2,1)S(1)}, u32[]{:S(2)}, u32[]{:S(2)}) collective-permute-start(bf16[8,64,128]{2,1,0:T(8,128)(2,1)} %get-tuple-element.87), channel_id=1, source_target_pairs={{0,28},{2,30},{4,24},{6,26},{8,20},{10,22},{12,16},{14,18},{16,12}... | collective-permute-start | bytes 393224 | tf_op jit(solution)/shard_map/ppermute | solution.py:362
  212.2 14.3 %collective-permute-start.14 = (bf16[8,64,128]{2,1,0:T(8,128)(2,1)}, bf16[8,64,128]{2,1,0:T(8,128)(2,1)S(1)}, u32[]{:S(2)}, u32[]{:S(2)}) collective-permute-start(bf16[8,64,128]{2,1,0:T(8,128)(2,1)} %get-tuple-element.88), channel_id=1, source_target_pairs={{0,30},{2,28},{4,26},{6,24},{8,22},{10,20},{12,18},{14,16},{16,14}... | collective-permute-start | bytes 393224 | tf_op jit(solution)/shard_map/ppermute | solution.py:362
  215.9 16.1 %collective-permute-start.2 = (bf16[8,64,128]{2,1,0:T(8,128)(2,1)}, bf16[8,64,128]{2,1,0:T(8,128)(2,1)S(1)}, u32[]{:S(2)}, u32[]{:S(2)}) collective-permute-start(bf16[8,64,128]{2,1,0:T(8,128)(2,1)} %get-tuple-element.76), channel_id=1, source_target_pairs={{0,6},{2,4},{4,2},{6,0},{8,14},{10,12},{12,10},{14,8},{16,22},{18,... | collective-permute-start | bytes 393224 | tf_op jit(solution)/shard_map/ppermute | solution.py:362
  215.9 17.5 %collective-permute-start.3 = (bf16[8,64,128]{2,1,0:T(8,128)(2,1)}, bf16[8,64,128]{2,1,0:T(8,128)(2,1)S(1)}, u32[]{:S(2)}, u32[]{:S(2)}) collective-permute-start(bf16[8,64,128]{2,1,0:T(8,128)(2,1)} %get-tuple-element.77), channel_id=1, source_target_pairs={{0,8},{2,10},{4,12},{6,14},{8,0},{10,2},{12,4},{14,6},{16,24},{18,... | collective-permute-start | bytes 393224 | tf_op jit(solution)/shard_map/ppermute | solution.py:362
  218.6 14.8 %collective-permute-start.4 = (bf16[8,64,128]{2,1,0:T(8,128)(2,1)}, bf16[8,64,128]{2,1,0:T(8,128)(2,1)S(1)}, u32[]{:S(2)}, u32[]{:S(2)}) collective-permute-start(bf16[8,64,128]{2,1,0:T(8,128)(2,1)} %get-tuple-element.78), channel_id=1, source_target_pairs={{0,10},{2,8},{4,14},{6,12},{8,2},{10,0},{12,6},{14,4},{16,26},{18,... | collective-permute-start | bytes 393224 | tf_op jit(solution)/shard_map/ppermute | solution.py:362
  223.1 10.3 %collective-permute-start.5 = (bf16[8,64,128]{2,1,0:T(8,128)(2,1)}, bf16[8,64,128]{2,1,0:T(8,128)(2,1)}, u32[]{:S(2)}, u32[]{:S(2)}) collective-permute-start(bf16[8,64,128]{2,1,0:T(8,128)(2,1)} %get-tuple-element.79), channel_id=1, source_target_pairs={{0,12},{2,14},{4,8},{6,10},{8,4},{10,6},{12,0},{14,2},{16,28},{18,... | collective-permute-start | bytes 393224 | tf_op jit(solution)/shard_map/ppermute | solution.py:362
  232.0 24.6 %collective-permute-start.16 = (bf16[8,8,64,128]{3,2,1,0:T(8,128)(2,1)}, bf16[8,8,64,128]{3,2,1,0:T(8,128)(2,1)S(1)}, u32[]{:S(2)}, u32[]{:S(2)}) collective-permute-start(bf16[8,8,64,128]{3,2,1,0:T(8,128)(2,1)} %shard_map.48.rest_1_), channel_id=1, source_target_pairs={{0,1},{1,0},{2,3},{3,2},{4,5},{5,4},{6,7},{7,6},{8,9},{9,8},{10,11... | collective-permute-start | bytes 3145736 | tf_op jit(solution)/shard_map/ppermute | solution.py:370
  236.5 42.7 %collective-permute-start.15 = (bf16[8,8,64,128]{3,2,1,0:T(8,128)(2,1)}, bf16[8,8,64,128]{3,2,1,0:T(8,128)(2,1)}, u32[]{:S(2)}, u32[]{:S(2)}) collective-permute-start(bf16[8,8,64,128]{3,2,1,0:T(8,128)(2,1)} %shard_map.47.rest_0_), channel_id=1, source_target_pairs={{0,1},{1,0},{2,3},{3,2},{4,5},{5,4},{6,7},{7,6},{8,9},{9,8},{10,11... | collective-permute-start | bytes 3145736 | tf_op jit(solution)/shard_map/ppermute | solution.py:370
  295.2 164.3 %all-to-all-start = ((bf16[16,8,64,128]{3,2,1,0:T(8,128)(2,1)}), bf16[16,8,64,128]{3,2,1,0:T(8,128)(2,1)S(1)}, u32[]{:S(2)}, u32[]{:S(2)}) async-start(bf16[16,8,64,128]{3,2,1,0:T(8,128)(2,1)} %shard_map.49), calls=%async_computation | async-start | bytes 4194304 | tf_op jit(solution)/shard_map/all_to_all | solution.py:374
  316.6 9.4 %collective-permute-start.52 = (bf16[8,64,128]{2,1,0:T(8,128)(2,1)}, bf16[8,64,128]{2,1,0:T(8,128)(2,1)S(1)}, u32[]{:S(2)}, u32[]{:S(2)}) collective-permute-start(bf16[8,64,128]{2,1,0:T(8,128)(2,1)} %get-tuple-element.123), channel_id=1, source_target_pairs={{0,4},{2,6},{4,0},{6,2},{8,12},{10,14},{12,8},{14,10},{16,20},{18,... | collective-permute-start | bytes 393224 | tf_op jit(solution)/shard_map/ppermute | solution.py:362
  318.2 47.4 %collective-permute-start.58 = (bf16[8,64,128]{2,1,0:T(8,128)(2,1)}, bf16[8,64,128]{2,1,0:T(8,128)(2,1)S(1)}, u32[]{:S(2)}, u32[]{:S(2)}) collective-permute-start(bf16[8,64,128]{2,1,0:T(8,128)(2,1)} %get-tuple-element.129), channel_id=1, source_target_pairs={{0,16},{2,18},{4,20},{6,22},{8,24},{10,26},{12,28},{14,30},{16,0},... | collective-permute-start | bytes 393224 | tf_op jit(solution)/shard_map/ppermute | solution.py:362
  320.3 49.0 %collective-permute-start.59 = (bf16[8,64,128]{2,1,0:T(8,128)(2,1)}, bf16[8,64,128]{2,1,0:T(8,128)(2,1)S(1)}, u32[]{:S(2)}, u32[]{:S(2)}) collective-permute-start(bf16[8,64,128]{2,1,0:T(8,128)(2,1)} %get-tuple-element.130), channel_id=1, source_target_pairs={{0,18},{2,16},{4,22},{6,20},{8,26},{10,24},{12,30},{14,28},{16,2},... | collective-permute-start | bytes 393224 | tf_op jit(solution)/shard_map/ppermute | solution.py:362
  321.2 56.7 %collective-permute-start.60 = (bf16[8,64,128]{2,1,0:T(8,128)(2,1)}, bf16[8,64,128]{2,1,0:T(8,128)(2,1)S(1)}, u32[]{:S(2)}, u32[]{:S(2)}) collective-permute-start(bf16[8,64,128]{2,1,0:T(8,128)(2,1)} %get-tuple-element.131), channel_id=1, source_target_pairs={{0,20},{2,22},{4,16},{6,18},{8,28},{10,30},{12,24},{14,26},{16,4},... | collective-permute-start | bytes 393224 | tf_op jit(solution)/shard_map/ppermute | solution.py:362
  323.3 58.3 %collective-permute-start.61 = (bf16[8,64,128]{2,1,0:T(8,128)(2,1)}, bf16[8,64,128]{2,1,0:T(8,128)(2,1)S(1)}, u32[]{:S(2)}, u32[]{:S(2)}) collective-permute-start(bf16[8,64,128]{2,1,0:T(8,128)(2,1)} %get-tuple-element.132), channel_id=1, source_target_pairs={{0,22},{2,20},{4,18},{6,16},{8,30},{10,28},{12,26},{14,24},{16,6},... | collective-permute-start | bytes 393224 | tf_op jit(solution)/shard_map/ppermute | solution.py:362
  326.0 55.5 %collective-permute-start.62 = (bf16[8,64,128]{2,1,0:T(8,128)(2,1)}, bf16[8,64,128]{2,1,0:T(8,128)(2,1)S(1)}, u32[]{:S(2)}, u32[]{:S(2)}) collective-permute-start(bf16[8,64,128]{2,1,0:T(8,128)(2,1)} %get-tuple-element.133), channel_id=1, source_target_pairs={{0,24},{2,26},{4,28},{6,30},{8,16},{10,18},{12,20},{14,22},{16,8},... | collective-permute-start | bytes 393224 | tf_op jit(solution)/shard_map/ppermute | solution.py:362
  365.7 18.5 %collective-permute-start.63 = (bf16[8,64,128]{2,1,0:T(8,128)(2,1)}, bf16[8,64,128]{2,1,0:T(8,128)(2,1)S(1)}, u32[]{:S(2)}, u32[]{:S(2)}) collective-permute-start(bf16[8,64,128]{2,1,0:T(8,128)(2,1)} %get-tuple-element.134), channel_id=1, source_target_pairs={{0,26},{2,24},{4,30},{6,28},{8,18},{10,16},{12,22},{14,20},{16,10}... | collective-permute-start | bytes 393224 | tf_op jit(solution)/shard_map/ppermute | solution.py:362
  369.3 19.4 %collective-permute-start.64 = (bf16[8,64,128]{2,1,0:T(8,128)(2,1)}, bf16[8,64,128]{2,1,0:T(8,128)(2,1)S(1)}, u32[]{:S(2)}, u32[]{:S(2)}) collective-permute-start(bf16[8,64,128]{2,1,0:T(8,128)(2,1)} %get-tuple-element.135), channel_id=1, source_target_pairs={{0,28},{2,30},{4,24},{6,26},{8,20},{10,22},{12,16},{14,18},{16,12}... | collective-permute-start | bytes 393224 | tf_op jit(solution)/shard_map/ppermute | solution.py:362
  377.9 14.3 %collective-permute-start.65 = (bf16[8,64,128]{2,1,0:T(8,128)(2,1)}, bf16[8,64,128]{2,1,0:T(8,128)(2,1)S(1)}, u32[]{:S(2)}, u32[]{:S(2)}) collective-permute-start(bf16[8,64,128]{2,1,0:T(8,128)(2,1)} %get-tuple-element.136), channel_id=1, source_target_pairs={{0,30},{2,28},{4,26},{6,24},{8,22},{10,20},{12,18},{14,16},{16,14}... | collective-permute-start | bytes 393224 | tf_op jit(solution)/shard_map/ppermute | solution.py:362
  381.5 16.1 %collective-permute-start.53 = (bf16[8,64,128]{2,1,0:T(8,128)(2,1)}, bf16[8,64,128]{2,1,0:T(8,128)(2,1)S(1)}, u32[]{:S(2)}, u32[]{:S(2)}) collective-permute-start(bf16[8,64,128]{2,1,0:T(8,128)(2,1)} %get-tuple-element.124), channel_id=1, source_target_pairs={{0,6},{2,4},{4,2},{6,0},{8,14},{10,12},{12,10},{14,8},{16,22},{18,... | collective-permute-start | bytes 393224 | tf_op jit(solution)/shard_map/ppermute | solution.py:362
  381.5 17.4 %collective-permute-start.54 = (bf16[8,64,128]{2,1,0:T(8,128)(2,1)}, bf16[8,64,128]{2,1,0:T(8,128)(2,1)S(1)}, u32[]{:S(2)}, u32[]{:S(2)}) collective-permute-start(bf16[8,64,128]{2,1,0:T(8,128)(2,1)} %get-tuple-element.125), channel_id=1, source_target_pairs={{0,8},{2,10},{4,12},{6,14},{8,0},{10,2},{12,4},{14,6},{16,24},{18,... | collective-permute-start | bytes 393224 | tf_op jit(solution)/shard_map/ppermute | solution.py:362
  384.2 14.8 %collective-permute-start.55 = (bf16[8,64,128]{2,1,0:T(8,128)(2,1)}, bf16[8,64,128]{2,1,0:T(8,128)(2,1)S(1)}, u32[]{:S(2)}, u32[]{:S(2)}) collective-permute-start(bf16[8,64,128]{2,1,0:T(8,128)(2,1)} %get-tuple-element.126), channel_id=1, source_target_pairs={{0,10},{2,8},{4,14},{6,12},{8,2},{10,0},{12,6},{14,4},{16,26},{18,... | collective-permute-start | bytes 393224 | tf_op jit(solution)/shard_map/ppermute | solution.py:362
  388.7 10.3 %collective-permute-start.56 = (bf16[8,64,128]{2,1,0:T(8,128)(2,1)}, bf16[8,64,128]{2,1,0:T(8,128)(2,1)}, u32[]{:S(2)}, u32[]{:S(2)}) collective-permute-start(bf16[8,64,128]{2,1,0:T(8,128)(2,1)} %get-tuple-element.127), channel_id=1, source_target_pairs={{0,12},{2,14},{4,8},{6,10},{8,4},{10,6},{12,0},{14,2},{16,28},{18,... | collective-permute-start | bytes 393224 | tf_op jit(solution)/shard_map/ppermute | solution.py:362
  397.6 24.6 %collective-permute-start.67 = (bf16[8,8,64,128]{3,2,1,0:T(8,128)(2,1)}, bf16[8,8,64,128]{3,2,1,0:T(8,128)(2,1)S(1)}, u32[]{:S(2)}, u32[]{:S(2)}) collective-permute-start(bf16[8,8,64,128]{3,2,1,0:T(8,128)(2,1)} %shard_map.60.rest_1_), channel_id=1, source_target_pairs={{0,1},{1,0},{2,3},{3,2},{4,5},{5,4},{6,7},{7,6},{8,9},{9,8},{10,11... | collective-permute-start | bytes 3145736 | tf_op jit(solution)/shard_map/ppermute | solution.py:370
  402.1 42.7 %collective-permute-start.66 = (bf16[8,8,64,128]{3,2,1,0:T(8,128)(2,1)}, bf16[8,8,64,128]{3,2,1,0:T(8,128)(2,1)}, u32[]{:S(2)}, u32[]{:S(2)}) collective-permute-start(bf16[8,8,64,128]{3,2,1,0:T(8,128)(2,1)} %shard_map.59.rest_0_), channel_id=1, source_target_pairs={{0,1},{1,0},{2,3},{3,2},{4,5},{5,4},{6,7},{7,6},{8,9},{9,8},{10,11... | collective-permute-start | bytes 3145736 | tf_op jit(solution)/shard_map/ppermute | solution.py:370
  460.8 164.3 %all-to-all-start.3 = ((bf16[16,8,64,128]{3,2,1,0:T(8,128)(2,1)}), bf16[16,8,64,128]{3,2,1,0:T(8,128)(2,1)S(1)}, u32[]{:S(2)}, u32[]{:S(2)}) async-start(bf16[16,8,64,128]{3,2,1,0:T(8,128)(2,1)} %shard_map.61), calls=%async_computation.3 | async-start | bytes 4194304 | tf_op jit(solution)/shard_map/all_to_all | solution.py:374
  481.4 9.3 %collective-permute-start.18 = (bf16[8,64,128]{2,1,0:T(8,128)(2,1)}, bf16[8,64,128]{2,1,0:T(8,128)(2,1)S(1)}, u32[]{:S(2)}, u32[]{:S(2)}) collective-permute-start(bf16[8,64,128]{2,1,0:T(8,128)(2,1)} %get-tuple-element.91), channel_id=1, source_target_pairs={{0,4},{2,6},{4,0},{6,2},{8,12},{10,14},{12,8},{14,10},{16,20},{18,... | collective-permute-start | bytes 393224 | tf_op jit(solution)/shard_map/ppermute | solution.py:362
  483.0 48.3 %collective-permute-start.24 = (bf16[8,64,128]{2,1,0:T(8,128)(2,1)}, bf16[8,64,128]{2,1,0:T(8,128)(2,1)S(1)}, u32[]{:S(2)}, u32[]{:S(2)}) collective-permute-start(bf16[8,64,128]{2,1,0:T(8,128)(2,1)} %get-tuple-element.97), channel_id=1, source_target_pairs={{0,16},{2,18},{4,20},{6,22},{8,24},{10,26},{12,28},{14,30},{16,0},... | collective-permute-start | bytes 393224 | tf_op jit(solution)/shard_map/ppermute | solution.py:362
  485.1 49.8 %collective-permute-start.25 = (bf16[8,64,128]{2,1,0:T(8,128)(2,1)}, bf16[8,64,128]{2,1,0:T(8,128)(2,1)S(1)}, u32[]{:S(2)}, u32[]{:S(2)}) collective-permute-start(bf16[8,64,128]{2,1,0:T(8,128)(2,1)} %get-tuple-element.98), channel_id=1, source_target_pairs={{0,18},{2,16},{4,22},{6,20},{8,26},{10,24},{12,30},{14,28},{16,2},... | collective-permute-start | bytes 393224 | tf_op jit(solution)/shard_map/ppermute | solution.py:362
  485.9 57.5 %collective-permute-start.26 = (bf16[8,64,128]{2,1,0:T(8,128)(2,1)}, bf16[8,64,128]{2,1,0:T(8,128)(2,1)S(1)}, u32[]{:S(2)}, u32[]{:S(2)}) collective-permute-start(bf16[8,64,128]{2,1,0:T(8,128)(2,1)} %get-tuple-element.99), channel_id=1, source_target_pairs={{0,20},{2,22},{4,16},{6,18},{8,28},{10,30},{12,24},{14,26},{16,4},... | collective-permute-start | bytes 393224 | tf_op jit(solution)/shard_map/ppermute | solution.py:362
  488.0 59.1 %collective-permute-start.27 = (bf16[8,64,128]{2,1,0:T(8,128)(2,1)}, bf16[8,64,128]{2,1,0:T(8,128)(2,1)S(1)}, u32[]{:S(2)}, u32[]{:S(2)}) collective-permute-start(bf16[8,64,128]{2,1,0:T(8,128)(2,1)} %get-tuple-element.100), channel_id=1, source_target_pairs={{0,22},{2,20},{4,18},{6,16},{8,30},{10,28},{12,26},{14,24},{16,6},... | collective-permute-start | bytes 393224 | tf_op jit(solution)/shard_map/ppermute | solution.py:362
  490.7 56.5 %collective-permute-start.28 = (bf16[8,64,128]{2,1,0:T(8,128)(2,1)}, bf16[8,64,128]{2,1,0:T(8,128)(2,1)S(1)}, u32[]{:S(2)}, u32[]{:S(2)}) collective-permute-start(bf16[8,64,128]{2,1,0:T(8,128)(2,1)} %get-tuple-element.101), channel_id=1, source_target_pairs={{0,24},{2,26},{4,28},{6,30},{8,16},{10,18},{12,20},{14,22},{16,8},... | collective-permute-start | bytes 393224 | tf_op jit(solution)/shard_map/ppermute | solution.py:362
  531.3 18.5 %collective-permute-start.29 = (bf16[8,64,128]{2,1,0:T(8,128)(2,1)}, bf16[8,64,128]{2,1,0:T(8,128)(2,1)S(1)}, u32[]{:S(2)}, u32[]{:S(2)}) collective-permute-start(bf16[8,64,128]{2,1,0:T(8,128)(2,1)} %get-tuple-element.102), channel_id=1, source_target_pairs={{0,26},{2,24},{4,30},{6,28},{8,18},{10,16},{12,22},{14,20},{16,10}... | collective-permute-start | bytes 393224 | tf_op jit(solution)/shard_map/ppermute | solution.py:362
  534.9 19.4 %collective-permute-start.30 = (bf16[8,64,128]{2,1,0:T(8,128)(2,1)}, bf16[8,64,128]{2,1,0:T(8,128)(2,1)S(1)}, u32[]{:S(2)}, u32[]{:S(2)}) collective-permute-start(bf16[8,64,128]{2,1,0:T(8,128)(2,1)} %get-tuple-element.103), channel_id=1, source_target_pairs={{0,28},{2,30},{4,24},{6,26},{8,20},{10,22},{12,16},{14,18},{16,12}... | collective-permute-start | bytes 393224 | tf_op jit(solution)/shard_map/ppermute | solution.py:362
  543.5 14.3 %collective-permute-start.31 = (bf16[8,64,128]{2,1,0:T(8,128)(2,1)}, bf16[8,64,128]{2,1,0:T(8,128)(2,1)S(1)}, u32[]{:S(2)}, u32[]{:S(2)}) collective-permute-start(bf16[8,64,128]{2,1,0:T(8,128)(2,1)} %get-tuple-element.104), channel_id=1, source_target_pairs={{0,30},{2,28},{4,26},{6,24},{8,22},{10,20},{12,18},{14,16},{16,14}... | collective-permute-start | bytes 393224 | tf_op jit(solution)/shard_map/ppermute | solution.py:362
  547.1 16.1 %collective-permute-start.19 = (bf16[8,64,128]{2,1,0:T(8,128)(2,1)}, bf16[8,64,128]{2,1,0:T(8,128)(2,1)S(1)}, u32[]{:S(2)}, u32[]{:S(2)}) collective-permute-start(bf16[8,64,128]{2,1,0:T(8,128)(2,1)} %get-tuple-element.92), channel_id=1, source_target_pairs={{0,6},{2,4},{4,2},{6,0},{8,14},{10,12},{12,10},{14,8},{16,22},{18,... | collective-permute-start | bytes 393224 | tf_op jit(solution)/shard_map/ppermute | solution.py:362
  547.1 17.5 %collective-permute-start.20 = (bf16[8,64,128]{2,1,0:T(8,128)(2,1)}, bf16[8,64,128]{2,1,0:T(8,128)(2,1)S(1)}, u32[]{:S(2)}, u32[]{:S(2)}) collective-permute-start(bf16[8,64,128]{2,1,0:T(8,128)(2,1)} %get-tuple-element.93), channel_id=1, source_target_pairs={{0,8},{2,10},{4,12},{6,14},{8,0},{10,2},{12,4},{14,6},{16,24},{18,... | collective-permute-start | bytes 393224 | tf_op jit(solution)/shard_map/ppermute | solution.py:362
  549.8 14.8 %collective-permute-start.21 = (bf16[8,64,128]{2,1,0:T(8,128)(2,1)}, bf16[8,64,128]{2,1,0:T(8,128)(2,1)S(1)}, u32[]{:S(2)}, u32[]{:S(2)}) collective-permute-start(bf16[8,64,128]{2,1,0:T(8,128)(2,1)} %get-tuple-element.94), channel_id=1, source_target_pairs={{0,10},{2,8},{4,14},{6,12},{8,2},{10,0},{12,6},{14,4},{16,26},{18,... | collective-permute-start | bytes 393224 | tf_op jit(solution)/shard_map/ppermute | solution.py:362
  554.3 10.3 %collective-permute-start.22 = (bf16[8,64,128]{2,1,0:T(8,128)(2,1)}, bf16[8,64,128]{2,1,0:T(8,128)(2,1)}, u32[]{:S(2)}, u32[]{:S(2)}) collective-permute-start(bf16[8,64,128]{2,1,0:T(8,128)(2,1)} %get-tuple-element.95), channel_id=1, source_target_pairs={{0,12},{2,14},{4,8},{6,10},{8,4},{10,6},{12,0},{14,2},{16,28},{18,... | collective-permute-start | bytes 393224 | tf_op jit(solution)/shard_map/ppermute | solution.py:362
  563.3 24.6 %collective-permute-start.33 = (bf16[8,8,64,128]{3,2,1,0:T(8,128)(2,1)}, bf16[8,8,64,128]{3,2,1,0:T(8,128)(2,1)S(1)}, u32[]{:S(2)}, u32[]{:S(2)}) collective-permute-start(bf16[8,8,64,128]{3,2,1,0:T(8,128)(2,1)} %shard_map.52.rest_1_), channel_id=1, source_target_pairs={{0,1},{1,0},{2,3},{3,2},{4,5},{5,4},{6,7},{7,6},{8,9},{9,8},{10,11... | collective-permute-start | bytes 3145736 | tf_op jit(solution)/shard_map/ppermute | solution.py:370
  567.6 42.8 %collective-permute-start.32 = (bf16[8,8,64,128]{3,2,1,0:T(8,128)(2,1)}, bf16[8,8,64,128]{3,2,1,0:T(8,128)(2,1)}, u32[]{:S(2)}, u32[]{:S(2)}) collective-permute-start(bf16[8,8,64,128]{3,2,1,0:T(8,128)(2,1)} %shard_map.51.rest_0_), channel_id=1, source_target_pairs={{0,1},{1,0},{2,3},{3,2},{4,5},{5,4},{6,7},{7,6},{8,9},{9,8},{10,11... | collective-permute-start | bytes 3145736 | tf_op jit(solution)/shard_map/ppermute | solution.py:370
  626.5 47.1 %all-to-all-start.1 = ((bf16[16,8,64,128]{3,2,1,0:T(8,128)(2,1)}), bf16[16,8,64,128]{3,2,1,0:T(8,128)(2,1)}, u32[]{:S(2)}, u32[]{:S(2)}) async-start(bf16[16,8,64,128]{3,2,1,0:T(8,128)(2,1)} %shard_map.53), calls=%async_computation.1 | async-start | bytes 4194304 | tf_op jit(solution)/shard_map/all_to_all | solution.py:374
  (71 other events, 1218.4 us)

commit v3 on v2

--- a/solution.py
+++ b/solution.py
@@ -17,12 +17,13 @@
 CHUNKS = 2
 GROUP = 16
 QUAD = 4
-SLOTS = 4
-BATCH = 8
+SLOTS = 3
+BATCH = 16
 REACHES = 2
 F32 = jnp.float32
 BF16 = jnp.bfloat16
-VMEM_LIMIT = 60 * 1024 * 1024
+VMEM_LIMIT = 24 * 1024 * 1024
+TIME_VMEM_LIMIT = 50 * 1024 * 1024
 
 
 def phase_tables():
@@ -170,7 +171,7 @@
         out_shape=out_shape,
         scratch_shapes=[rows_scratch] * scratches,
         input_output_aliases=aliases,
-        compiler_params=pltpu.CompilerParams(vmem_limit_bytes=VMEM_LIMIT),
+        compiler_params=pltpu.CompilerParams(vmem_limit_bytes=TIME_VMEM_LIMIT),
         cost_estimate=pl.CostEstimate(
             flops=4 * passes * elements * NF, bytes_accessed=8 * elements, transcendentals=0
         ),
@@ -205,6 +206,7 @@
             jax.ShapeDtypeStruct((freqs * row_tiles * column_tiles + BATCH,), jnp.int32),
             jax.ShapeDtypeStruct((1,), jnp.int32),
         ],
+        compiler_params=pltpu.CompilerParams(vmem_limit_bytes=1024 * 1024),
         name="list_tiles",
     )(tile_mask)
 

time: 690 us -> 674 us (0.977)
  Pallas kernels: 150 us -> 124 us
  starting transfers between devices: 167 us -> 176 us
    pallas_call x4, Pallas kernels: 58.7 us -> 44.3 us  [product_call(): pl.pallas_call(functools.partial(product_kernel, parts=parts), in_specs=[...]
    pallas_call x8, Pallas kernels: 18.7 us -> 11.2 us  [collect_call(): pl.pallas_call(collect_kernel, in_specs=[pl.BlockSpec(memory_space=pl.ANY...]
  transfers between devices with their start and end apart: 72 -> 72, of which waited for: 29 -> 30; matrix products, arithmetic and copies ran while one was open for 0% -> 0% of each run, Pallas kernels for 17% -> 14%
where the time goes in v3:
time: 674 us; the launch traced here: 667 us
  waiting for transfers between devices  360 us (53%)
  starting transfers between devices  176 us (26%)
  Pallas kernels  124 us (18%)
    ppermute x60, waiting for transfers between devices, spread(): got[shift] = lax.ppermute(blocks[shift], 'freq', pairs)  166 us
    ppermute x8, waiting for transfers between devices, spread(): fields[shift].append(lax.ppermute(mine, 'rows', ring))  162 us
    ppermute x60, starting transfers between devices, spread(): got[shift] = lax.ppermute(blocks[shift], 'freq', pairs)  136 us
    pallas_call x6, Pallas kernels, time_call(): pl.pallas_call(functools.partial(body, half=half), grid=(receivers // GRO...  64 us
    pallas_call x4, Pallas kernels, product_call(): pl.pallas_call(functools.partial(product_kernel, parts=parts), in_specs=[...  44.3 us
    all_to_all x4, waiting for transfers between devices, gather(): return lax.all_to_all(bands, 'freq', 0, 0, tiled=True)  31.9 us
    all_to_all x4, starting transfers between devices, gather(): return lax.all_to_all(bands, 'freq', 0, 0, tiled=True)  26.7 us
  transfers between devices with their start and end apart: 72, of which 30 were waited for; matrix products, arithmetic and copies ran while one was open for 0% of the time, Pallas kernels for 14%

profile of v3, /device:TPU:1, one launch (start us, length us, event | category | flops | bytes accessed | tf_op | source)
XLA Modules:
  0.0 667.0 jit_solution(8889479037813573045)
XLA Ops:
  0.7 8.2 %shard_map.54 = (bf16[8,64,128]{2,1,0:T(8,128)(2,1)S(1)}, bf16[8,64,128]{2,1,0:T(8,128)(2,1)S(1)}, bf16[8,64,128]{2,1,0:T(8,128)(2,1)S(1)}, bf16[8,64,128]{2,1,0...) custom-call(s32[1]{0:T(128)} %bitcast.mine_ref, ...), custom_call_target="tpu_custom_call" | custom-call | flops 3221225472 | bytes 16777216 | tf_op jit(solution)/shard_map/pallas_call | solution.py:166
  8.9 2.7 collective-permute-start.35
  11.7 2.3 collective-permute-start.41
  14.6 2.2 collective-permute-start.43
  18.1 3.1 collective-permute-start.45
  21.2 10.1 %collective-permute-done.41.refs_0_ = bf16[8,64,128]{2,1,0:T(8,128)(2,1)S(1)} collective-permute-done((bf16[8,64,128]{2,1,0:T(8,128)(2,1)S(1)}, bf16[8,64,128]{2,1,0:T(8,128)(2,1)S(1)}, u32[]{:S(2)}, u32[]{:S(2)}) %collective-permute-start.41) | collective-permute-done | bytes 131104 | tf_op jit(solution)/shard_map/ppermute | solution.py:364
  31.3 4.4 collective-permute-start.46
  35.8 2.3 collective-permute-start.47
  38.0 9.8 %collective-permute-start.48 = (bf16[8,64,128]{2,1,0:T(8,128)(2,1)S(1)}, bf16[8,64,128]{2,1,0:T(8,128)(2,1)S(1)}, u32[]{:S(2)}, u32[]{:S(2)}) collective-permute-start(bf16[8,64,128]{2,1,0:T(8,128)(2,1)S(1)} %get-tuple-element.120), channel_id=1, source_target_pairs={{0,30},{2,28},{4,26},{6,24},{8,22},{10,20},{12,18},{14,16},{16,14}... | collective-permute-start | bytes 393224 | tf_op jit(solution)/shard_map/ppermute | solution.py:364
  49.3 6.0 collective-permute-start.38
  55.3 2.4 collective-permute-start.39
  57.8 3.1 collective-permute-start.40
  67.2 4.8 list_tiles.1
  72.1 14.3 %collective-permute-done.50.rest_3_ = bf16[8,8,64,128]{3,2,1,0:T(8,128)(2,1)S(1)} collective-permute-done((bf16[8,8,64,128]{3,2,1,0:T(8,128)(2,1)S(1)}, bf16[8,8,64,128]{3,2,1,0:T(8,128)(2,1)S(1)}, u32[]{:S(2)}, u32[]{:S(2)}) %collective-permute-start.50) | collective-permute-done | bytes 1048608 | tf_op jit(solution)/shard_map/ppermute | solution.py:372
  86.4 22.6 %collective-permute-done.49.rest_2_ = bf16[8,8,64,128]{3,2,1,0:T(8,128)(2,1)} collective-permute-done((bf16[8,8,64,128]{3,2,1,0:T(8,128)(2,1)S(1)}, bf16[8,8,64,128]{3,2,1,0:T(8,128)(2,1)}, u32[]{:S(2)}, u32[]{:S(2)}) %collective-permute-start.49) | collective-permute-done | bytes 1048608 | tf_op jit(solution)/shard_map/ppermute | solution.py:372
  109.0 11.7 %shard_map.57 = bf16[16,8,64,128]{3,2,1,0:T(8,128)(2,1)} custom-call(s32[1040]{0:T(1024)S(1)} %get-tuple-element.71.tiles_ref, s32[1]{0:T(128)} %get-tuple-element.72.count_ref, s32[3]{0:T(128)S(1)} %pad_add_fusion.place_ref, bf16[2,8,1024,2048]{3,2,1,0:T(8,128)(2,1)} %kernel_ref.7, bf16[8,8,64,128]{3,2,1,0:T(8,128)(2,1)S(1)} %shard_map.55.rest_0_, ...), custom_call_target="tpu_custom_call" | custom-call | flops 1073741824 | bytes 8388608 | tf_op jit(solution)/shard_map/pallas_call | solution.py:304
  120.7 8.5 %all-to-all-start.2 = ((bf16[16,8,64,128]{3,2,1,0:T(8,128)(2,1)}), bf16[16,8,64,128]{3,2,1,0:T(8,128)(2,1)S(1)}, u32[]{:S(2)}, u32[]{:S(2)}) async-start(bf16[16,8,64,128]{3,2,1,0:T(8,128)(2,1)} %shard_map.57), calls=%async_computation.2 | async-start | bytes 4194304 | tf_op jit(solution)/shard_map/all_to_all | solution.py:376
  129.2 8.1 %shard_map.46 = (bf16[8,64,128]{2,1,0:T(8,128)(2,1)S(1)}, bf16[8,64,128]{2,1,0:T(8,128)(2,1)S(1)}, bf16[8,64,128]{2,1,0:T(8,128)(2,1)S(1)}, bf16[8,64,128]{2,1,0...) custom-call(s32[1]{0:T(128)} %bitcast.mine_ref, ...), custom_call_target="tpu_custom_call" | custom-call | flops 3221225472 | bytes 16777216 | tf_op jit(solution)/shard_map/pallas_call | solution.py:166
  146.5 2.8 collective-permute-start.11
  149.3 44.9 %collective-permute-done.7.refs_0_ = bf16[8,64,128]{2,1,0:T(8,128)(2,1)S(1)} collective-permute-done((bf16[8,64,128]{2,1,0:T(8,128)(2,1)S(1)}, bf16[8,64,128]{2,1,0:T(8,128)(2,1)S(1)}, u32[]{:S(2)}, u32[]{:S(2)}) %collective-permute-start.7) | collective-permute-done | bytes 131104 | tf_op jit(solution)/shard_map/ppermute | solution.py:364
  194.2 2.6 collective-permute-start.12
  199.9 6.5 collective-permute-done.9.refs_2_
  206.4 2.6 collective-permute-start.14
  210.0 4.1 collective-permute-start.3
  214.1 3.1 collective-permute-start.4
  217.2 3.4 collective-permute-start.5
  220.7 3.1 collective-permute-start.6
  230.6 19.2 %collective-permute-done.16.rest_3_ = bf16[8,8,64,128]{3,2,1,0:T(8,128)(2,1)S(1)} collective-permute-done((bf16[8,8,64,128]{3,2,1,0:T(8,128)(2,1)S(1)}, bf16[8,8,64,128]{3,2,1,0:T(8,128)(2,1)S(1)}, u32[]{:S(2)}, u32[]{:S(2)}) %collective-permute-start.16) | collective-permute-done | bytes 1048608 | tf_op jit(solution)/shard_map/ppermute | solution.py:372
  249.8 22.5 %collective-permute-done.15.rest_2_ = bf16[8,8,64,128]{3,2,1,0:T(8,128)(2,1)S(1)} collective-permute-done((bf16[8,8,64,128]{3,2,1,0:T(8,128)(2,1)S(1)}, bf16[8,8,64,128]{3,2,1,0:T(8,128)(2,1)S(1)}, u32[]{:S(2)}, u32[]{:S(2)}) %collective-permute-start.15) | collective-permute-done | bytes 1048608 | tf_op jit(solution)/shard_map/ppermute | solution.py:372
  272.3 11.7 %shard_map.49 = bf16[16,8,64,128]{3,2,1,0:T(8,128)(2,1)} custom-call(s32[1040]{0:T(1024)S(1)} %get-tuple-element.71.tiles_ref, s32[1]{0:T(128)} %get-tuple-element.72.count_ref, s32[3]{0:T(128)S(1)} %pad_add_fusion.place_ref, bf16[2,8,1024,2048]{3,2,1,0:T(8,128)(2,1)} %kernel_ref.7, bf16[8,8,64,128]{3,2,1,0:T(8,128)(2,1)S(1)} %shard_map.47.rest_0_, ...), custom_call_target="tpu_custom_call" | custom-call | flops 1073741824 | bytes 8388608 | tf_op jit(solution)/shard_map/pallas_call | solution.py:304
  285.3 6.2 all-to-all-start
  291.6 13.9 %shard_map.58 = (bf16[8,64,128]{2,1,0:T(8,128)(2,1)S(1)}, bf16[8,64,128]{2,1,0:T(8,128)(2,1)S(1)}, bf16[8,64,128]{2,1,0:T(8,128)(2,1)S(1)}, bf16[8,64,128]{2,1,0...) custom-call(s32[1]{0:T(128)} %bitcast.mine_ref, ...), custom_call_target="tpu_custom_call" | custom-call | flops 5368709120 | bytes 16777216 | tf_op jit(solution)/shard_map/pallas_call | solution.py:166
  307.4 2.1 collective-permute-start.58
  314.4 2.5 collective-permute-start.62
  316.9 39.6 %collective-permute-done.58.refs_0_ = bf16[8,64,128]{2,1,0:T(8,128)(2,1)S(1)} collective-permute-done((bf16[8,64,128]{2,1,0:T(8,128)(2,1)S(1)}, bf16[8,64,128]{2,1,0:T(8,128)(2,1)S(1)}, u32[]{:S(2)}, u32[]{:S(2)}) %collective-permute-start.58) | collective-permute-done | bytes 131104 | tf_op jit(solution)/shard_map/ppermute | solution.py:364
  356.5 2.6 collective-permute-start.63
  362.2 6.5 collective-permute-done.60.refs_2_
  368.6 2.6 collective-permute-start.65
  372.3 4.1 collective-permute-start.54
  376.4 3.1 collective-permute-start.55
  379.5 3.4 collective-permute-start.56
  382.9 3.1 collective-permute-start.57
  393.0 19.4 %collective-permute-done.67.rest_3_ = bf16[8,8,64,128]{3,2,1,0:T(8,128)(2,1)S(1)} collective-permute-done((bf16[8,8,64,128]{3,2,1,0:T(8,128)(2,1)S(1)}, bf16[8,8,64,128]{3,2,1,0:T(8,128)(2,1)S(1)}, u32[]{:S(2)}, u32[]{:S(2)}) %collective-permute-start.67) | collective-permute-done | bytes 1048608 | tf_op jit(solution)/shard_map/ppermute | solution.py:372
  412.4 22.5 %collective-permute-done.66.rest_2_ = bf16[8,8,64,128]{3,2,1,0:T(8,128)(2,1)S(1)} collective-permute-done((bf16[8,8,64,128]{3,2,1,0:T(8,128)(2,1)S(1)}, bf16[8,8,64,128]{3,2,1,0:T(8,128)(2,1)S(1)}, u32[]{:S(2)}, u32[]{:S(2)}) %collective-permute-start.66) | collective-permute-done | bytes 1048608 | tf_op jit(solution)/shard_map/ppermute | solution.py:372
  434.8 10.3 %shard_map.61 = bf16[16,8,64,128]{3,2,1,0:T(8,128)(2,1)S(1)} custom-call(s32[1040]{0:T(1024)S(1)} %get-tuple-element.71.tiles_ref, s32[1]{0:T(128)} %get-tuple-element.72.count_ref, s32[3]{0:T(128)S(1)} %pad_add_fusion.place_ref, bf16[2,8,1024,2048]{3,2,1,0:T(8,128)(2,1)} %kernel_ref.7, bf16[8,8,64,128]{3,2,1,0:T(8,128)(2,1)S(1)} %shard_map.59.rest_0_, ...), custom_call_target="tpu_custom_call" | custom-call | flops 1073741824 | bytes 8388608 | tf_op jit(solution)/shard_map/pallas_call | solution.py:304
  447.8 6.0 all-to-all-start.3
  453.8 13.9 %shard_map.50 = (bf16[8,64,128]{2,1,0:T(8,128)(2,1)S(1)}, bf16[8,64,128]{2,1,0:T(8,128)(2,1)S(1)}, bf16[8,64,128]{2,1,0:T(8,128)(2,1)S(1)}, bf16[8,64,128]{2,1,0...) custom-call(s32[1]{0:T(128)} %bitcast.mine_ref, ...), custom_call_target="tpu_custom_call" | custom-call | flops 5368709120 | bytes 16777216 | tf_op jit(solution)/shard_map/pallas_call | solution.py:166
  472.5 2.1 collective-permute-start.26
  476.4 2.6 collective-permute-start.28
  479.0 39.9 %collective-permute-done.24.refs_0_ = bf16[8,64,128]{2,1,0:T(8,128)(2,1)S(1)} collective-permute-done((bf16[8,64,128]{2,1,0:T(8,128)(2,1)S(1)}, bf16[8,64,128]{2,1,0:T(8,128)(2,1)S(1)}, u32[]{:S(2)}, u32[]{:S(2)}) %collective-permute-start.24) | collective-permute-done | bytes 131104 | tf_op jit(solution)/shard_map/ppermute | solution.py:364
  518.8 2.6 collective-permute-start.29
  524.5 6.5 collective-permute-done.26.refs_2_
  531.0 2.6 collective-permute-start.31
  534.7 4.1 collective-permute-start.20
  538.8 3.1 collective-permute-start.21
  541.9 3.4 collective-permute-start.22
  545.3 3.1 collective-permute-start.23
  555.4 19.4 %collective-permute-done.33.rest_3_ = bf16[8,8,64,128]{3,2,1,0:T(8,128)(2,1)S(1)} collective-permute-done((bf16[8,8,64,128]{3,2,1,0:T(8,128)(2,1)S(1)}, bf16[8,8,64,128]{3,2,1,0:T(8,128)(2,1)S(1)}, u32[]{:S(2)}, u32[]{:S(2)}) %collective-permute-start.33) | collective-permute-done | bytes 1048608 | tf_op jit(solution)/shard_map/ppermute | solution.py:372
  574.7 22.5 %collective-permute-done.32.rest_2_ = bf16[8,8,64,128]{3,2,1,0:T(8,128)(2,1)S(1)} collective-permute-done((bf16[8,8,64,128]{3,2,1,0:T(8,128)(2,1)S(1)}, bf16[8,8,64,128]{3,2,1,0:T(8,128)(2,1)S(1)}, u32[]{:S(2)}, u32[]{:S(2)}) %collective-permute-start.32) | collective-permute-done | bytes 1048608 | tf_op jit(solution)/shard_map/ppermute | solution.py:372
  597.2 10.6 %shard_map.53 = bf16[16,8,64,128]{3,2,1,0:T(8,128)(2,1)S(1)} custom-call(s32[1040]{0:T(1024)S(1)} %get-tuple-element.71.tiles_ref, s32[1]{0:T(128)} %get-tuple-element.72.count_ref, s32[3]{0:T(128)S(1)} %pad_add_fusion.place_ref, bf16[2,8,1024,2048]{3,2,1,0:T(8,128)(2,1)} %kernel_ref.7, bf16[8,8,64,128]{3,2,1,0:T(8,128)(2,1)S(1)} %shard_map.51.rest_0_, ...), custom_call_target="tpu_custom_call" | custom-call | flops 1073741824 | bytes 8388608 | tf_op jit(solution)/shard_map/pallas_call | solution.py:304
  609.2 6.1 all-to-all-start.1
  615.2 9.8 %shard_map.62.rest_0_ = f32[64,128,512]{2,1,0:T(8,128)} custom-call(s32[1]{0:T(128)} %bitcast.mine_ref, f32[64,128,512]{2,1,0:T(8,128)} %direct_ref.11, bf16[2,256,256]{2,1,0:T(8,128)(2,1)S(1)} %pad_maximum_fusion.tables_ref, s32[4,128,16]{2,1,0:T(8,128)S(1)} %bitcast.12, bf16[16,8,64,128]{3,2,1,0:T(8,128)(2,1)S(1)} %all-to-all-done.3.bands_ref), custom_call_target="tpu_custom_call" | custom-call | flops 2147483648 | bytes 16777216 | tf_op jit(solution)/shard_map/pallas_call | solution.py:166
  625.0 31.9 %all-to-all-done.1.bands_ref = bf16[16,8,64,128]{3,2,1,0:T(8,128)(2,1)} async-done(((bf16[16,8,64,128]{3,2,1,0:T(8,128)(2,1)}), bf16[16,8,64,128]{3,2,1,0:T(8,128)(2,1)}, u32[]{:S(2)}, u32[]{:S(2)}) %all-to-all-start.1) | async-done | bytes 2097184 | tf_op jit(solution)/shard_map/all_to_all | solution.py:376
  656.9 10.0 %shard_map.63 = f32[64,128,512]{2,1,0:T(8,128)} custom-call(s32[1]{0:T(128)} %bitcast.mine_ref, f32[64,128,512]{2,1,0:T(8,128)} %direct_ref.11, bf16[2,256,256]{2,1,0:T(8,128)(2,1)S(1)} %pad_maximum_fusion.tables_ref, s32[4,128,16]{2,1,0:T(8,128)S(1)} %bitcast.13, bf16[16,8,64,128]{3,2,1,0:T(8,128)(2,1)} %all-to-all-done.1.bands_ref, ...), custom_call_target="tpu_custom_call", output_to_operand_aliasing={{}: (5, {})} | custom-call | flops 2147483648 | bytes 16777216 | tf_op jit(solution)/shard_map/pallas_call | solution.py:166
  (118 shorter events, 71.7 us)
Async XLA Ops:
  8.9 9.1 %collective-permute-start.35 = (bf16[8,64,128]{2,1,0:T(8,128)(2,1)S(1)}, bf16[8,64,128]{2,1,0:T(8,128)(2,1)S(1)}, u32[]{:S(2)}, u32[]{:S(2)}) collective-permute-start(bf16[8,64,128]{2,1,0:T(8,128)(2,1)S(1)} %get-tuple-element.107), channel_id=1, source_target_pairs={{0,4},{2,6},{4,0},{6,2},{8,12},{10,14},{12,8},{14,10},{16,20},{18,... | collective-permute-start | bytes 393224 | tf_op jit(solution)/shard_map/ppermute | solution.py:364
  11.7 19.6 %collective-permute-start.41 = (bf16[8,64,128]{2,1,0:T(8,128)(2,1)S(1)}, bf16[8,64,128]{2,1,0:T(8,128)(2,1)S(1)}, u32[]{:S(2)}, u32[]{:S(2)}) collective-permute-start(bf16[8,64,128]{2,1,0:T(8,128)(2,1)S(1)} %get-tuple-element.113), channel_id=1, source_target_pairs={{0,16},{2,18},{4,20},{6,22},{8,24},{10,26},{12,28},{14,30},{16,0},... | collective-permute-start | bytes 393224 | tf_op jit(solution)/shard_map/ppermute | solution.py:364
  14.0 21.8 %collective-permute-start.42 = (bf16[8,64,128]{2,1,0:T(8,128)(2,1)S(1)}, bf16[8,64,128]{2,1,0:T(8,128)(2,1)S(1)}, u32[]{:S(2)}, u32[]{:S(2)}) collective-permute-start(bf16[8,64,128]{2,1,0:T(8,128)(2,1)S(1)} %get-tuple-element.114), channel_id=1, source_target_pairs={{0,18},{2,16},{4,22},{6,20},{8,26},{10,24},{12,30},{14,28},{16,2},... | collective-permute-start | bytes 393224 | tf_op jit(solution)/shard_map/ppermute | solution.py:364
  14.6 23.5 %collective-permute-start.43 = (bf16[8,64,128]{2,1,0:T(8,128)(2,1)S(1)}, bf16[8,64,128]{2,1,0:T(8,128)(2,1)S(1)}, u32[]{:S(2)}, u32[]{:S(2)}) collective-permute-start(bf16[8,64,128]{2,1,0:T(8,128)(2,1)S(1)} %get-tuple-element.115), channel_id=1, source_target_pairs={{0,20},{2,22},{4,16},{6,18},{8,28},{10,30},{12,24},{14,26},{16,4},... | collective-permute-start | bytes 393224 | tf_op jit(solution)/shard_map/ppermute | solution.py:364
  16.8 31.0 %collective-permute-start.44 = (bf16[8,64,128]{2,1,0:T(8,128)(2,1)S(1)}, bf16[8,64,128]{2,1,0:T(8,128)(2,1)S(1)}, u32[]{:S(2)}, u32[]{:S(2)}) collective-permute-start(bf16[8,64,128]{2,1,0:T(8,128)(2,1)S(1)} %get-tuple-element.116), channel_id=1, source_target_pairs={{0,22},{2,20},{4,18},{6,16},{8,30},{10,28},{12,26},{14,24},{16,6},... | collective-permute-start | bytes 393224 | tf_op jit(solution)/shard_map/ppermute | solution.py:364
  18.1 29.8 %collective-permute-start.45 = (bf16[8,64,128]{2,1,0:T(8,128)(2,1)S(1)}, bf16[8,64,128]{2,1,0:T(8,128)(2,1)S(1)}, u32[]{:S(2)}, u32[]{:S(2)}) collective-permute-start(bf16[8,64,128]{2,1,0:T(8,128)(2,1)S(1)} %get-tuple-element.117), channel_id=1, source_target_pairs={{0,24},{2,26},{4,28},{6,30},{8,16},{10,18},{12,20},{14,22},{16,8},... | collective-permute-start | bytes 393224 | tf_op jit(solution)/shard_map/ppermute | solution.py:364
  31.3 18.0 %collective-permute-start.46 = (bf16[8,64,128]{2,1,0:T(8,128)(2,1)S(1)}, bf16[8,64,128]{2,1,0:T(8,128)(2,1)S(1)}, u32[]{:S(2)}, u32[]{:S(2)}) collective-permute-start(bf16[8,64,128]{2,1,0:T(8,128)(2,1)S(1)} %get-tuple-element.118), channel_id=1, source_target_pairs={{0,26},{2,24},{4,30},{6,28},{8,18},{10,16},{12,22},{14,20},{16,10}... | collective-permute-start | bytes 393224 | tf_op jit(solution)/shard_map/ppermute | solution.py:364
  35.8 19.6 %collective-permute-start.47 = (bf16[8,64,128]{2,1,0:T(8,128)(2,1)S(1)}, bf16[8,64,128]{2,1,0:T(8,128)(2,1)S(1)}, u32[]{:S(2)}, u32[]{:S(2)}) collective-permute-start(bf16[8,64,128]{2,1,0:T(8,128)(2,1)S(1)} %get-tuple-element.119), channel_id=1, source_target_pairs={{0,28},{2,30},{4,24},{6,26},{8,20},{10,22},{12,16},{14,18},{16,12}... | collective-permute-start | bytes 393224 | tf_op jit(solution)/shard_map/ppermute | solution.py:364
  38.0 19.8 %collective-permute-start.48 = (bf16[8,64,128]{2,1,0:T(8,128)(2,1)S(1)}, bf16[8,64,128]{2,1,0:T(8,128)(2,1)S(1)}, u32[]{:S(2)}, u32[]{:S(2)}) collective-permute-start(bf16[8,64,128]{2,1,0:T(8,128)(2,1)S(1)} %get-tuple-element.120), channel_id=1, source_target_pairs={{0,30},{2,28},{4,26},{6,24},{8,22},{10,20},{12,18},{14,16},{16,14}... | collective-permute-start | bytes 393224 | tf_op jit(solution)/shard_map/ppermute | solution.py:364
  47.8 14.4 %collective-permute-start.36 = (bf16[8,64,128]{2,1,0:T(8,128)(2,1)S(1)}, bf16[8,64,128]{2,1,0:T(8,128)(2,1)S(1)}, u32[]{:S(2)}, u32[]{:S(2)}) collective-permute-start(bf16[8,64,128]{2,1,0:T(8,128)(2,1)S(1)} %get-tuple-element.108), channel_id=1, source_target_pairs={{0,6},{2,4},{4,2},{6,0},{8,14},{10,12},{12,10},{14,8},{16,22},{18,... | collective-permute-start | bytes 393224 | tf_op jit(solution)/shard_map/ppermute | solution.py:364
  47.8 15.7 %collective-permute-start.37 = (bf16[8,64,128]{2,1,0:T(8,128)(2,1)S(1)}, bf16[8,64,128]{2,1,0:T(8,128)(2,1)S(1)}, u32[]{:S(2)}, u32[]{:S(2)}) collective-permute-start(bf16[8,64,128]{2,1,0:T(8,128)(2,1)S(1)} %get-tuple-element.109), channel_id=1, source_target_pairs={{0,8},{2,10},{4,12},{6,14},{8,0},{10,2},{12,4},{14,6},{16,24},{18,... | collective-permute-start | bytes 393224 | tf_op jit(solution)/shard_map/ppermute | solution.py:364
  49.3 14.3 %collective-permute-start.38 = (bf16[8,64,128]{2,1,0:T(8,128)(2,1)S(1)}, bf16[8,64,128]{2,1,0:T(8,128)(2,1)S(1)}, u32[]{:S(2)}, u32[]{:S(2)}) collective-permute-start(bf16[8,64,128]{2,1,0:T(8,128)(2,1)S(1)} %get-tuple-element.110), channel_id=1, source_target_pairs={{0,10},{2,8},{4,14},{6,12},{8,2},{10,0},{12,6},{14,4},{16,26},{18,... | collective-permute-start | bytes 393224 | tf_op jit(solution)/shard_map/ppermute | solution.py:364
  55.3 8.2 %collective-permute-start.39 = (bf16[8,64,128]{2,1,0:T(8,128)(2,1)S(1)}, bf16[8,64,128]{2,1,0:T(8,128)(2,1)S(1)}, u32[]{:S(2)}, u32[]{:S(2)}) collective-permute-start(bf16[8,64,128]{2,1,0:T(8,128)(2,1)S(1)} %get-tuple-element.111), channel_id=1, source_target_pairs={{0,12},{2,14},{4,8},{6,10},{8,4},{10,6},{12,0},{14,2},{16,28},{18,... | collective-permute-start | bytes 393224 | tf_op jit(solution)/shard_map/ppermute | solution.py:364
  62.3 24.1 %collective-permute-start.50 = (bf16[8,8,64,128]{3,2,1,0:T(8,128)(2,1)S(1)}, bf16[8,8,64,128]{3,2,1,0:T(8,128)(2,1)S(1)}, u32[]{:S(2)}, u32[]{:S(2)}) collective-permute-start(bf16[8,8,64,128]{3,2,1,0:T(8,128)(2,1)S(1)} %shard_map.56.rest_1_), channel_id=1, source_target_pairs={{0,1},{1,0},{2,3},{3,2},{4,5},{5,4},{6,7},{7,6},{8,9},{9,8},{10,11... | collective-permute-start | bytes 3145736 | tf_op jit(solution)/shard_map/ppermute | solution.py:372
  65.9 43.1 %collective-permute-start.49 = (bf16[8,8,64,128]{3,2,1,0:T(8,128)(2,1)S(1)}, bf16[8,8,64,128]{3,2,1,0:T(8,128)(2,1)}, u32[]{:S(2)}, u32[]{:S(2)}) collective-permute-start(bf16[8,8,64,128]{3,2,1,0:T(8,128)(2,1)S(1)} %shard_map.55.rest_0_), channel_id=1, source_target_pairs={{0,1},{1,0},{2,3},{3,2},{4,5},{5,4},{6,7},{7,6},{8,9},{9,8},{10,11... | collective-permute-start | bytes 3145736 | tf_op jit(solution)/shard_map/ppermute | solution.py:372
  120.7 163.3 %all-to-all-start.2 = ((bf16[16,8,64,128]{3,2,1,0:T(8,128)(2,1)}), bf16[16,8,64,128]{3,2,1,0:T(8,128)(2,1)S(1)}, u32[]{:S(2)}, u32[]{:S(2)}) async-start(bf16[16,8,64,128]{3,2,1,0:T(8,128)(2,1)} %shard_map.57), calls=%async_computation.2 | async-start | bytes 4194304 | tf_op jit(solution)/shard_map/all_to_all | solution.py:376
  137.5 9.0 %collective-permute-start.1 = (bf16[8,64,128]{2,1,0:T(8,128)(2,1)S(1)}, bf16[8,64,128]{2,1,0:T(8,128)(2,1)S(1)}, u32[]{:S(2)}, u32[]{:S(2)}) collective-permute-start(bf16[8,64,128]{2,1,0:T(8,128)(2,1)S(1)} %get-tuple-element.75), channel_id=1, source_target_pairs={{0,4},{2,6},{4,0},{6,2},{8,12},{10,14},{12,8},{14,10},{16,20},{18,... | collective-permute-start | bytes 393224 | tf_op jit(solution)/shard_map/ppermute | solution.py:364
  139.1 55.1 %collective-permute-start.7 = (bf16[8,64,128]{2,1,0:T(8,128)(2,1)S(1)}, bf16[8,64,128]{2,1,0:T(8,128)(2,1)S(1)}, u32[]{:S(2)}, u32[]{:S(2)}) collective-permute-start(bf16[8,64,128]{2,1,0:T(8,128)(2,1)S(1)} %get-tuple-element.81), channel_id=1, source_target_pairs={{0,16},{2,18},{4,20},{6,22},{8,24},{10,26},{12,28},{14,30},{16,0},... | collective-permute-start | bytes 393224 | tf_op jit(solution)/shard_map/ppermute | solution.py:364
  141.2 56.6 %collective-permute-start.8 = (bf16[8,64,128]{2,1,0:T(8,128)(2,1)S(1)}, bf16[8,64,128]{2,1,0:T(8,128)(2,1)S(1)}, u32[]{:S(2)}, u32[]{:S(2)}) collective-permute-start(bf16[8,64,128]{2,1,0:T(8,128)(2,1)S(1)} %get-tuple-element.82), channel_id=1, source_target_pairs={{0,18},{2,16},{4,22},{6,20},{8,26},{10,24},{12,30},{14,28},{16,2},... | collective-permute-start | bytes 393224 | tf_op jit(solution)/shard_map/ppermute | solution.py:364
  142.1 64.3 %collective-permute-start.9 = (bf16[8,64,128]{2,1,0:T(8,128)(2,1)S(1)}, bf16[8,64,128]{2,1,0:T(8,128)(2,1)S(1)}, u32[]{:S(2)}, u32[]{:S(2)}) collective-permute-start(bf16[8,64,128]{2,1,0:T(8,128)(2,1)S(1)} %get-tuple-element.83), channel_id=1, source_target_pairs={{0,20},{2,22},{4,16},{6,18},{8,28},{10,30},{12,24},{14,26},{16,4},... | collective-permute-start | bytes 393224 | tf_op jit(solution)/shard_map/ppermute | solution.py:364
  144.2 65.9 %collective-permute-start.10 = (bf16[8,64,128]{2,1,0:T(8,128)(2,1)S(1)}, bf16[8,64,128]{2,1,0:T(8,128)(2,1)S(1)}, u32[]{:S(2)}, u32[]{:S(2)}) collective-permute-start(bf16[8,64,128]{2,1,0:T(8,128)(2,1)S(1)} %get-tuple-element.84), channel_id=1, source_target_pairs={{0,22},{2,20},{4,18},{6,16},{8,30},{10,28},{12,26},{14,24},{16,6},... | collective-permute-start | bytes 393224 | tf_op jit(solution)/shard_map/ppermute | solution.py:364
  146.5 63.5 %collective-permute-start.11 = (bf16[8,64,128]{2,1,0:T(8,128)(2,1)S(1)}, bf16[8,64,128]{2,1,0:T(8,128)(2,1)S(1)}, u32[]{:S(2)}, u32[]{:S(2)}) collective-permute-start(bf16[8,64,128]{2,1,0:T(8,128)(2,1)S(1)} %get-tuple-element.85), channel_id=1, source_target_pairs={{0,24},{2,26},{4,28},{6,30},{8,16},{10,18},{12,20},{14,22},{16,8},... | collective-permute-start | bytes 393224 | tf_op jit(solution)/shard_map/ppermute | solution.py:364
  194.2 19.9 %collective-permute-start.12 = (bf16[8,64,128]{2,1,0:T(8,128)(2,1)S(1)}, bf16[8,64,128]{2,1,0:T(8,128)(2,1)S(1)}, u32[]{:S(2)}, u32[]{:S(2)}) collective-permute-start(bf16[8,64,128]{2,1,0:T(8,128)(2,1)S(1)} %get-tuple-element.86), channel_id=1, source_target_pairs={{0,26},{2,24},{4,30},{6,28},{8,18},{10,16},{12,22},{14,20},{16,10}... | collective-permute-start | bytes 393224 | tf_op jit(solution)/shard_map/ppermute | solution.py:364
  197.9 19.4 %collective-permute-start.13 = (bf16[8,64,128]{2,1,0:T(8,128)(2,1)S(1)}, bf16[8,64,128]{2,1,0:T(8,128)(2,1)S(1)}, u32[]{:S(2)}, u32[]{:S(2)}) collective-permute-start(bf16[8,64,128]{2,1,0:T(8,128)(2,1)S(1)} %get-tuple-element.87), channel_id=1, source_target_pairs={{0,28},{2,30},{4,24},{6,26},{8,20},{10,22},{12,16},{14,18},{16,12}... | collective-permute-start | bytes 393224 | tf_op jit(solution)/shard_map/ppermute | solution.py:364
  206.4 14.3 %collective-permute-start.14 = (bf16[8,64,128]{2,1,0:T(8,128)(2,1)S(1)}, bf16[8,64,128]{2,1,0:T(8,128)(2,1)S(1)}, u32[]{:S(2)}, u32[]{:S(2)}) collective-permute-start(bf16[8,64,128]{2,1,0:T(8,128)(2,1)S(1)} %get-tuple-element.88), channel_id=1, source_target_pairs={{0,30},{2,28},{4,26},{6,24},{8,22},{10,20},{12,18},{14,16},{16,14}... | collective-permute-start | bytes 393224 | tf_op jit(solution)/shard_map/ppermute | solution.py:364
  210.0 15.1 %collective-permute-start.2 = (bf16[8,64,128]{2,1,0:T(8,128)(2,1)S(1)}, bf16[8,64,128]{2,1,0:T(8,128)(2,1)S(1)}, u32[]{:S(2)}, u32[]{:S(2)}) collective-permute-start(bf16[8,64,128]{2,1,0:T(8,128)(2,1)S(1)} %get-tuple-element.76), channel_id=1, source_target_pairs={{0,6},{2,4},{4,2},{6,0},{8,14},{10,12},{12,10},{14,8},{16,22},{18,... | collective-permute-start | bytes 393224 | tf_op jit(solution)/shard_map/ppermute | solution.py:364
  210.0 16.8 %collective-permute-start.3 = (bf16[8,64,128]{2,1,0:T(8,128)(2,1)S(1)}, bf16[8,64,128]{2,1,0:T(8,128)(2,1)S(1)}, u32[]{:S(2)}, u32[]{:S(2)}) collective-permute-start(bf16[8,64,128]{2,1,0:T(8,128)(2,1)S(1)} %get-tuple-element.77), channel_id=1, source_target_pairs={{0,8},{2,10},{4,12},{6,14},{8,0},{10,2},{12,4},{14,6},{16,24},{18,... | collective-permute-start | bytes 393224 | tf_op jit(solution)/shard_map/ppermute | solution.py:364
  214.1 12.7 %collective-permute-start.4 = (bf16[8,64,128]{2,1,0:T(8,128)(2,1)S(1)}, bf16[8,64,128]{2,1,0:T(8,128)(2,1)S(1)}, u32[]{:S(2)}, u32[]{:S(2)}) collective-permute-start(bf16[8,64,128]{2,1,0:T(8,128)(2,1)S(1)} %get-tuple-element.78), channel_id=1, source_target_pairs={{0,10},{2,8},{4,14},{6,12},{8,2},{10,0},{12,6},{14,4},{16,26},{18,... | collective-permute-start | bytes 393224 | tf_op jit(solution)/shard_map/ppermute | solution.py:364
  217.2 9.6 %collective-permute-start.5 = (bf16[8,64,128]{2,1,0:T(8,128)(2,1)S(1)}, bf16[8,64,128]{2,1,0:T(8,128)(2,1)S(1)}, u32[]{:S(2)}, u32[]{:S(2)}) collective-permute-start(bf16[8,64,128]{2,1,0:T(8,128)(2,1)S(1)} %get-tuple-element.79), channel_id=1, source_target_pairs={{0,12},{2,14},{4,8},{6,10},{8,4},{10,6},{12,0},{14,2},{16,28},{18,... | collective-permute-start | bytes 393224 | tf_op jit(solution)/shard_map/ppermute | solution.py:364
  225.2 24.6 %collective-permute-start.16 = (bf16[8,8,64,128]{3,2,1,0:T(8,128)(2,1)S(1)}, bf16[8,8,64,128]{3,2,1,0:T(8,128)(2,1)S(1)}, u32[]{:S(2)}, u32[]{:S(2)}) collective-permute-start(bf16[8,8,64,128]{3,2,1,0:T(8,128)(2,1)S(1)} %shard_map.48.rest_1_), channel_id=1, source_target_pairs={{0,1},{1,0},{2,3},{3,2},{4,5},{5,4},{6,7},{7,6},{8,9},{9,8},{10,11... | collective-permute-start | bytes 3145736 | tf_op jit(solution)/shard_map/ppermute | solution.py:372
  228.9 43.4 %collective-permute-start.15 = (bf16[8,8,64,128]{3,2,1,0:T(8,128)(2,1)S(1)}, bf16[8,8,64,128]{3,2,1,0:T(8,128)(2,1)S(1)}, u32[]{:S(2)}, u32[]{:S(2)}) collective-permute-start(bf16[8,8,64,128]{3,2,1,0:T(8,128)(2,1)S(1)} %shard_map.47.rest_0_), channel_id=1, source_target_pairs={{0,1},{1,0},{2,3},{3,2},{4,5},{5,4},{6,7},{7,6},{8,9},{9,8},{10,11... | collective-permute-start | bytes 3145736 | tf_op jit(solution)/shard_map/ppermute | solution.py:372
  285.3 161.2 %all-to-all-start = ((bf16[16,8,64,128]{3,2,1,0:T(8,128)(2,1)}), bf16[16,8,64,128]{3,2,1,0:T(8,128)(2,1)S(1)}, u32[]{:S(2)}, u32[]{:S(2)}) async-start(bf16[16,8,64,128]{3,2,1,0:T(8,128)(2,1)} %shard_map.49), calls=%async_computation | async-start | bytes 4194304 | tf_op jit(solution)/shard_map/all_to_all | solution.py:376
  305.7 8.6 %collective-permute-start.52 = (bf16[8,64,128]{2,1,0:T(8,128)(2,1)S(1)}, bf16[8,64,128]{2,1,0:T(8,128)(2,1)S(1)}, u32[]{:S(2)}, u32[]{:S(2)}) collective-permute-start(bf16[8,64,128]{2,1,0:T(8,128)(2,1)S(1)} %get-tuple-element.123), channel_id=1, source_target_pairs={{0,4},{2,6},{4,0},{6,2},{8,12},{10,14},{12,8},{14,10},{16,20},{18,... | collective-permute-start | bytes 393224 | tf_op jit(solution)/shard_map/ppermute | solution.py:364
  307.4 49.1 %collective-permute-start.58 = (bf16[8,64,128]{2,1,0:T(8,128)(2,1)S(1)}, bf16[8,64,128]{2,1,0:T(8,128)(2,1)S(1)}, u32[]{:S(2)}, u32[]{:S(2)}) collective-permute-start(bf16[8,64,128]{2,1,0:T(8,128)(2,1)S(1)} %get-tuple-element.129), channel_id=1, source_target_pairs={{0,16},{2,18},{4,20},{6,22},{8,24},{10,26},{12,28},{14,30},{16,0},... | collective-permute-start | bytes 393224 | tf_op jit(solution)/shard_map/ppermute | solution.py:364
  309.4 50.7 %collective-permute-start.59 = (bf16[8,64,128]{2,1,0:T(8,128)(2,1)S(1)}, bf16[8,64,128]{2,1,0:T(8,128)(2,1)S(1)}, u32[]{:S(2)}, u32[]{:S(2)}) collective-permute-start(bf16[8,64,128]{2,1,0:T(8,128)(2,1)S(1)} %get-tuple-element.130), channel_id=1, source_target_pairs={{0,18},{2,16},{4,22},{6,20},{8,26},{10,24},{12,30},{14,28},{16,2},... | collective-permute-start | bytes 393224 | tf_op jit(solution)/shard_map/ppermute | solution.py:364
  310.3 58.4 %collective-permute-start.60 = (bf16[8,64,128]{2,1,0:T(8,128)(2,1)S(1)}, bf16[8,64,128]{2,1,0:T(8,128)(2,1)S(1)}, u32[]{:S(2)}, u32[]{:S(2)}) collective-permute-start(bf16[8,64,128]{2,1,0:T(8,128)(2,1)S(1)} %get-tuple-element.131), channel_id=1, source_target_pairs={{0,20},{2,22},{4,16},{6,18},{8,28},{10,30},{12,24},{14,26},{16,4},... | collective-permute-start | bytes 393224 | tf_op jit(solution)/shard_map/ppermute | solution.py:364
  312.4 59.9 %collective-permute-start.61 = (bf16[8,64,128]{2,1,0:T(8,128)(2,1)S(1)}, bf16[8,64,128]{2,1,0:T(8,128)(2,1)S(1)}, u32[]{:S(2)}, u32[]{:S(2)}) collective-permute-start(bf16[8,64,128]{2,1,0:T(8,128)(2,1)S(1)} %get-tuple-element.132), channel_id=1, source_target_pairs={{0,22},{2,20},{4,18},{6,16},{8,30},{10,28},{12,26},{14,24},{16,6},... | collective-permute-start | bytes 393224 | tf_op jit(solution)/shard_map/ppermute | solution.py:364
  314.4 58.0 %collective-permute-start.62 = (bf16[8,64,128]{2,1,0:T(8,128)(2,1)S(1)}, bf16[8,64,128]{2,1,0:T(8,128)(2,1)S(1)}, u32[]{:S(2)}, u32[]{:S(2)}) collective-permute-start(bf16[8,64,128]{2,1,0:T(8,128)(2,1)S(1)} %get-tuple-element.133), channel_id=1, source_target_pairs={{0,24},{2,26},{4,28},{6,30},{8,16},{10,18},{12,20},{14,22},{16,8},... | collective-permute-start | bytes 393224 | tf_op jit(solution)/shard_map/ppermute | solution.py:364
  356.5 19.9 %collective-permute-start.63 = (bf16[8,64,128]{2,1,0:T(8,128)(2,1)S(1)}, bf16[8,64,128]{2,1,0:T(8,128)(2,1)S(1)}, u32[]{:S(2)}, u32[]{:S(2)}) collective-permute-start(bf16[8,64,128]{2,1,0:T(8,128)(2,1)S(1)} %get-tuple-element.134), channel_id=1, source_target_pairs={{0,26},{2,24},{4,30},{6,28},{8,18},{10,16},{12,22},{14,20},{16,10}... | collective-permute-start | bytes 393224 | tf_op jit(solution)/shard_map/ppermute | solution.py:364
  360.1 19.4 %collective-permute-start.64 = (bf16[8,64,128]{2,1,0:T(8,128)(2,1)S(1)}, bf16[8,64,128]{2,1,0:T(8,128)(2,1)S(1)}, u32[]{:S(2)}, u32[]{:S(2)}) collective-permute-start(bf16[8,64,128]{2,1,0:T(8,128)(2,1)S(1)} %get-tuple-element.135), channel_id=1, source_target_pairs={{0,28},{2,30},{4,24},{6,26},{8,20},{10,22},{12,16},{14,18},{16,12}... | collective-permute-start | bytes 393224 | tf_op jit(solution)/shard_map/ppermute | solution.py:364
  368.6 14.3 %collective-permute-start.65 = (bf16[8,64,128]{2,1,0:T(8,128)(2,1)S(1)}, bf16[8,64,128]{2,1,0:T(8,128)(2,1)S(1)}, u32[]{:S(2)}, u32[]{:S(2)}) collective-permute-start(bf16[8,64,128]{2,1,0:T(8,128)(2,1)S(1)} %get-tuple-element.136), channel_id=1, source_target_pairs={{0,30},{2,28},{4,26},{6,24},{8,22},{10,20},{12,18},{14,16},{16,14}... | collective-permute-start | bytes 393224 | tf_op jit(solution)/shard_map/ppermute | solution.py:364
  372.3 15.1 %collective-permute-start.53 = (bf16[8,64,128]{2,1,0:T(8,128)(2,1)S(1)}, bf16[8,64,128]{2,1,0:T(8,128)(2,1)S(1)}, u32[]{:S(2)}, u32[]{:S(2)}) collective-permute-start(bf16[8,64,128]{2,1,0:T(8,128)(2,1)S(1)} %get-tuple-element.124), channel_id=1, source_target_pairs={{0,6},{2,4},{4,2},{6,0},{8,14},{10,12},{12,10},{14,8},{16,22},{18,... | collective-permute-start | bytes 393224 | tf_op jit(solution)/shard_map/ppermute | solution.py:364
  372.3 16.9 %collective-permute-start.54 = (bf16[8,64,128]{2,1,0:T(8,128)(2,1)S(1)}, bf16[8,64,128]{2,1,0:T(8,128)(2,1)S(1)}, u32[]{:S(2)}, u32[]{:S(2)}) collective-permute-start(bf16[8,64,128]{2,1,0:T(8,128)(2,1)S(1)} %get-tuple-element.125), channel_id=1, source_target_pairs={{0,8},{2,10},{4,12},{6,14},{8,0},{10,2},{12,4},{14,6},{16,24},{18,... | collective-permute-start | bytes 393224 | tf_op jit(solution)/shard_map/ppermute | solution.py:364
  376.4 12.8 %collective-permute-start.55 = (bf16[8,64,128]{2,1,0:T(8,128)(2,1)S(1)}, bf16[8,64,128]{2,1,0:T(8,128)(2,1)S(1)}, u32[]{:S(2)}, u32[]{:S(2)}) collective-permute-start(bf16[8,64,128]{2,1,0:T(8,128)(2,1)S(1)} %get-tuple-element.126), channel_id=1, source_target_pairs={{0,10},{2,8},{4,14},{6,12},{8,2},{10,0},{12,6},{14,4},{16,26},{18,... | collective-permute-start | bytes 393224 | tf_op jit(solution)/shard_map/ppermute | solution.py:364
  379.5 9.7 %collective-permute-start.56 = (bf16[8,64,128]{2,1,0:T(8,128)(2,1)S(1)}, bf16[8,64,128]{2,1,0:T(8,128)(2,1)S(1)}, u32[]{:S(2)}, u32[]{:S(2)}) collective-permute-start(bf16[8,64,128]{2,1,0:T(8,128)(2,1)S(1)} %get-tuple-element.127), channel_id=1, source_target_pairs={{0,12},{2,14},{4,8},{6,10},{8,4},{10,6},{12,0},{14,2},{16,28},{18,... | collective-permute-start | bytes 393224 | tf_op jit(solution)/shard_map/ppermute | solution.py:364
  387.4 24.9 %collective-permute-start.67 = (bf16[8,8,64,128]{3,2,1,0:T(8,128)(2,1)S(1)}, bf16[8,8,64,128]{3,2,1,0:T(8,128)(2,1)S(1)}, u32[]{:S(2)}, u32[]{:S(2)}) collective-permute-start(bf16[8,8,64,128]{3,2,1,0:T(8,128)(2,1)S(1)} %shard_map.60.rest_1_), channel_id=1, source_target_pairs={{0,1},{1,0},{2,3},{3,2},{4,5},{5,4},{6,7},{7,6},{8,9},{9,8},{10,11... | collective-permute-start | bytes 3145736 | tf_op jit(solution)/shard_map/ppermute | solution.py:372
  391.2 43.6 %collective-permute-start.66 = (bf16[8,8,64,128]{3,2,1,0:T(8,128)(2,1)S(1)}, bf16[8,8,64,128]{3,2,1,0:T(8,128)(2,1)S(1)}, u32[]{:S(2)}, u32[]{:S(2)}) collective-permute-start(bf16[8,8,64,128]{3,2,1,0:T(8,128)(2,1)S(1)} %shard_map.59.rest_0_), channel_id=1, source_target_pairs={{0,1},{1,0},{2,3},{3,2},{4,5},{5,4},{6,7},{7,6},{8,9},{9,8},{10,11... | collective-permute-start | bytes 3145736 | tf_op jit(solution)/shard_map/ppermute | solution.py:372
  447.8 161.3 %all-to-all-start.3 = ((bf16[16,8,64,128]{3,2,1,0:T(8,128)(2,1)}), bf16[16,8,64,128]{3,2,1,0:T(8,128)(2,1)S(1)}, u32[]{:S(2)}, u32[]{:S(2)}) async-start(bf16[16,8,64,128]{3,2,1,0:T(8,128)(2,1)} %copy-done), calls=%async_computation.3 | async-start | bytes 4194304 | tf_op jit(solution)/shard_map/all_to_all | solution.py:376
  468.0 8.5 %collective-permute-start.18 = (bf16[8,64,128]{2,1,0:T(8,128)(2,1)S(1)}, bf16[8,64,128]{2,1,0:T(8,128)(2,1)S(1)}, u32[]{:S(2)}, u32[]{:S(2)}) collective-permute-start(bf16[8,64,128]{2,1,0:T(8,128)(2,1)S(1)} %get-tuple-element.91), channel_id=1, source_target_pairs={{0,4},{2,6},{4,0},{6,2},{8,12},{10,14},{12,8},{14,10},{16,20},{18,... | collective-permute-start | bytes 393224 | tf_op jit(solution)/shard_map/ppermute | solution.py:364
  469.6 49.3 %collective-permute-start.24 = (bf16[8,64,128]{2,1,0:T(8,128)(2,1)S(1)}, bf16[8,64,128]{2,1,0:T(8,128)(2,1)S(1)}, u32[]{:S(2)}, u32[]{:S(2)}) collective-permute-start(bf16[8,64,128]{2,1,0:T(8,128)(2,1)S(1)} %get-tuple-element.97), channel_id=1, source_target_pairs={{0,16},{2,18},{4,20},{6,22},{8,24},{10,26},{12,28},{14,30},{16,0},... | collective-permute-start | bytes 393224 | tf_op jit(solution)/shard_map/ppermute | solution.py:364
  471.7 50.8 %collective-permute-start.25 = (bf16[8,64,128]{2,1,0:T(8,128)(2,1)S(1)}, bf16[8,64,128]{2,1,0:T(8,128)(2,1)S(1)}, u32[]{:S(2)}, u32[]{:S(2)}) collective-permute-start(bf16[8,64,128]{2,1,0:T(8,128)(2,1)S(1)} %get-tuple-element.98), channel_id=1, source_target_pairs={{0,18},{2,16},{4,22},{6,20},{8,26},{10,24},{12,30},{14,28},{16,2},... | collective-permute-start | bytes 393224 | tf_op jit(solution)/shard_map/ppermute | solution.py:364
  472.5 58.5 %collective-permute-start.26 = (bf16[8,64,128]{2,1,0:T(8,128)(2,1)S(1)}, bf16[8,64,128]{2,1,0:T(8,128)(2,1)S(1)}, u32[]{:S(2)}, u32[]{:S(2)}) collective-permute-start(bf16[8,64,128]{2,1,0:T(8,128)(2,1)S(1)} %get-tuple-element.99), channel_id=1, source_target_pairs={{0,20},{2,22},{4,16},{6,18},{8,28},{10,30},{12,24},{14,26},{16,4},... | collective-permute-start | bytes 393224 | tf_op jit(solution)/shard_map/ppermute | solution.py:364
  474.6 60.1 %collective-permute-start.27 = (bf16[8,64,128]{2,1,0:T(8,128)(2,1)S(1)}, bf16[8,64,128]{2,1,0:T(8,128)(2,1)S(1)}, u32[]{:S(2)}, u32[]{:S(2)}) collective-permute-start(bf16[8,64,128]{2,1,0:T(8,128)(2,1)S(1)} %get-tuple-element.100), channel_id=1, source_target_pairs={{0,22},{2,20},{4,18},{6,16},{8,30},{10,28},{12,26},{14,24},{16,6},... | collective-permute-start | bytes 393224 | tf_op jit(solution)/shard_map/ppermute | solution.py:364
  476.4 58.3 %collective-permute-start.28 = (bf16[8,64,128]{2,1,0:T(8,128)(2,1)S(1)}, bf16[8,64,128]{2,1,0:T(8,128)(2,1)S(1)}, u32[]{:S(2)}, u32[]{:S(2)}) collective-permute-start(bf16[8,64,128]{2,1,0:T(8,128)(2,1)S(1)} %get-tuple-element.101), channel_id=1, source_target_pairs={{0,24},{2,26},{4,28},{6,30},{8,16},{10,18},{12,20},{14,22},{16,8},... | collective-permute-start | bytes 393224 | tf_op jit(solution)/shard_map/ppermute | solution.py:364
  518.8 19.9 %collective-permute-start.29 = (bf16[8,64,128]{2,1,0:T(8,128)(2,1)S(1)}, bf16[8,64,128]{2,1,0:T(8,128)(2,1)S(1)}, u32[]{:S(2)}, u32[]{:S(2)}) collective-permute-start(bf16[8,64,128]{2,1,0:T(8,128)(2,1)S(1)} %get-tuple-element.102), channel_id=1, source_target_pairs={{0,26},{2,24},{4,30},{6,28},{8,18},{10,16},{12,22},{14,20},{16,10}... | collective-permute-start | bytes 393224 | tf_op jit(solution)/shard_map/ppermute | solution.py:364
  522.5 19.4 %collective-permute-start.30 = (bf16[8,64,128]{2,1,0:T(8,128)(2,1)S(1)}, bf16[8,64,128]{2,1,0:T(8,128)(2,1)S(1)}, u32[]{:S(2)}, u32[]{:S(2)}) collective-permute-start(bf16[8,64,128]{2,1,0:T(8,128)(2,1)S(1)} %get-tuple-element.103), channel_id=1, source_target_pairs={{0,28},{2,30},{4,24},{6,26},{8,20},{10,22},{12,16},{14,18},{16,12}... | collective-permute-start | bytes 393224 | tf_op jit(solution)/shard_map/ppermute | solution.py:364
  531.0 14.3 %collective-permute-start.31 = (bf16[8,64,128]{2,1,0:T(8,128)(2,1)S(1)}, bf16[8,64,128]{2,1,0:T(8,128)(2,1)S(1)}, u32[]{:S(2)}, u32[]{:S(2)}) collective-permute-start(bf16[8,64,128]{2,1,0:T(8,128)(2,1)S(1)} %get-tuple-element.104), channel_id=1, source_target_pairs={{0,30},{2,28},{4,26},{6,24},{8,22},{10,20},{12,18},{14,16},{16,14}... | collective-permute-start | bytes 393224 | tf_op jit(solution)/shard_map/ppermute | solution.py:364
  534.7 15.1 %collective-permute-start.19 = (bf16[8,64,128]{2,1,0:T(8,128)(2,1)S(1)}, bf16[8,64,128]{2,1,0:T(8,128)(2,1)S(1)}, u32[]{:S(2)}, u32[]{:S(2)}) collective-permute-start(bf16[8,64,128]{2,1,0:T(8,128)(2,1)S(1)} %get-tuple-element.92), channel_id=1, source_target_pairs={{0,6},{2,4},{4,2},{6,0},{8,14},{10,12},{12,10},{14,8},{16,22},{18,... | collective-permute-start | bytes 393224 | tf_op jit(solution)/shard_map/ppermute | solution.py:364
  534.7 16.9 %collective-permute-start.20 = (bf16[8,64,128]{2,1,0:T(8,128)(2,1)S(1)}, bf16[8,64,128]{2,1,0:T(8,128)(2,1)S(1)}, u32[]{:S(2)}, u32[]{:S(2)}) collective-permute-start(bf16[8,64,128]{2,1,0:T(8,128)(2,1)S(1)} %get-tuple-element.93), channel_id=1, source_target_pairs={{0,8},{2,10},{4,12},{6,14},{8,0},{10,2},{12,4},{14,6},{16,24},{18,... | collective-permute-start | bytes 393224 | tf_op jit(solution)/shard_map/ppermute | solution.py:364
  538.8 12.8 %collective-permute-start.21 = (bf16[8,64,128]{2,1,0:T(8,128)(2,1)S(1)}, bf16[8,64,128]{2,1,0:T(8,128)(2,1)S(1)}, u32[]{:S(2)}, u32[]{:S(2)}) collective-permute-start(bf16[8,64,128]{2,1,0:T(8,128)(2,1)S(1)} %get-tuple-element.94), channel_id=1, source_target_pairs={{0,10},{2,8},{4,14},{6,12},{8,2},{10,0},{12,6},{14,4},{16,26},{18,... | collective-permute-start | bytes 393224 | tf_op jit(solution)/shard_map/ppermute | solution.py:364
  541.9 9.7 %collective-permute-start.22 = (bf16[8,64,128]{2,1,0:T(8,128)(2,1)S(1)}, bf16[8,64,128]{2,1,0:T(8,128)(2,1)S(1)}, u32[]{:S(2)}, u32[]{:S(2)}) collective-permute-start(bf16[8,64,128]{2,1,0:T(8,128)(2,1)S(1)} %get-tuple-element.95), channel_id=1, source_target_pairs={{0,12},{2,14},{4,8},{6,10},{8,4},{10,6},{12,0},{14,2},{16,28},{18,... | collective-permute-start | bytes 393224 | tf_op jit(solution)/shard_map/ppermute | solution.py:364
  549.8 24.9 %collective-permute-start.33 = (bf16[8,8,64,128]{3,2,1,0:T(8,128)(2,1)S(1)}, bf16[8,8,64,128]{3,2,1,0:T(8,128)(2,1)S(1)}, u32[]{:S(2)}, u32[]{:S(2)}) collective-permute-start(bf16[8,8,64,128]{3,2,1,0:T(8,128)(2,1)S(1)} %shard_map.52.rest_1_), channel_id=1, source_target_pairs={{0,1},{1,0},{2,3},{3,2},{4,5},{5,4},{6,7},{7,6},{8,9},{9,8},{10,11... | collective-permute-start | bytes 3145736 | tf_op jit(solution)/shard_map/ppermute | solution.py:372
  553.6 43.6 %collective-permute-start.32 = (bf16[8,8,64,128]{3,2,1,0:T(8,128)(2,1)S(1)}, bf16[8,8,64,128]{3,2,1,0:T(8,128)(2,1)S(1)}, u32[]{:S(2)}, u32[]{:S(2)}) collective-permute-start(bf16[8,8,64,128]{3,2,1,0:T(8,128)(2,1)S(1)} %shard_map.51.rest_0_), channel_id=1, source_target_pairs={{0,1},{1,0},{2,3},{3,2},{4,5},{5,4},{6,7},{7,6},{8,9},{9,8},{10,11... | collective-permute-start | bytes 3145736 | tf_op jit(solution)/shard_map/ppermute | solution.py:372
  609.2 47.8 %all-to-all-start.1 = ((bf16[16,8,64,128]{3,2,1,0:T(8,128)(2,1)}), bf16[16,8,64,128]{3,2,1,0:T(8,128)(2,1)}, u32[]{:S(2)}, u32[]{:S(2)}) async-start(bf16[16,8,64,128]{3,2,1,0:T(8,128)(2,1)} %copy-done.1), calls=%async_computation.1 | async-start | bytes 4194304 | tf_op jit(solution)/shard_map/all_to_all | solution.py:376
  (14 other events, 77.9 us)

commit v4 on v3

--- a/solution.py
+++ b/solution.py
@@ -20,6 +20,7 @@
 SLOTS = 3
 BATCH = 16
 REACHES = 2
+MERGED = (0,)
 F32 = jnp.float32
 BF16 = jnp.bfloat16
 VMEM_LIMIT = 24 * 1024 * 1024
@@ -104,11 +105,18 @@
         out_ref[...] = rows.reshape(out_ref.shape).astype(BF16)
 
 
-def load_in(rows_ref, bands_ref):
-    rows_ref[...] = bands_ref[...].astype(F32).reshape(NF * GROUP, LANES)
-
-
-def first_kernel(mine_ref, direct_ref, tables_ref, *rest, half):
+def load_in(rows_ref, bands_refs, mine):
+    if len(bands_refs) == 1:
+        rows_ref[...] = bands_refs[0][...].astype(F32).reshape(NF * GROUP, LANES)
+        return
+    size = NF // len(bands_refs) * GROUP
+    for shift, bands_ref in enumerate(bands_refs):
+        owner = lax.bitwise_xor(mine, shift)
+        rows = bands_ref[...].astype(F32).reshape(size, LANES)
+        rows_ref[pl.ds(pl.multiple_of(owner * size, size), size), :] = rows
+
+
+def first_kernel(mine_ref, direct_ref, tables_ref, *rest, half, sources):
     out_refs, rows_ref = rest[:-1], rest[-1]
     for first in range(0, GROUP, QUAD):
         series = direct_ref[first : first + QUAD].reshape(QUAD * half, NT)
@@ -116,9 +124,9 @@
     store_out(out_refs, rows_ref, mine_ref[0])
 
 
-def middle_kernel(mine_ref, direct_ref, tables_ref, onsets_ref, bands_ref, *rest, half):
-    out_refs, (in_rows, rows_ref) = rest[:-2], rest[-2:]
-    load_in(in_rows, bands_ref)
+def middle_kernel(mine_ref, direct_ref, tables_ref, onsets_ref, *rest, half, sources):
+    bands_refs, out_refs, (in_rows, rows_ref) = rest[:sources], rest[sources:-2], rest[-2:]
+    load_in(in_rows, bands_refs, mine_ref[0])
     for first in range(0, GROUP, QUAD):
         traces = to_traces(in_rows, tables_ref, half, first)
         series = subtracted(direct_ref, traces, onsets_ref, half, first)
@@ -126,9 +134,9 @@
     store_out(out_refs, rows_ref, mine_ref[0])
 
 
-def last_kernel(mine_ref, direct_ref, tables_ref, onsets_ref, bands_ref, *rest, half):
-    out_ref, in_rows = rest[-2:]
-    load_in(in_rows, bands_ref)
+def last_kernel(mine_ref, direct_ref, tables_ref, onsets_ref, *rest, half, sources):
+    bands_refs, (out_ref, in_rows) = rest[:sources], rest[-2:]
+    load_in(in_rows, bands_refs, mine_ref[0])
     for first in range(0, GROUP, QUAD):
         traces = to_traces(in_rows, tables_ref, half, first)
         series = subtracted(direct_ref, traces, onsets_ref, half, first)
@@ -143,9 +151,12 @@
     rows_spec = pl.BlockSpec((owners, freqs, GROUP, LANES), lambda g: (0, 0, g, 0))
     operands = [mine, direct, tables]
     specs = [pl.BlockSpec(memory_space=pltpu.SMEM), series_spec, pl.BlockSpec((2, 2 * NF, NT // 2), lambda g: (0, 0, 0))]
+    block_spec = pl.BlockSpec((freqs, GROUP, LANES), lambda g: (0, g, 0))
+    bands = bands or []
     if kind != "first":
-        operands += [onsets, bands]
-        specs += [pl.BlockSpec((1, half, GROUP), lambda g: (g, chunk, 0)), rows_spec]
+        operands += [onsets, *bands]
+        specs.append(pl.BlockSpec((1, half, GROUP), lambda g: (g, chunk, 0)))
+        specs += [rows_spec] if len(bands) == 1 else [block_spec] * owners
     aliases = {}
     if out is not None:
         aliases = {len(operands): 0}
@@ -155,7 +166,7 @@
     if kind == "last":
         out_specs, out_shape = series_spec, jax.ShapeDtypeStruct(direct.shape, F32)
     else:
-        out_specs = [pl.BlockSpec((freqs, GROUP, LANES), lambda g: (0, g, 0))] * owners
+        out_specs = [block_spec] * owners
         out_shape = [jax.ShapeDtypeStruct((freqs, receivers, LANES), BF16)] * owners
     body, passes, scratches = {
         "first": (first_kernel, 3, 1),
@@ -164,7 +175,7 @@
     }[kind]
     elements = receivers * half * NT
     return pl.pallas_call(
-        functools.partial(body, half=half),
+        functools.partial(body, half=half, sources=len(bands)),
         grid=(receivers // GROUP,),
         in_specs=specs,
         out_specs=out_specs,
@@ -211,10 +222,12 @@
     )(tile_mask)
 
 
-def product_kernel(tiles_ref, count_ref, place_ref, kernel_ref, *rest, parts):
-    field_refs, (out_ref, fields, sums, slots, slot_sems, field_sems) = rest[:-6], rest[-6:]
+def product_kernel(tiles_ref, count_ref, place_ref, kernel_ref, *rest, parts, sources):
+    field_refs, out_refs, scratch = rest[:sources], rest[sources:-6], rest[-6:]
+    bands_ref, fields, sums, slots, slot_sems, field_sems = scratch
+    out_ref = out_refs[0] if len(out_refs) == 1 else bands_ref
     _, _, rows, columns = kernel_ref.shape
-    _, freqs, depth, lanes = out_ref.shape
+    _, _, freqs, depth, lanes = fields.shape
     row_tiles, column_tiles = rows // TILE, columns // TILE
     lines = row_tiles * freqs
     per_tile = TILE // depth
@@ -293,20 +306,26 @@
         return 0
 
     lax.fori_loop(0, lines, finish, 0)
-
-
-def product_call(tiles, count, places, kernel, fields, parts):
+    if len(out_refs) > 1:
+        for shift, block_ref in enumerate(out_refs):
+            block_ref[...] = bands_ref[lax.bitwise_xor(mine, shift)]
+
+
+def product_call(chunk, tiles, count, places, kernel, fields, parts):
     owners = sum(field.shape[0] for field in fields) // parts
     _, freqs, depth, lanes = fields[0].shape
     lines = kernel.shape[2] // TILE * freqs
     smem = pl.BlockSpec(memory_space=pltpu.SMEM)
     anywhere = pl.BlockSpec(memory_space=pl.ANY)
     return pl.pallas_call(
-        functools.partial(product_kernel, parts=parts),
+        functools.partial(product_kernel, parts=parts, sources=len(fields)),
         in_specs=[smem, smem, smem, anywhere] + [anywhere] * len(fields),
-        out_specs=pl.BlockSpec(memory_space=pltpu.VMEM),
-        out_shape=jax.ShapeDtypeStruct((owners, freqs, depth, lanes), BF16),
+        out_specs=[pl.BlockSpec(memory_space=pltpu.VMEM)] * (1 if chunk in MERGED else owners),
+        out_shape=[jax.ShapeDtypeStruct((owners, freqs, depth, lanes), BF16)]
+        if chunk in MERGED
+        else [jax.ShapeDtypeStruct((freqs, depth, lanes), BF16)] * owners,
         scratch_shapes=[
+            pltpu.VMEM((8, 128) if chunk in MERGED else (owners, freqs, depth, lanes), BF16),
             pltpu.VMEM((parts, owners, freqs, depth, lanes), BF16),
             pltpu.VMEM((lines + 1, TILE, lanes), F32),
             pltpu.VMEM((SLOTS, BATCH, 2, TILE, TILE), BF16),
@@ -357,11 +376,15 @@
     def time_at(kind, chunk, *operands):
         return time_call(kind, chunk, owners, mine, direct, tables, *operands)
 
-    def spread(blocks):
+    def permuted(blocks):
         got = list(blocks)
         for shift in range(1, owners):
             pairs = [(place, place ^ shift) for place in range(owners)]
             got[shift] = lax.ppermute(blocks[shift], "freq", pairs)
+        return got
+
+    def spread(blocks):
+        got = permuted(blocks)
         size = owners // REACHES
         fields = [[] for _ in range(halves)]
         for reach in range(REACHES):
@@ -372,8 +395,10 @@
                 fields[shift].append(lax.ppermute(mine, "rows", ring))
         return [field for of_shift in fields for field in of_shift]
 
-    def gather(bands):
-        return lax.all_to_all(bands, "freq", 0, 0, tiled=True)
+    def gather(bands, chunk):
+        if chunk in MERGED:
+            return [lax.all_to_all(bands[0], "freq", 0, 0, tiled=True)]
+        return permuted(bands)
 
     blocks = [time_at("first", chunk) for chunk in range(CHUNKS)]
     out = None
@@ -381,8 +406,8 @@
         bands = [None] * CHUNKS
         for chunk in range(CHUNKS):
             fields = spread(blocks[chunk])
-            bands[chunk] = product_call(tiles, count, places, kernel, fields, halves)
-        bands = [gather(bands[chunk]) for chunk in range(CHUNKS)]
+            bands[chunk] = product_call(chunk, tiles, count, places, kernel, fields, halves)
+        bands = [gather(bands[chunk], chunk) for chunk in range(CHUNKS)]
         for chunk in range(CHUNKS):
             if turn + 1 < ITERS:
                 blocks[chunk] = time_at("middle", chunk, onsets, bands[chunk])

time: 674 us -> 645 us (0.957)
  waiting for transfers between devices: 360 us -> 276 us
  starting transfers between devices: 176 us -> 228 us
    ppermute x60 -> x90, starting transfers between devices: 136 us -> 203 us  [permuted(): got[shift] = lax.ppermute(blocks[shift], 'freq', pairs)]
    ppermute x60 -> x90, waiting for transfers between devices: 166 us -> 112 us  [permuted(): got[shift] = lax.ppermute(blocks[shift], 'freq', pairs)]
    ppermute x8, waiting for transfers between devices: 162 us -> 123 us  [spread(): fields[shift].append(lax.ppermute(mine, 'rows', ring))]
    all_to_all x4 -> x2, starting transfers between devices: 26.7 us -> 15.2 us  [gather(): return [lax.all_to_all(bands[0], 'freq', 0, 0, tiled=True)]]
    all_to_all x4 -> x2, waiting for transfers between devices: 31.9 us -> 41.4 us  [gather(): return [lax.all_to_all(bands[0], 'freq', 0, 0, tiled=True)]]
  transfers between devices with their start and end apart: 72 -> 100, of which waited for: 30 -> 35; matrix products, arithmetic and copies ran while one was open for 0% -> 0% of each run, Pallas kernels for 14% -> 13%
where the time goes in v4:
time: 645 us; the launch traced here: 640 us
  waiting for transfers between devices  276 us (43%)
  starting transfers between devices  228 us (35%)
  Pallas kernels  126 us (20%)
  local copies, waits for them, and re-layouts  9.16 us (1%)
    ppermute x90, starting transfers between devices, permuted(): got[shift] = lax.ppermute(blocks[shift], 'freq', pairs)  203 us
    ppermute x8, waiting for transfers between devices, spread(): fields[shift].append(lax.ppermute(mine, 'rows', ring))  123 us
    ppermute x90, waiting for transfers between devices, permuted(): got[shift] = lax.ppermute(blocks[shift], 'freq', pairs)  112 us
    pallas_call x6, Pallas kernels, time_call(): pl.pallas_call(functools.partial(body, half=half, sources=len(bands)), gr...  65.2 us
    pallas_call x4, Pallas kernels, product_call(): pl.pallas_call(functools.partial(product_kernel, parts=parts, sources=len...  44 us
    all_to_all x2, waiting for transfers between devices, gather(): return [lax.all_to_all(bands[0], 'freq', 0, 0, tiled=True)]  41.4 us
    all_to_all x2, starting transfers between devices, gather(): return [lax.all_to_all(bands[0], 'freq', 0, 0, tiled=True)]  15.2 us
  transfers between devices with their start and end apart: 100, of which 35 were waited for; matrix products, arithmetic and copies ran while one was open for 0% of the time, Pallas kernels for 13%

profile of v4, /device:TPU:1, one launch (start us, length us, event | category | flops | bytes accessed | tf_op | source)
XLA Modules:
  0.0 639.5 jit_solution(10196047896168717545)
XLA Ops:
  0.7 8.2 %shard_map.54 = (bf16[8,64,128]{2,1,0:T(8,128)(2,1)S(1)}, bf16[8,64,128]{2,1,0:T(8,128)(2,1)S(1)}, bf16[8,64,128]{2,1,0:T(8,128)(2,1)S(1)}, bf16[8,64,128]{2,1,0...) custom-call(s32[1]{0:T(128)} %bitcast.mine_ref, ...), custom_call_target="tpu_custom_call" | custom-call | flops 3221225472 | bytes 16777216 | tf_op jit(solution)/shard_map/pallas_call | solution.py:177
  18.1 3.1 collective-permute-start.75
  21.3 10.1 %collective-permute-done.71.refs_0_ = bf16[8,64,128]{2,1,0:T(8,128)(2,1)S(1)} collective-permute-done((bf16[8,64,128]{2,1,0:T(8,128)(2,1)S(1)}, bf16[8,64,128]{2,1,0:T(8,128)(2,1)S(1)}, u32[]{:S(2)}, u32[]{:S(2)}) %collective-permute-start.71) | collective-permute-done | bytes 131104 | tf_op jit(solution)/shard_map/ppermute | solution.py:383
  31.4 4.4 collective-permute-start.76
  38.1 9.8 %collective-permute-start.78 = (bf16[8,64,128]{2,1,0:T(8,128)(2,1)S(1)}, bf16[8,64,128]{2,1,0:T(8,128)(2,1)S(1)}, u32[]{:S(2)}, u32[]{:S(2)}) collective-permute-start(bf16[8,64,128]{2,1,0:T(8,128)(2,1)S(1)} %get-tuple-element.184), channel_id=1, source_target_pairs={{0,30},{2,28},{4,26},{6,24},{8,22},{10,20},{12,18},{14,16},{16,14}... | collective-permute-start | bytes 393224 | tf_op jit(solution)/shard_map/ppermute | solution.py:383
  49.4 6.0 collective-permute-start.68
  57.9 3.1 collective-permute-start.70
  67.3 4.8 list_tiles.1
  72.2 14.3 %collective-permute-done.80.rest_3_ = bf16[8,8,64,128]{3,2,1,0:T(8,128)(2,1)S(1)} collective-permute-done((bf16[8,8,64,128]{3,2,1,0:T(8,128)(2,1)S(1)}, bf16[8,8,64,128]{3,2,1,0:T(8,128)(2,1)S(1)}, u32[]{:S(2)}, u32[]{:S(2)}) %collective-permute-start.80) | collective-permute-done | bytes 1048608 | tf_op jit(solution)/shard_map/ppermute | solution.py:395
  86.5 22.6 %collective-permute-done.79.rest_2_ = bf16[8,8,64,128]{3,2,1,0:T(8,128)(2,1)} collective-permute-done((bf16[8,8,64,128]{3,2,1,0:T(8,128)(2,1)S(1)}, bf16[8,8,64,128]{3,2,1,0:T(8,128)(2,1)}, u32[]{:S(2)}, u32[]{:S(2)}) %collective-permute-start.79) | collective-permute-done | bytes 1048608 | tf_op jit(solution)/shard_map/ppermute | solution.py:395
  109.1 11.6 %shard_map.57 = bf16[16,8,64,128]{3,2,1,0:T(8,128)(2,1)} custom-call(s32[1040]{0:T(1024)S(1)} %get-tuple-element.103.tiles_ref, s32[1]{0:T(128)} %get-tuple-element.104.count_ref, s32[3]{0:T(128)S(1)} %pad_add_fusion.place_ref, bf16[2,8,1024,2048]{3,2,1,0:T(8,128)(2,1)} %kernel_ref.7, bf16[8,8,64,128]{3,2,1,0:T(8,128)(2,1)S(1)} %shard_map.55.rest_0_, ...), custom_call_target="tpu_custom_call" | custom-call | flops 1073741824 | bytes 8388608 | tf_op jit(solution)/shard_map/pallas_call | solution.py:320
  120.7 8.4 %all-to-all-start = ((bf16[16,8,64,128]{3,2,1,0:T(8,128)(2,1)}), bf16[16,8,64,128]{3,2,1,0:T(8,128)(2,1)S(1)}, u32[]{:S(2)}, u32[]{:S(2)}) async-start(bf16[16,8,64,128]{3,2,1,0:T(8,128)(2,1)} %shard_map.57), calls=%async_computation | async-start | bytes 4194304 | tf_op jit(solution)/shard_map/all_to_all | solution.py:400
  129.3 41.4 %all-to-all-done.rest_0_ = bf16[16,8,64,128]{3,2,1,0:T(8,128)(2,1)S(1)} async-done(((bf16[16,8,64,128]{3,2,1,0:T(8,128)(2,1)}), bf16[16,8,64,128]{3,2,1,0:T(8,128)(2,1)S(1)}, u32[]{:S(2)}, u32[]{:S(2)}) %all-to-all-start) | async-done | bytes 2097184 | tf_op jit(solution)/shard_map/all_to_all | solution.py:400
  172.0 13.9 %shard_map.58 = (bf16[8,64,128]{2,1,0:T(8,128)(2,1)S(1)}, bf16[8,64,128]{2,1,0:T(8,128)(2,1)S(1)}, bf16[8,64,128]{2,1,0:T(8,128)(2,1)S(1)}, bf16[8,64,128]{2,1,0...) custom-call(s32[1]{0:T(128)} %bitcast.mine_ref, ...), custom_call_target="tpu_custom_call" | custom-call | flops 5368709120 | bytes 16777216 | tf_op jit(solution)/shard_map/pallas_call | solution.py:177
  186.0 3.1 collective-permute-start.82
  189.1 5.6 collective-permute-start.88
  194.8 4.0 collective-permute-start.90
  198.8 2.8 collective-permute-start.92
  201.6 10.9 %collective-permute-done.88.refs_0_ = bf16[8,64,128]{2,1,0:T(8,128)(2,1)S(1)} collective-permute-done((bf16[8,64,128]{2,1,0:T(8,128)(2,1)S(1)}, bf16[8,64,128]{2,1,0:T(8,128)(2,1)S(1)}, u32[]{:S(2)}, u32[]{:S(2)}) %collective-permute-start.88) | collective-permute-done | bytes 131104 | tf_op jit(solution)/shard_map/ppermute | solution.py:383
  212.5 4.0 collective-permute-start.93
  218.9 5.8 collective-permute-done.90.refs_2_
  224.7 3.9 collective-permute-start.95
  228.6 3.8 collective-permute-start.84
  232.4 3.7 collective-permute-start.85
  236.1 2.8 collective-permute-start.86
  238.9 3.1 collective-permute-start.87
  249.4 8.8 %shard_map.46 = (bf16[8,64,128]{2,1,0:T(8,128)(2,1)S(1)}, bf16[8,64,128]{2,1,0:T(8,128)(2,1)S(1)}, bf16[8,64,128]{2,1,0:T(8,128)(2,1)S(1)}, bf16[8,64,128]{2,1,0...) custom-call(s32[1]{0:T(128)} %bitcast.mine_ref, ...), custom_call_target="tpu_custom_call" | custom-call | flops 3221225472 | bytes 16777216 | tf_op jit(solution)/shard_map/pallas_call | solution.py:177
  264.0 3.4 collective-permute-start.9
  267.5 7.3 %collective-permute-done.7.refs_0_ = bf16[8,64,128]{2,1,0:T(8,128)(2,1)S(1)} collective-permute-done((bf16[8,64,128]{2,1,0:T(8,128)(2,1)S(1)}, bf16[8,64,128]{2,1,0:T(8,128)(2,1)S(1)}, u32[]{:S(2)}, u32[]{:S(2)}) %collective-permute-start.7) | collective-permute-done | bytes 131104 | tf_op jit(solution)/shard_map/ppermute | solution.py:383
  275.5 2.8 collective-permute-done.8.refs_1_
  278.2 4.9 collective-permute-start.11
  284.1 4.3 collective-permute-start.12
  298.2 7.9 %collective-permute-start.3 = (bf16[8,64,128]{2,1,0:T(8,128)(2,1)}, bf16[8,64,128]{2,1,0:T(8,128)(2,1)S(1)}, u32[]{:S(2)}, u32[]{:S(2)}) collective-permute-start(bf16[8,64,128]{2,1,0:T(8,128)(2,1)} %get-tuple-element.109), channel_id=1, source_target_pairs={{0,8},{2,10},{4,12},{6,14},{8,0},{10,2},{12,4},{14,6},{16,24},{18,... | collective-permute-start | bytes 393224 | tf_op jit(solution)/shard_map/ppermute | solution.py:383
  312.5 10.2 %shard_map.61 = bf16[16,8,64,128]{3,2,1,0:T(8,128)(2,1)S(1)} custom-call(s32[1040]{0:T(1024)S(1)} %get-tuple-element.103.tiles_ref, s32[1]{0:T(128)} %get-tuple-element.104.count_ref, s32[3]{0:T(128)S(1)} %pad_add_fusion.place_ref, bf16[2,8,1024,2048]{3,2,1,0:T(8,128)(2,1)} %kernel_ref.7, bf16[8,8,64,128]{3,2,1,0:T(8,128)(2,1)S(1)} %shard_map.59.rest_0_, ...), custom_call_target="tpu_custom_call" | custom-call | flops 1073741824 | bytes 8388608 | tf_op jit(solution)/shard_map/pallas_call | solution.py:320
  324.0 6.8 %all-to-all-start.1 = ((bf16[16,8,64,128]{3,2,1,0:T(8,128)(2,1)}), bf16[16,8,64,128]{3,2,1,0:T(8,128)(2,1)S(1)}, u32[]{:S(2)}, u32[]{:S(2)}) async-start(bf16[16,8,64,128]{3,2,1,0:T(8,128)(2,1)} %copy-done), calls=%async_computation.1 | async-start | bytes 4194304 | tf_op jit(solution)/shard_map/all_to_all | solution.py:400
  337.6 21.1 %collective-permute-done.16.rest_3_ = bf16[8,8,64,128]{3,2,1,0:T(8,128)(2,1)S(1)} collective-permute-done((bf16[8,8,64,128]{3,2,1,0:T(8,128)(2,1)S(1)}, bf16[8,8,64,128]{3,2,1,0:T(8,128)(2,1)S(1)}, u32[]{:S(2)}, u32[]{:S(2)}) %collective-permute-start.16) | collective-permute-done | bytes 1048608 | tf_op jit(solution)/shard_map/ppermute | solution.py:395
  358.7 22.5 %collective-permute-done.15.rest_2_ = bf16[8,8,64,128]{3,2,1,0:T(8,128)(2,1)S(1)} collective-permute-done((bf16[8,8,64,128]{3,2,1,0:T(8,128)(2,1)S(1)}, bf16[8,8,64,128]{3,2,1,0:T(8,128)(2,1)S(1)}, u32[]{:S(2)}, u32[]{:S(2)}) %collective-permute-start.15) | collective-permute-done | bytes 1048608 | tf_op jit(solution)/shard_map/ppermute | solution.py:395
  381.2 10.6 %shard_map.49 = (bf16[8,64,128]{2,1,0:T(8,128)(2,1)S(1)}, bf16[8,64,128]{2,1,0:T(8,128)(2,1)S(1)}, bf16[8,64,128]{2,1,0:T(8,128)(2,1)S(1)}, bf16[8,64,128]{2,1,0...) custom-call(s32[1040]{0:T(1024)S(1)} %get-tuple-element.103.tiles_re, ...), custom_call_target="tpu_custom_call" | custom-call | flops 1073741824 | bytes 8388608 | tf_op jit(solution)/shard_map/pallas_call | solution.py:320
  398.9 2.8 collective-permute-start.23
  402.1 2.9 collective-permute-start.24
  405.1 3.5 collective-permute-start.26
  408.7 4.2 collective-permute-start.27
  418.7 10.3 %collective-permute-done.25.rest_9_ = bf16[8,64,128]{2,1,0:T(8,128)(2,1)S(1)} collective-permute-done((bf16[8,64,128]{2,1,0:T(8,128)(2,1)S(1)}, bf16[8,64,128]{2,1,0:T(8,128)(2,1)S(1)}, u32[]{:S(2)}, u32[]{:S(2)}) %collective-permute-start.25) | collective-permute-done | bytes 131104 | tf_op jit(solution)/shard_map/ppermute | solution.py:383
  432.7 3.0 collective-permute-start.31
  438.4 3.0 collective-permute-done.31.rest_15_
  442.0 14.6 %shard_map.50 = (bf16[8,64,128]{2,1,0:T(8,128)(2,1)S(1)}, bf16[8,64,128]{2,1,0:T(8,128)(2,1)S(1)}, bf16[8,64,128]{2,1,0:T(8,128)(2,1)S(1)}, bf16[8,64,128]{2,1,0...) custom-call(s32[1]{0:T(128)} %bitcast.mine_ref, ...), custom_call_target="tpu_custom_call" | custom-call | flops 5368709120 | bytes 16777216 | tf_op jit(solution)/shard_map/pallas_call | solution.py:177
  457.1 12.8 %collective-permute-start.39 = (bf16[8,64,128]{2,1,0:T(8,128)(2,1)S(1)}, bf16[8,64,128]{2,1,0:T(8,128)(2,1)S(1)}, u32[]{:S(2)}, u32[]{:S(2)}) collective-permute-start(bf16[8,64,128]{2,1,0:T(8,128)(2,1)S(1)} %get-tuple-element.145), channel_id=1, source_target_pairs={{0,16},{2,18},{4,20},{6,22},{8,24},{10,26},{12,28},{14,30},{16,0},... | collective-permute-start | bytes 393224 | tf_op jit(solution)/shard_map/ppermute | solution.py:383
  470.2 3.6 collective-permute-start.41
  474.6 12.8 %collective-permute-done.39.refs_0_ = bf16[8,64,128]{2,1,0:T(8,128)(2,1)S(1)} collective-permute-done((bf16[8,64,128]{2,1,0:T(8,128)(2,1)S(1)}, bf16[8,64,128]{2,1,0:T(8,128)(2,1)S(1)}, u32[]{:S(2)}, u32[]{:S(2)}) %collective-permute-start.39) | collective-permute-done | bytes 131104 | tf_op jit(solution)/shard_map/ppermute | solution.py:383
  493.2 6.5 %collective-permute-done.41.refs_2_ = bf16[8,64,128]{2,1,0:T(8,128)(2,1)S(1)} collective-permute-done((bf16[8,64,128]{2,1,0:T(8,128)(2,1)S(1)}, bf16[8,64,128]{2,1,0:T(8,128)(2,1)S(1)}, u32[]{:S(2)}, u32[]{:S(2)}) %collective-permute-start.41) | collective-permute-done | bytes 131104 | tf_op jit(solution)/shard_map/ppermute | solution.py:383
  499.6 3.7 collective-permute-done.42.refs_3_
  503.4 4.0 collective-permute-start.35
  507.4 3.1 collective-permute-start.36
  510.5 3.4 collective-permute-start.37
  513.9 3.1 collective-permute-start.38
  523.1 19.7 %collective-permute-done.48.rest_3_ = bf16[8,8,64,128]{3,2,1,0:T(8,128)(2,1)S(1)} collective-permute-done((bf16[8,8,64,128]{3,2,1,0:T(8,128)(2,1)S(1)}, bf16[8,8,64,128]{3,2,1,0:T(8,128)(2,1)S(1)}, u32[]{:S(2)}, u32[]{:S(2)}) %collective-permute-start.48) | collective-permute-done | bytes 1048608 | tf_op jit(solution)/shard_map/ppermute | solution.py:395
  542.8 22.5 %collective-permute-done.47.rest_2_ = bf16[8,8,64,128]{3,2,1,0:T(8,128)(2,1)S(1)} collective-permute-done((bf16[8,8,64,128]{3,2,1,0:T(8,128)(2,1)S(1)}, bf16[8,8,64,128]{3,2,1,0:T(8,128)(2,1)S(1)}, u32[]{:S(2)}, u32[]{:S(2)}) %collective-permute-start.47) | collective-permute-done | bytes 1048608 | tf_op jit(solution)/shard_map/ppermute | solution.py:395
  565.3 11.5 %shard_map.53 = (bf16[8,64,128]{2,1,0:T(8,128)(2,1)S(1)}, bf16[8,64,128]{2,1,0:T(8,128)(2,1)S(1)}, bf16[8,64,128]{2,1,0:T(8,128)(2,1)S(1)}, bf16[8,64,128]{2,1,0...) custom-call(s32[1040]{0:T(1024)S(1)} %get-tuple-element.103.tiles_re, ...), custom_call_target="tpu_custom_call" | custom-call | flops 1073741824 | bytes 8388608 | tf_op jit(solution)/shard_map/pallas_call | solution.py:320
  590.8 5.2 collective-permute-done.54.rest_6_
  596.5 3.1 collective-permute-done.55.rest_7_
  604.1 9.3 %collective-permute-done.57.rest_9_ = bf16[8,64,128]{2,1,0:T(8,128)(2,1)S(1)} collective-permute-done((bf16[8,64,128]{2,1,0:T(8,128)(2,1)S(1)}, bf16[8,64,128]{2,1,0:T(8,128)(2,1)S(1)}, u32[]{:S(2)}, u32[]{:S(2)}) %collective-permute-start.57) | collective-permute-done | bytes 131104 | tf_op jit(solution)/shard_map/ppermute | solution.py:383
  614.1 2.9 collective-permute-start.62
  619.7 9.9 %shard_map.62.rest_16_ = f32[64,128,512]{2,1,0:T(8,128)} custom-call(s32[1]{0:T(128)} %bitcast.mine_ref, f32[64,128,512]{2,1,0:T(8,128)} %direct_ref.11, bf16[2,256,256]{2,1,0:T(8,128)(2,1)S(1)} %copy-done.2, s32[4,128,16]{2,1,0:T(8,128)S(1)} %bitcast.12, bf16[16,8,64,128]{3,2,1,0:T(8,128)(2,1)S(1)} %all-to-all-done.1.rest_0_), custom_call_target="tpu_custom_call" | custom-call | flops 2147483648 | bytes 16777216 | tf_op jit(solution)/shard_map/pallas_call | solution.py:177
  629.7 9.9 %shard_map.63 = f32[64,128,512]{2,1,0:T(8,128)} custom-call(s32[1]{0:T(128)} %bitcast.mine_ref, f32[64,128,512]{2,1,0:T(8,128)} %direct_ref.11, bf16[2,256,256]{2,1,0:T(8,128)(2,1)S(1)} %copy-done.2, s32[4,128,16]{2,1,0:T(8,128)S(1)} %bitcast.13, bf16[8,64,128]{2,1,0:T(8,128)(2,1)S(1)} %get-tuple-element.153.rest_0_, ...), custom_call_target="tpu_custom_call", output_to_operand_aliasing={{}: (20, {})} | custom-call | flops 2147483648 | bytes 16777216 | tf_op jit(solution)/shard_map/pallas_call | solution.py:177
  (204 shorter events, 121.7 us)
Async XLA Ops:
  11.8 19.6 %collective-permute-start.71 = (bf16[8,64,128]{2,1,0:T(8,128)(2,1)S(1)}, bf16[8,64,128]{2,1,0:T(8,128)(2,1)S(1)}, u32[]{:S(2)}, u32[]{:S(2)}) collective-permute-start(bf16[8,64,128]{2,1,0:T(8,128)(2,1)S(1)} %get-tuple-element.177), channel_id=1, source_target_pairs={{0,16},{2,18},{4,20},{6,22},{8,24},{10,26},{12,28},{14,30},{16,0},... | collective-permute-start | bytes 393224 | tf_op jit(solution)/shard_map/ppermute | solution.py:383
  14.1 21.8 %collective-permute-start.72 = (bf16[8,64,128]{2,1,0:T(8,128)(2,1)S(1)}, bf16[8,64,128]{2,1,0:T(8,128)(2,1)S(1)}, u32[]{:S(2)}, u32[]{:S(2)}) collective-permute-start(bf16[8,64,128]{2,1,0:T(8,128)(2,1)S(1)} %get-tuple-element.178), channel_id=1, source_target_pairs={{0,18},{2,16},{4,22},{6,20},{8,26},{10,24},{12,30},{14,28},{16,2},... | collective-permute-start | bytes 393224 | tf_op jit(solution)/shard_map/ppermute | solution.py:383
  14.7 23.5 %collective-permute-start.73 = (bf16[8,64,128]{2,1,0:T(8,128)(2,1)S(1)}, bf16[8,64,128]{2,1,0:T(8,128)(2,1)S(1)}, u32[]{:S(2)}, u32[]{:S(2)}) collective-permute-start(bf16[8,64,128]{2,1,0:T(8,128)(2,1)S(1)} %get-tuple-element.179), channel_id=1, source_target_pairs={{0,20},{2,22},{4,16},{6,18},{8,28},{10,30},{12,24},{14,26},{16,4},... | collective-permute-start | bytes 393224 | tf_op jit(solution)/shard_map/ppermute | solution.py:383
  16.9 31.0 %collective-permute-start.74 = (bf16[8,64,128]{2,1,0:T(8,128)(2,1)S(1)}, bf16[8,64,128]{2,1,0:T(8,128)(2,1)S(1)}, u32[]{:S(2)}, u32[]{:S(2)}) collective-permute-start(bf16[8,64,128]{2,1,0:T(8,128)(2,1)S(1)} %get-tuple-element.180), channel_id=1, source_target_pairs={{0,22},{2,20},{4,18},{6,16},{8,30},{10,28},{12,26},{14,24},{16,6},... | collective-permute-start | bytes 393224 | tf_op jit(solution)/shard_map/ppermute | solution.py:383
  18.1 29.8 %collective-permute-start.75 = (bf16[8,64,128]{2,1,0:T(8,128)(2,1)S(1)}, bf16[8,64,128]{2,1,0:T(8,128)(2,1)S(1)}, u32[]{:S(2)}, u32[]{:S(2)}) collective-permute-start(bf16[8,64,128]{2,1,0:T(8,128)(2,1)S(1)} %get-tuple-element.181), channel_id=1, source_target_pairs={{0,24},{2,26},{4,28},{6,30},{8,16},{10,18},{12,20},{14,22},{16,8},... | collective-permute-start | bytes 393224 | tf_op jit(solution)/shard_map/ppermute | solution.py:383
  31.4 18.0 %collective-permute-start.76 = (bf16[8,64,128]{2,1,0:T(8,128)(2,1)S(1)}, bf16[8,64,128]{2,1,0:T(8,128)(2,1)S(1)}, u32[]{:S(2)}, u32[]{:S(2)}) collective-permute-start(bf16[8,64,128]{2,1,0:T(8,128)(2,1)S(1)} %get-tuple-element.182), channel_id=1, source_target_pairs={{0,26},{2,24},{4,30},{6,28},{8,18},{10,16},{12,22},{14,20},{16,10}... | collective-permute-start | bytes 393224 | tf_op jit(solution)/shard_map/ppermute | solution.py:383
  35.8 19.6 %collective-permute-start.77 = (bf16[8,64,128]{2,1,0:T(8,128)(2,1)S(1)}, bf16[8,64,128]{2,1,0:T(8,128)(2,1)S(1)}, u32[]{:S(2)}, u32[]{:S(2)}) collective-permute-start(bf16[8,64,128]{2,1,0:T(8,128)(2,1)S(1)} %get-tuple-element.183), channel_id=1, source_target_pairs={{0,28},{2,30},{4,24},{6,26},{8,20},{10,22},{12,16},{14,18},{16,12}... | collective-permute-start | bytes 393224 | tf_op jit(solution)/shard_map/ppermute | solution.py:383
  38.1 19.8 %collective-permute-start.78 = (bf16[8,64,128]{2,1,0:T(8,128)(2,1)S(1)}, bf16[8,64,128]{2,1,0:T(8,128)(2,1)S(1)}, u32[]{:S(2)}, u32[]{:S(2)}) collective-permute-start(bf16[8,64,128]{2,1,0:T(8,128)(2,1)S(1)} %get-tuple-element.184), channel_id=1, source_target_pairs={{0,30},{2,28},{4,26},{6,24},{8,22},{10,20},{12,18},{14,16},{16,14}... | collective-permute-start | bytes 393224 | tf_op jit(solution)/shard_map/ppermute | solution.py:383
  47.9 14.4 %collective-permute-start.66 = (bf16[8,64,128]{2,1,0:T(8,128)(2,1)S(1)}, bf16[8,64,128]{2,1,0:T(8,128)(2,1)S(1)}, u32[]{:S(2)}, u32[]{:S(2)}) collective-permute-start(bf16[8,64,128]{2,1,0:T(8,128)(2,1)S(1)} %get-tuple-element.172), channel_id=1, source_target_pairs={{0,6},{2,4},{4,2},{6,0},{8,14},{10,12},{12,10},{14,8},{16,22},{18,... | collective-permute-start | bytes 393224 | tf_op jit(solution)/shard_map/ppermute | solution.py:383
  47.9 15.7 %collective-permute-start.67 = (bf16[8,64,128]{2,1,0:T(8,128)(2,1)S(1)}, bf16[8,64,128]{2,1,0:T(8,128)(2,1)S(1)}, u32[]{:S(2)}, u32[]{:S(2)}) collective-permute-start(bf16[8,64,128]{2,1,0:T(8,128)(2,1)S(1)} %get-tuple-element.173), channel_id=1, source_target_pairs={{0,8},{2,10},{4,12},{6,14},{8,0},{10,2},{12,4},{14,6},{16,24},{18,... | collective-permute-start | bytes 393224 | tf_op jit(solution)/shard_map/ppermute | solution.py:383
  62.4 24.1 %collective-permute-start.80 = (bf16[8,8,64,128]{3,2,1,0:T(8,128)(2,1)S(1)}, bf16[8,8,64,128]{3,2,1,0:T(8,128)(2,1)S(1)}, u32[]{:S(2)}, u32[]{:S(2)}) collective-permute-start(bf16[8,8,64,128]{3,2,1,0:T(8,128)(2,1)S(1)} %shard_map.56.rest_1_), channel_id=1, source_target_pairs={{0,1},{1,0},{2,3},{3,2},{4,5},{5,4},{6,7},{7,6},{8,9},{9,8},{10,11... | collective-permute-start | bytes 3145736 | tf_op jit(solution)/shard_map/ppermute | solution.py:395
  66.0 43.1 %collective-permute-start.79 = (bf16[8,8,64,128]{3,2,1,0:T(8,128)(2,1)S(1)}, bf16[8,8,64,128]{3,2,1,0:T(8,128)(2,1)}, u32[]{:S(2)}, u32[]{:S(2)}) collective-permute-start(bf16[8,8,64,128]{3,2,1,0:T(8,128)(2,1)S(1)} %shard_map.55.rest_0_), channel_id=1, source_target_pairs={{0,1},{1,0},{2,3},{3,2},{4,5},{5,4},{6,7},{7,6},{8,9},{9,8},{10,11... | collective-permute-start | bytes 3145736 | tf_op jit(solution)/shard_map/ppermute | solution.py:395
  120.7 50.0 %all-to-all-start = ((bf16[16,8,64,128]{3,2,1,0:T(8,128)(2,1)}), bf16[16,8,64,128]{3,2,1,0:T(8,128)(2,1)S(1)}, u32[]{:S(2)}, u32[]{:S(2)}) async-start(bf16[16,8,64,128]{3,2,1,0:T(8,128)(2,1)} %shard_map.57), calls=%async_computation | async-start | bytes 4194304 | tf_op jit(solution)/shard_map/all_to_all | solution.py:400
  189.1 23.3 %collective-permute-start.88 = (bf16[8,64,128]{2,1,0:T(8,128)(2,1)S(1)}, bf16[8,64,128]{2,1,0:T(8,128)(2,1)S(1)}, u32[]{:S(2)}, u32[]{:S(2)}) collective-permute-start(bf16[8,64,128]{2,1,0:T(8,128)(2,1)S(1)} %get-tuple-element.193), channel_id=1, source_target_pairs={{0,16},{2,18},{4,20},{6,22},{8,24},{10,26},{12,28},{14,30},{16,0},... | collective-permute-start | bytes 393224 | tf_op jit(solution)/shard_map/ppermute | solution.py:383
  194.7 21.7 %collective-permute-start.89 = (bf16[8,64,128]{2,1,0:T(8,128)(2,1)S(1)}, bf16[8,64,128]{2,1,0:T(8,128)(2,1)S(1)}, u32[]{:S(2)}, u32[]{:S(2)}) collective-permute-start(bf16[8,64,128]{2,1,0:T(8,128)(2,1)S(1)} %get-tuple-element.194), channel_id=1, source_target_pairs={{0,18},{2,16},{4,22},{6,20},{8,26},{10,24},{12,30},{14,28},{16,2},... | collective-permute-start | bytes 393224 | tf_op jit(solution)/shard_map/ppermute | solution.py:383
  194.8 29.9 %collective-permute-start.90 = (bf16[8,64,128]{2,1,0:T(8,128)(2,1)S(1)}, bf16[8,64,128]{2,1,0:T(8,128)(2,1)S(1)}, u32[]{:S(2)}, u32[]{:S(2)}) collective-permute-start(bf16[8,64,128]{2,1,0:T(8,128)(2,1)S(1)} %get-tuple-element.195), channel_id=1, source_target_pairs={{0,20},{2,22},{4,16},{6,18},{8,28},{10,30},{12,24},{14,26},{16,4},... | collective-permute-start | bytes 393224 | tf_op jit(solution)/shard_map/ppermute | solution.py:383
  198.8 29.8 %collective-permute-start.91 = (bf16[8,64,128]{2,1,0:T(8,128)(2,1)S(1)}, bf16[8,64,128]{2,1,0:T(8,128)(2,1)S(1)}, u32[]{:S(2)}, u32[]{:S(2)}) collective-permute-start(bf16[8,64,128]{2,1,0:T(8,128)(2,1)S(1)} %get-tuple-element.196), channel_id=1, source_target_pairs={{0,22},{2,20},{4,18},{6,16},{8,30},{10,28},{12,26},{14,24},{16,6},... | collective-permute-start | bytes 393224 | tf_op jit(solution)/shard_map/ppermute | solution.py:383
  198.8 29.8 %collective-permute-start.92 = (bf16[8,64,128]{2,1,0:T(8,128)(2,1)S(1)}, bf16[8,64,128]{2,1,0:T(8,128)(2,1)S(1)}, u32[]{:S(2)}, u32[]{:S(2)}) collective-permute-start(bf16[8,64,128]{2,1,0:T(8,128)(2,1)S(1)} %get-tuple-element.197), channel_id=1, source_target_pairs={{0,24},{2,26},{4,28},{6,30},{8,16},{10,18},{12,20},{14,22},{16,8},... | collective-permute-start | bytes 393224 | tf_op jit(solution)/shard_map/ppermute | solution.py:383
  212.5 19.9 %collective-permute-start.93 = (bf16[8,64,128]{2,1,0:T(8,128)(2,1)S(1)}, bf16[8,64,128]{2,1,0:T(8,128)(2,1)S(1)}, u32[]{:S(2)}, u32[]{:S(2)}) collective-permute-start(bf16[8,64,128]{2,1,0:T(8,128)(2,1)S(1)} %get-tuple-element.198), channel_id=1, source_target_pairs={{0,26},{2,24},{4,30},{6,28},{8,18},{10,16},{12,22},{14,20},{16,10}... | collective-permute-start | bytes 393224 | tf_op jit(solution)/shard_map/ppermute | solution.py:383
  216.4 19.7 %collective-permute-start.94 = (bf16[8,64,128]{2,1,0:T(8,128)(2,1)S(1)}, bf16[8,64,128]{2,1,0:T(8,128)(2,1)S(1)}, u32[]{:S(2)}, u32[]{:S(2)}) collective-permute-start(bf16[8,64,128]{2,1,0:T(8,128)(2,1)S(1)} %get-tuple-element.199), channel_id=1, source_target_pairs={{0,28},{2,30},{4,24},{6,26},{8,20},{10,22},{12,16},{14,18},{16,12}... | collective-permute-start | bytes 393224 | tf_op jit(solution)/shard_map/ppermute | solution.py:383
  228.6 14.8 %collective-permute-start.83 = (bf16[8,64,128]{2,1,0:T(8,128)(2,1)S(1)}, bf16[8,64,128]{2,1,0:T(8,128)(2,1)S(1)}, u32[]{:S(2)}, u32[]{:S(2)}) collective-permute-start(bf16[8,64,128]{2,1,0:T(8,128)(2,1)S(1)} %get-tuple-element.188), channel_id=1, source_target_pairs={{0,6},{2,4},{4,2},{6,0},{8,14},{10,12},{12,10},{14,8},{16,22},{18,... | collective-permute-start | bytes 393224 | tf_op jit(solution)/shard_map/ppermute | solution.py:383
  228.6 16.6 %collective-permute-start.84 = (bf16[8,64,128]{2,1,0:T(8,128)(2,1)S(1)}, bf16[8,64,128]{2,1,0:T(8,128)(2,1)S(1)}, u32[]{:S(2)}, u32[]{:S(2)}) collective-permute-start(bf16[8,64,128]{2,1,0:T(8,128)(2,1)S(1)} %get-tuple-element.189), channel_id=1, source_target_pairs={{0,8},{2,10},{4,12},{6,14},{8,0},{10,2},{12,4},{14,6},{16,24},{18,... | collective-permute-start | bytes 393224 | tf_op jit(solution)/shard_map/ppermute | solution.py:383
  243.4 65.9 %collective-permute-start.97 = (bf16[8,8,64,128]{3,2,1,0:T(8,128)(2,1)S(1)}, bf16[8,8,64,128]{3,2,1,0:T(8,128)(2,1)S(1)}, u32[]{:S(2)}, u32[]{:S(2)}) collective-permute-start(bf16[8,8,64,128]{3,2,1,0:T(8,128)(2,1)S(1)} %shard_map.60.rest_1_), channel_id=1, source_target_pairs={{0,1},{1,0},{2,3},{3,2},{4,5},{5,4},{6,7},{7,6},{8,9},{9,8},{10,11... | collective-permute-start | bytes 3145736 | tf_op jit(solution)/shard_map/ppermute | solution.py:395
  247.7 63.5 %collective-permute-start.96 = (bf16[8,8,64,128]{3,2,1,0:T(8,128)(2,1)S(1)}, bf16[8,8,64,128]{3,2,1,0:T(8,128)(2,1)S(1)}, u32[]{:S(2)}, u32[]{:S(2)}) collective-permute-start(bf16[8,8,64,128]{3,2,1,0:T(8,128)(2,1)S(1)} %shard_map.59.rest_0_), channel_id=1, source_target_pairs={{0,1},{1,0},{2,3},{3,2},{4,5},{5,4},{6,7},{7,6},{8,9},{9,8},{10,11... | collective-permute-start | bytes 3145736 | tf_op jit(solution)/shard_map/ppermute | solution.py:395
  260.3 14.6 %collective-permute-start.7 = (bf16[8,64,128]{2,1,0:T(8,128)(2,1)S(1)}, bf16[8,64,128]{2,1,0:T(8,128)(2,1)S(1)}, u32[]{:S(2)}, u32[]{:S(2)}) collective-permute-start(bf16[8,64,128]{2,1,0:T(8,128)(2,1)S(1)} %get-tuple-element.113), channel_id=1, source_target_pairs={{0,16},{2,18},{4,20},{6,22},{8,24},{10,26},{12,28},{14,30},{16,0},... | collective-permute-start | bytes 393224 | tf_op jit(solution)/shard_map/ppermute | solution.py:383
  262.8 15.4 %collective-permute-start.8 = (bf16[8,64,128]{2,1,0:T(8,128)(2,1)S(1)}, bf16[8,64,128]{2,1,0:T(8,128)(2,1)S(1)}, u32[]{:S(2)}, u32[]{:S(2)}) collective-permute-start(bf16[8,64,128]{2,1,0:T(8,128)(2,1)S(1)} %get-tuple-element.114), channel_id=1, source_target_pairs={{0,18},{2,16},{4,22},{6,20},{8,26},{10,24},{12,30},{14,28},{16,2},... | collective-permute-start | bytes 393224 | tf_op jit(solution)/shard_map/ppermute | solution.py:383
  264.0 20.1 %collective-permute-start.9 = (bf16[8,64,128]{2,1,0:T(8,128)(2,1)S(1)}, bf16[8,64,128]{2,1,0:T(8,128)(2,1)S(1)}, u32[]{:S(2)}, u32[]{:S(2)}) collective-permute-start(bf16[8,64,128]{2,1,0:T(8,128)(2,1)S(1)} %get-tuple-element.115), channel_id=1, source_target_pairs={{0,20},{2,22},{4,16},{6,18},{8,28},{10,30},{12,24},{14,26},{16,4},... | collective-permute-start | bytes 393224 | tf_op jit(solution)/shard_map/ppermute | solution.py:383
  274.8 14.9 %collective-permute-start.10 = (bf16[8,64,128]{2,1,0:T(8,128)(2,1)S(1)}, bf16[8,64,128]{2,1,0:T(8,128)(2,1)S(1)}, u32[]{:S(2)}, u32[]{:S(2)}) collective-permute-start(bf16[8,64,128]{2,1,0:T(8,128)(2,1)S(1)} %get-tuple-element.116), channel_id=1, source_target_pairs={{0,22},{2,20},{4,18},{6,16},{8,30},{10,28},{12,26},{14,24},{16,6},... | collective-permute-start | bytes 393224 | tf_op jit(solution)/shard_map/ppermute | solution.py:383
  293.1 41.0 %collective-permute-start.2 = (bf16[8,64,128]{2,1,0:T(8,128)(2,1)}, bf16[8,64,128]{2,1,0:T(8,128)(2,1)S(1)}, u32[]{:S(2)}, u32[]{:S(2)}) collective-permute-start(bf16[8,64,128]{2,1,0:T(8,128)(2,1)} %get-tuple-element.108), channel_id=1, source_target_pairs={{0,6},{2,4},{4,2},{6,0},{8,14},{10,12},{12,10},{14,8},{16,22},{18,... | collective-permute-start | bytes 393224 | tf_op jit(solution)/shard_map/ppermute | solution.py:383
  298.2 35.9 %collective-permute-start.3 = (bf16[8,64,128]{2,1,0:T(8,128)(2,1)}, bf16[8,64,128]{2,1,0:T(8,128)(2,1)S(1)}, u32[]{:S(2)}, u32[]{:S(2)}) collective-permute-start(bf16[8,64,128]{2,1,0:T(8,128)(2,1)} %get-tuple-element.109), channel_id=1, source_target_pairs={{0,8},{2,10},{4,12},{6,14},{8,0},{10,2},{12,4},{14,6},{16,24},{18,... | collective-permute-start | bytes 393224 | tf_op jit(solution)/shard_map/ppermute | solution.py:383
  306.8 27.4 %collective-permute-start.4 = (bf16[8,64,128]{2,1,0:T(8,128)(2,1)}, bf16[8,64,128]{2,1,0:T(8,128)(2,1)}, u32[]{:S(2)}, u32[]{:S(2)}) collective-permute-start(bf16[8,64,128]{2,1,0:T(8,128)(2,1)} %get-tuple-element.110), channel_id=1, source_target_pairs={{0,10},{2,8},{4,14},{6,12},{8,2},{10,0},{12,6},{14,4},{16,26},{18,... | collective-permute-start | bytes 393224 | tf_op jit(solution)/shard_map/ppermute | solution.py:383
  309.3 24.8 %collective-permute-start.5 = (bf16[8,64,128]{2,1,0:T(8,128)(2,1)}, bf16[8,64,128]{2,1,0:T(8,128)(2,1)}, u32[]{:S(2)}, u32[]{:S(2)}) collective-permute-start(bf16[8,64,128]{2,1,0:T(8,128)(2,1)} %get-tuple-element.111), channel_id=1, source_target_pairs={{0,12},{2,14},{4,8},{6,10},{8,4},{10,6},{12,0},{14,2},{16,28},{18,... | collective-permute-start | bytes 393224 | tf_op jit(solution)/shard_map/ppermute | solution.py:383
  311.2 22.9 %collective-permute-start.6 = (bf16[8,64,128]{2,1,0:T(8,128)(2,1)}, bf16[8,64,128]{2,1,0:T(8,128)(2,1)}, u32[]{:S(2)}, u32[]{:S(2)}) collective-permute-start(bf16[8,64,128]{2,1,0:T(8,128)(2,1)} %get-tuple-element.112), channel_id=1, source_target_pairs={{0,14},{2,12},{4,10},{6,8},{8,6},{10,4},{12,2},{14,0},{16,30},{18,... | collective-permute-start | bytes 393224 | tf_op jit(solution)/shard_map/ppermute | solution.py:383
  324.0 295.6 %all-to-all-start.1 = ((bf16[16,8,64,128]{3,2,1,0:T(8,128)(2,1)}), bf16[16,8,64,128]{3,2,1,0:T(8,128)(2,1)S(1)}, u32[]{:S(2)}, u32[]{:S(2)}) async-start(bf16[16,8,64,128]{3,2,1,0:T(8,128)(2,1)} %copy-done), calls=%async_computation.1 | async-start | bytes 4194304 | tf_op jit(solution)/shard_map/all_to_all | solution.py:400
  334.0 24.7 %collective-permute-start.16 = (bf16[8,8,64,128]{3,2,1,0:T(8,128)(2,1)S(1)}, bf16[8,8,64,128]{3,2,1,0:T(8,128)(2,1)S(1)}, u32[]{:S(2)}, u32[]{:S(2)}) collective-permute-start(bf16[8,8,64,128]{3,2,1,0:T(8,128)(2,1)S(1)} %shard_map.48.rest_1_), channel_id=1, source_target_pairs={{0,1},{1,0},{2,3},{3,2},{4,5},{5,4},{6,7},{7,6},{8,9},{9,8},{10,11... | collective-permute-start | bytes 3145736 | tf_op jit(solution)/shard_map/ppermute | solution.py:395
  336.1 45.1 %collective-permute-start.15 = (bf16[8,8,64,128]{3,2,1,0:T(8,128)(2,1)S(1)}, bf16[8,8,64,128]{3,2,1,0:T(8,128)(2,1)S(1)}, u32[]{:S(2)}, u32[]{:S(2)}) collective-permute-start(bf16[8,8,64,128]{3,2,1,0:T(8,128)(2,1)S(1)} %shard_map.47.rest_0_), channel_id=1, source_target_pairs={{0,1},{1,0},{2,3},{3,2},{4,5},{5,4},{6,7},{7,6},{8,9},{9,8},{10,11... | collective-permute-start | bytes 3145736 | tf_op jit(solution)/shard_map/ppermute | solution.py:395
  398.9 16.5 %collective-permute-start.23 = (bf16[8,64,128]{2,1,0:T(8,128)(2,1)S(1)}, bf16[8,64,128]{2,1,0:T(8,128)(2,1)S(1)}, u32[]{:S(2)}, u32[]{:S(2)}) collective-permute-start(bf16[8,64,128]{2,1,0:T(8,128)(2,1)S(1)} %get-tuple-element.128), channel_id=1, source_target_pairs={{0,14},{2,12},{4,10},{6,8},{8,6},{10,4},{12,2},{14,0},{16,30},{18,... | collective-permute-start | bytes 393224 | tf_op jit(solution)/shard_map/ppermute | solution.py:383
  402.1 14.5 %collective-permute-start.24 = (bf16[8,64,128]{2,1,0:T(8,128)(2,1)S(1)}, bf16[8,64,128]{2,1,0:T(8,128)(2,1)S(1)}, u32[]{:S(2)}, u32[]{:S(2)}) collective-permute-start(bf16[8,64,128]{2,1,0:T(8,128)(2,1)S(1)} %get-tuple-element.129), channel_id=1, source_target_pairs={{0,16},{2,18},{4,20},{6,22},{8,24},{10,26},{12,28},{14,30},{16,0},... | collective-permute-start | bytes 393224 | tf_op jit(solution)/shard_map/ppermute | solution.py:383
  405.1 24.0 %collective-permute-start.25 = (bf16[8,64,128]{2,1,0:T(8,128)(2,1)S(1)}, bf16[8,64,128]{2,1,0:T(8,128)(2,1)S(1)}, u32[]{:S(2)}, u32[]{:S(2)}) collective-permute-start(bf16[8,64,128]{2,1,0:T(8,128)(2,1)S(1)} %get-tuple-element.130), channel_id=1, source_target_pairs={{0,18},{2,16},{4,22},{6,20},{8,26},{10,24},{12,30},{14,28},{16,2},... | collective-permute-start | bytes 393224 | tf_op jit(solution)/shard_map/ppermute | solution.py:383
  405.1 27.6 %collective-permute-start.26 = (bf16[8,64,128]{2,1,0:T(8,128)(2,1)S(1)}, bf16[8,64,128]{2,1,0:T(8,128)(2,1)S(1)}, u32[]{:S(2)}, u32[]{:S(2)}) collective-permute-start(bf16[8,64,128]{2,1,0:T(8,128)(2,1)S(1)} %get-tuple-element.131), channel_id=1, source_target_pairs={{0,20},{2,22},{4,16},{6,18},{8,28},{10,30},{12,24},{14,26},{16,4},... | collective-permute-start | bytes 393224 | tf_op jit(solution)/shard_map/ppermute | solution.py:383
  408.7 29.7 %collective-permute-start.27 = (bf16[8,64,128]{2,1,0:T(8,128)(2,1)S(1)}, bf16[8,64,128]{2,1,0:T(8,128)(2,1)S(1)}, u32[]{:S(2)}, u32[]{:S(2)}) collective-permute-start(bf16[8,64,128]{2,1,0:T(8,128)(2,1)S(1)} %get-tuple-element.132), channel_id=1, source_target_pairs={{0,22},{2,20},{4,18},{6,16},{8,30},{10,28},{12,26},{14,24},{16,6},... | collective-permute-start | bytes 393224 | tf_op jit(solution)/shard_map/ppermute | solution.py:383
  415.5 22.9 %collective-permute-start.28 = (bf16[8,64,128]{2,1,0:T(8,128)(2,1)S(1)}, bf16[8,64,128]{2,1,0:T(8,128)(2,1)S(1)}, u32[]{:S(2)}, u32[]{:S(2)}) collective-permute-start(bf16[8,64,128]{2,1,0:T(8,128)(2,1)S(1)} %get-tuple-element.133), channel_id=1, source_target_pairs={{0,24},{2,26},{4,28},{6,30},{8,16},{10,18},{12,20},{14,22},{16,8},... | collective-permute-start | bytes 393224 | tf_op jit(solution)/shard_map/ppermute | solution.py:383
  416.7 21.7 %collective-permute-start.29 = (bf16[8,64,128]{2,1,0:T(8,128)(2,1)S(1)}, bf16[8,64,128]{2,1,0:T(8,128)(2,1)S(1)}, u32[]{:S(2)}, u32[]{:S(2)}) collective-permute-start(bf16[8,64,128]{2,1,0:T(8,128)(2,1)S(1)} %get-tuple-element.134), channel_id=1, source_target_pairs={{0,26},{2,24},{4,30},{6,28},{8,18},{10,16},{12,22},{14,20},{16,10}... | collective-permute-start | bytes 393224 | tf_op jit(solution)/shard_map/ppermute | solution.py:383
  456.6 17.3 %collective-permute-start.32 = (bf16[8,64,128]{2,1,0:T(8,128)(2,1)S(1)}, bf16[8,64,128]{2,1,0:T(8,128)(2,1)S(1)}, u32[]{:S(2)}, u32[]{:S(2)}) collective-permute-start(bf16[8,64,128]{2,1,0:T(8,128)(2,1)S(1)} %get-tuple-element.138), channel_id=1, source_target_pairs={{0,2},{2,0},{4,6},{6,4},{8,10},{10,8},{12,14},{14,12},{16,18},{18,... | collective-permute-start | bytes 393224 | tf_op jit(solution)/shard_map/ppermute | solution.py:383
  457.1 17.0 %collective-permute-start.33 = (bf16[8,64,128]{2,1,0:T(8,128)(2,1)S(1)}, bf16[8,64,128]{2,1,0:T(8,128)(2,1)S(1)}, u32[]{:S(2)}, u32[]{:S(2)}) collective-permute-start(bf16[8,64,128]{2,1,0:T(8,128)(2,1)S(1)} %get-tuple-element.139), channel_id=1, source_target_pairs={{0,4},{2,6},{4,0},{6,2},{8,12},{10,14},{12,8},{14,10},{16,20},{18,... | collective-permute-start | bytes 393224 | tf_op jit(solution)/shard_map/ppermute | solution.py:383
  457.1 30.4 %collective-permute-start.39 = (bf16[8,64,128]{2,1,0:T(8,128)(2,1)S(1)}, bf16[8,64,128]{2,1,0:T(8,128)(2,1)S(1)}, u32[]{:S(2)}, u32[]{:S(2)}) collective-permute-start(bf16[8,64,128]{2,1,0:T(8,128)(2,1)S(1)} %get-tuple-element.145), channel_id=1, source_target_pairs={{0,16},{2,18},{4,20},{6,22},{8,24},{10,26},{12,28},{14,30},{16,0},... | collective-permute-start | bytes 393224 | tf_op jit(solution)/shard_map/ppermute | solution.py:383
  469.9 21.2 %collective-permute-start.40 = (bf16[8,64,128]{2,1,0:T(8,128)(2,1)S(1)}, bf16[8,64,128]{2,1,0:T(8,128)(2,1)S(1)}, u32[]{:S(2)}, u32[]{:S(2)}) collective-permute-start(bf16[8,64,128]{2,1,0:T(8,128)(2,1)S(1)} %get-tuple-element.146), channel_id=1, source_target_pairs={{0,18},{2,16},{4,22},{6,20},{8,26},{10,24},{12,30},{14,28},{16,2},... | collective-permute-start | bytes 393224 | tf_op jit(solution)/shard_map/ppermute | solution.py:383
  470.2 29.4 %collective-permute-start.41 = (bf16[8,64,128]{2,1,0:T(8,128)(2,1)S(1)}, bf16[8,64,128]{2,1,0:T(8,128)(2,1)S(1)}, u32[]{:S(2)}, u32[]{:S(2)}) collective-permute-start(bf16[8,64,128]{2,1,0:T(8,128)(2,1)S(1)} %get-tuple-element.147), channel_id=1, source_target_pairs={{0,20},{2,22},{4,16},{6,18},{8,28},{10,30},{12,24},{14,26},{16,4},... | collective-permute-start | bytes 393224 | tf_op jit(solution)/shard_map/ppermute | solution.py:383
  473.9 29.5 %collective-permute-start.42 = (bf16[8,64,128]{2,1,0:T(8,128)(2,1)S(1)}, bf16[8,64,128]{2,1,0:T(8,128)(2,1)S(1)}, u32[]{:S(2)}, u32[]{:S(2)}) collective-permute-start(bf16[8,64,128]{2,1,0:T(8,128)(2,1)S(1)} %get-tuple-element.148), channel_id=1, source_target_pairs={{0,22},{2,20},{4,18},{6,16},{8,30},{10,28},{12,26},{14,24},{16,6},... | collective-permute-start | bytes 393224 | tf_op jit(solution)/shard_map/ppermute | solution.py:383
  474.0 29.3 %collective-permute-start.43 = (bf16[8,64,128]{2,1,0:T(8,128)(2,1)S(1)}, bf16[8,64,128]{2,1,0:T(8,128)(2,1)S(1)}, u32[]{:S(2)}, u32[]{:S(2)}) collective-permute-start(bf16[8,64,128]{2,1,0:T(8,128)(2,1)S(1)} %get-tuple-element.149), channel_id=1, source_target_pairs={{0,24},{2,26},{4,28},{6,30},{8,16},{10,18},{12,20},{14,22},{16,8},... | collective-permute-start | bytes 393224 | tf_op jit(solution)/shard_map/ppermute | solution.py:383
  487.5 19.9 %collective-permute-start.44 = (bf16[8,64,128]{2,1,0:T(8,128)(2,1)S(1)}, bf16[8,64,128]{2,1,0:T(8,128)(2,1)S(1)}, u32[]{:S(2)}, u32[]{:S(2)}) collective-permute-start(bf16[8,64,128]{2,1,0:T(8,128)(2,1)S(1)} %get-tuple-element.150), channel_id=1, source_target_pairs={{0,26},{2,24},{4,30},{6,28},{8,18},{10,16},{12,22},{14,20},{16,10}... | collective-permute-start | bytes 393224 | tf_op jit(solution)/shard_map/ppermute | solution.py:383
  491.1 19.4 %collective-permute-start.45 = (bf16[8,64,128]{2,1,0:T(8,128)(2,1)S(1)}, bf16[8,64,128]{2,1,0:T(8,128)(2,1)S(1)}, u32[]{:S(2)}, u32[]{:S(2)}) collective-permute-start(bf16[8,64,128]{2,1,0:T(8,128)(2,1)S(1)} %get-tuple-element.151), channel_id=1, source_target_pairs={{0,28},{2,30},{4,24},{6,26},{8,20},{10,22},{12,16},{14,18},{16,12}... | collective-permute-start | bytes 393224 | tf_op jit(solution)/shard_map/ppermute | solution.py:383
  499.6 14.3 %collective-permute-start.46 = (bf16[8,64,128]{2,1,0:T(8,128)(2,1)S(1)}, bf16[8,64,128]{2,1,0:T(8,128)(2,1)S(1)}, u32[]{:S(2)}, u32[]{:S(2)}) collective-permute-start(bf16[8,64,128]{2,1,0:T(8,128)(2,1)S(1)} %get-tuple-element.152), channel_id=1, source_target_pairs={{0,30},{2,28},{4,26},{6,24},{8,22},{10,20},{12,18},{14,16},{16,14}... | collective-permute-start | bytes 393224 | tf_op jit(solution)/shard_map/ppermute | solution.py:383
  503.4 15.1 %collective-permute-start.34 = (bf16[8,64,128]{2,1,0:T(8,128)(2,1)S(1)}, bf16[8,64,128]{2,1,0:T(8,128)(2,1)S(1)}, u32[]{:S(2)}, u32[]{:S(2)}) collective-permute-start(bf16[8,64,128]{2,1,0:T(8,128)(2,1)S(1)} %get-tuple-element.140), channel_id=1, source_target_pairs={{0,6},{2,4},{4,2},{6,0},{8,14},{10,12},{12,10},{14,8},{16,22},{18,... | collective-permute-start | bytes 393224 | tf_op jit(solution)/shard_map/ppermute | solution.py:383
  503.4 15.8 %collective-permute-start.35 = (bf16[8,64,128]{2,1,0:T(8,128)(2,1)S(1)}, bf16[8,64,128]{2,1,0:T(8,128)(2,1)S(1)}, u32[]{:S(2)}, u32[]{:S(2)}) collective-permute-start(bf16[8,64,128]{2,1,0:T(8,128)(2,1)S(1)} %get-tuple-element.141), channel_id=1, source_target_pairs={{0,8},{2,10},{4,12},{6,14},{8,0},{10,2},{12,4},{14,6},{16,24},{18,... | collective-permute-start | bytes 393224 | tf_op jit(solution)/shard_map/ppermute | solution.py:383
  518.4 24.4 %collective-permute-start.48 = (bf16[8,8,64,128]{3,2,1,0:T(8,128)(2,1)S(1)}, bf16[8,8,64,128]{3,2,1,0:T(8,128)(2,1)S(1)}, u32[]{:S(2)}, u32[]{:S(2)}) collective-permute-start(bf16[8,8,64,128]{3,2,1,0:T(8,128)(2,1)S(1)} %shard_map.52.rest_1_), channel_id=1, source_target_pairs={{0,1},{1,0},{2,3},{3,2},{4,5},{5,4},{6,7},{7,6},{8,9},{9,8},{10,11... | collective-permute-start | bytes 3145736 | tf_op jit(solution)/shard_map/ppermute | solution.py:395
  522.2 43.1 %collective-permute-start.47 = (bf16[8,8,64,128]{3,2,1,0:T(8,128)(2,1)S(1)}, bf16[8,8,64,128]{3,2,1,0:T(8,128)(2,1)S(1)}, u32[]{:S(2)}, u32[]{:S(2)}) collective-permute-start(bf16[8,8,64,128]{3,2,1,0:T(8,128)(2,1)S(1)} %shard_map.51.rest_0_), channel_id=1, source_target_pairs={{0,1},{1,0},{2,3},{3,2},{4,5},{5,4},{6,7},{7,6},{8,9},{9,8},{10,11... | collective-permute-start | bytes 3145736 | tf_op jit(solution)/shard_map/ppermute | solution.py:395
  584.0 15.6 %collective-permute-start.55 = (bf16[8,64,128]{2,1,0:T(8,128)(2,1)S(1)}, bf16[8,64,128]{2,1,0:T(8,128)(2,1)S(1)}, u32[]{:S(2)}, u32[]{:S(2)}) collective-permute-start(bf16[8,64,128]{2,1,0:T(8,128)(2,1)S(1)} %get-tuple-element.160), channel_id=1, source_target_pairs={{0,14},{2,12},{4,10},{6,8},{8,6},{10,4},{12,2},{14,0},{16,30},{18,... | collective-permute-start | bytes 393224 | tf_op jit(solution)/shard_map/ppermute | solution.py:383
  588.3 25.2 %collective-permute-start.57 = (bf16[8,64,128]{2,1,0:T(8,128)(2,1)S(1)}, bf16[8,64,128]{2,1,0:T(8,128)(2,1)S(1)}, u32[]{:S(2)}, u32[]{:S(2)}) collective-permute-start(bf16[8,64,128]{2,1,0:T(8,128)(2,1)S(1)} %get-tuple-element.162), channel_id=1, source_target_pairs={{0,18},{2,16},{4,22},{6,20},{8,26},{10,24},{12,30},{14,28},{16,2},... | collective-permute-start | bytes 393224 | tf_op jit(solution)/shard_map/ppermute | solution.py:383
  589.7 27.3 %collective-permute-start.58 = (bf16[8,64,128]{2,1,0:T(8,128)(2,1)S(1)}, bf16[8,64,128]{2,1,0:T(8,128)(2,1)S(1)}, u32[]{:S(2)}, u32[]{:S(2)}) collective-permute-start(bf16[8,64,128]{2,1,0:T(8,128)(2,1)S(1)} %get-tuple-element.163), channel_id=1, source_target_pairs={{0,20},{2,22},{4,16},{6,18},{8,28},{10,30},{12,24},{14,26},{16,4},... | collective-permute-start | bytes 393224 | tf_op jit(solution)/shard_map/ppermute | solution.py:383
  596.0 33.6 %collective-permute-start.59 = (bf16[8,64,128]{2,1,0:T(8,128)(2,1)}, bf16[8,64,128]{2,1,0:T(8,128)(2,1)}, u32[]{:S(2)}, u32[]{:S(2)}) collective-permute-start(bf16[8,64,128]{2,1,0:T(8,128)(2,1)} %get-tuple-element.164), channel_id=1, source_target_pairs={{0,22},{2,20},{4,18},{6,16},{8,30},{10,28},{12,26},{14,24},{16,6},... | collective-permute-start | bytes 393224 | tf_op jit(solution)/shard_map/ppermute | solution.py:383
  600.2 29.4 %collective-permute-start.60 = (bf16[8,64,128]{2,1,0:T(8,128)(2,1)}, bf16[8,64,128]{2,1,0:T(8,128)(2,1)}, u32[]{:S(2)}, u32[]{:S(2)}) collective-permute-start(bf16[8,64,128]{2,1,0:T(8,128)(2,1)} %get-tuple-element.165), channel_id=1, source_target_pairs={{0,24},{2,26},{4,28},{6,30},{8,16},{10,18},{12,20},{14,22},{16,8},... | collective-permute-start | bytes 393224 | tf_op jit(solution)/shard_map/ppermute | solution.py:383
  601.8 27.8 %collective-permute-start.61 = (bf16[8,64,128]{2,1,0:T(8,128)(2,1)}, bf16[8,64,128]{2,1,0:T(8,128)(2,1)}, u32[]{:S(2)}, u32[]{:S(2)}) collective-permute-start(bf16[8,64,128]{2,1,0:T(8,128)(2,1)} %get-tuple-element.166), channel_id=1, source_target_pairs={{0,26},{2,24},{4,30},{6,28},{8,18},{10,16},{12,22},{14,20},{16,10}... | collective-permute-start | bytes 393224 | tf_op jit(solution)/shard_map/ppermute | solution.py:383
  614.1 15.5 %collective-permute-start.62 = (bf16[8,64,128]{2,1,0:T(8,128)(2,1)}, bf16[8,64,128]{2,1,0:T(8,128)(2,1)}, u32[]{:S(2)}, u32[]{:S(2)}) collective-permute-start(bf16[8,64,128]{2,1,0:T(8,128)(2,1)} %get-tuple-element.167), channel_id=1, source_target_pairs={{0,28},{2,30},{4,24},{6,26},{8,20},{10,22},{12,16},{14,18},{16,12}... | collective-permute-start | bytes 393224 | tf_op jit(solution)/shard_map/ppermute | solution.py:383
  (57 other events, 1045.0 us)
